TPU v7x, 32 devices: a whole 2x2x4 slice. The times are simulated.
32 devices in a mesh: groups: 2 (over y), basin: 4 (over z), member: 4 (over x, core).
Axes of the slice: x: 2, y: 2, z: 4, core: 2. Of those that a mesh axis runs over, the one named last changes fastest.
Arguments:
- runoff: bfloat16 [64, 32, 2048], P(('groups', 'basin'), 'member'), parts along dimension 0, may hold values from 0.099609375 to 3
- route_params: float32 [3, 64, 32], P(None, ('groups', 'basin'), 'member'), parts along dimension 1, may hold values from 0.1 to 0.5
- unit_shapes: float32 [3, 256], replicated, may hold values from 0 to 2
- level_map: int32 [64], P(('groups', 'basin')), parts along dimension 0, may hold values from 0 to 7, as said below
- down_map: int32 [64], P(('groups', 'basin')), parts along dimension 0, may hold values from 0 to 16
- gauge_reach: int32 [16], P(('groups', 'basin')), parts along dimension 0, may hold values from 0 to 7
- gauge_sigma: float32 [16], P(('groups', 'basin')), parts along dimension 0, may hold values from 0.5 to 5
- observed: float32 [16, 64], P(('groups', 'basin')), parts along dimension 0, may hold values from 0.5 to 5
- obs_noise: float32 [16, 32, 64], P(('groups', 'basin'), 'member'), parts along dimension 0, may hold values from -6 to 6
Outputs:
- flows: bfloat16 [64, 32, 2048], P(('groups', 'basin'), 'member'), parts along dimension 0
- new_params: float32 [3, 64, 32], P(None, ('groups', 'basin'), 'member'), parts along dimension 1
There are 2 independent parts, one for each index of `groups`. A program takes and returns all parts, laid end to end along the dimension named above; an argument that names none is the same for every part. Nothing has to cross between parts.
Inputs may be any that keep to these rules, and one draw needn't show every extreme that they name: `level_map`: within one block of 8 reaches at most 2 reaches share a level, and some level of each block holds exactly 2. `gauge_reach`: index of the gauged reach within its block of 8 reaches; gauge g lies in block g // 2.
All inputs are finite; a program needn't handle non-finite values.
Results may differ from a plain program's by a relative error of at most 0.0023.
Values may be sent and summed in bfloat16 or wider, within the bound.
No kernel may reach another device: no remote copies, remote signals or barrier semaphores. Data moves between devices by JAX's collectives and lax.ppermute only.
A program may use at most 192 MiB of HBM per device.

v0:
```python
import jax
import jax.numpy as jnp
from jax import lax
from jax.sharding import PartitionSpec as P

LEVELS = 8
WINDOWS = 64


def passed_along(x, axis, by):
    length = lax.axis_size(axis)
    pairs = [(i, i + by) for i in range(length) if 0 <= i + by < length]
    return lax.ppermute(x, axis, pairs)


def kernel_table(unit_shapes):
    block_len = unit_shapes.shape[1]
    row_ids = jnp.arange(2 * block_len, dtype=jnp.int32)[:, None]
    col_ids = jnp.arange(block_len, dtype=jnp.int32)[None, :]
    lag_index = jnp.where(row_ids < block_len, col_ids - row_ids, 2 * block_len + col_ids - row_ids)
    usable = (lag_index >= 0) & (lag_index < block_len)
    shape_values = jnp.take(unit_shapes, jnp.clip(lag_index, 0, block_len - 1), axis=1)
    shape_values = jnp.where(usable[None], shape_values, 0.0) / block_len
    return jnp.transpose(shape_values, (1, 0, 2)).reshape(2 * block_len, -1).astype(jnp.bfloat16)


def route_rows(inflow_rows, slot_weights, conv_table):
    block_len = conv_table.shape[0] // 2
    row_count, series_len = inflow_rows.shape
    blocks = inflow_rows.reshape(row_count, series_len // block_len, block_len)
    earlier = jnp.concatenate([jnp.zeros_like(blocks[:, :1]), blocks[:, :-1]], axis=1)
    joined = jnp.concatenate([blocks, earlier], axis=2).reshape(-1, 2 * block_len)
    mixed_blocks = jnp.dot(joined, conv_table, preferred_element_type=jnp.float32)
    mixed_blocks = mixed_blocks.reshape(
        row_count, series_len // block_len, slot_weights.shape[1], block_len
    )
    return jnp.sum(mixed_blocks * slot_weights[:, None, :, None], axis=2).reshape(
        row_count, series_len
    )


def level_select(level_block, down_block, level_now, slot_count):
    entry_count = level_block.shape[0]
    entry_ids = jnp.arange(entry_count, dtype=jnp.int32)
    in_level = level_block == level_now
    before = (entry_ids[None, :] < entry_ids[:, None]) & in_level[None, :]
    rank = jnp.sum(before.astype(jnp.int32), axis=1)
    slot_ids = jnp.arange(slot_count, dtype=jnp.int32)
    select = (rank[None, :] == slot_ids[:, None]) & in_level[None, :]
    slot_valid = slot_ids < jnp.sum(in_level.astype(jnp.int32))
    slot_target = jnp.sum(jnp.where(select, down_block[None, :], 0), axis=1)
    return (select, slot_valid, slot_target)


def per_device(
    runoff,
    route_params,
    unit_shapes,
    level_map,
    down_map,
    gauge_reach,
    gauge_sigma,
    observed,
    obs_noise,
):
    conv_table = kernel_table(unit_shapes)
    reach_count, members_dev, series_len = runoff.shape
    flat_len = members_dev * series_len
    slot_count = reach_count // 4
    shape_count = route_params.shape[0]
    inflow = runoff.astype(jnp.float32).reshape(reach_count, flat_len)
    outflow = jnp.zeros_like(inflow)
    reach_ids = jnp.arange(reach_count, dtype=jnp.int32)[:, None]
    params_rows = jnp.transpose(route_params, (1, 2, 0))
    prev_level, prev_down = passed_along((level_map, down_map), "basin", 1)
    for level_now in range(LEVELS):
        select, slot_valid, slot_target_row = level_select(
            level_map, down_map, level_now, slot_count
        )
        gathered = jnp.dot(
            select.astype(jnp.bfloat16),
            inflow.astype(jnp.bfloat16),
            preferred_element_type=jnp.float32,
        )
        gathered = gathered.astype(jnp.bfloat16).reshape(slot_count * members_dev, series_len)
        slot_weights = jnp.einsum(
            "cr,rms->cms", select.astype(jnp.float32), params_rows, precision=lax.Precision.HIGHEST
        ).reshape(-1, shape_count)
        routed = (
            route_rows(gathered, slot_weights, conv_table)
            .astype(jnp.bfloat16)
            .reshape(slot_count, flat_len)
        )
        slot_target = slot_target_row[None, :]
        slot_mask = slot_valid[None, :]
        local_edges = (slot_target == reach_ids) & slot_mask
        chosen = jnp.transpose(select) & slot_mask
        edge_matrix = jnp.concatenate([local_edges, chosen], axis=0).astype(jnp.bfloat16)
        spread_flows = jnp.dot(edge_matrix, routed, preferred_element_type=jnp.float32)
        inflow = inflow + spread_flows[:reach_count]
        outflow = outflow + spread_flows[reach_count:]
        if level_now + 1 < LEVELS:
            arrived = passed_along(routed, "basin", 1)
            prev_select, prev_valid, prev_target = level_select(
                prev_level, prev_down, level_now, slot_count
            )
            incoming = (prev_target[None, :] == reach_ids + reach_count) & prev_valid[None, :]
            inflow = inflow + jnp.dot(
                incoming.astype(jnp.bfloat16), arrived, preferred_element_type=jnp.float32
            )
    flows = outflow.astype(jnp.bfloat16)
    gauge_pick = (gauge_reach[:, None] == jnp.arange(reach_count, dtype=jnp.int32)[None, :]).astype(
        jnp.bfloat16
    )
    gauged = jnp.dot(gauge_pick, flows, preferred_element_type=jnp.float32)
    predicted = jnp.mean(gauged.reshape(-1, members_dev, WINDOWS, series_len // WINDOWS), axis=3)
    scaled = predicted / gauge_sigma[:, None, None]
    innovation = observed[:, None, :] / gauge_sigma[:, None, None] + obs_noise - scaled
    scaled = jnp.transpose(scaled, (0, 2, 1))
    innovation = jnp.transpose(innovation, (0, 2, 1))
    scaled, innovation = (
        lax.all_gather(scaled, "member", axis=2, tiled=True),
        lax.all_gather(innovation, "member", axis=2, tiled=True),
    )
    members = scaled.shape[2]
    scaled = scaled.reshape(-1, members)
    innovation = innovation.reshape(-1, members)
    spread = (scaled - jnp.mean(scaled, axis=1, keepdims=True)) / jnp.sqrt(members - 1.0)
    gram_part = jnp.dot(spread.T, spread, precision=lax.Precision.HIGHEST)
    cross_part = jnp.dot(spread.T, innovation, precision=lax.Precision.HIGHEST)
    gram_part, cross_part = lax.psum((gram_part, cross_part), "basin")
    gram = jnp.eye(members, dtype=jnp.float32) + gram_part
    factor = jnp.linalg.cholesky(gram)
    kalman_gain = jax.scipy.linalg.cho_solve((factor, True), cross_part)
    col_start = lax.axis_index("member") * members_dev
    all_params = lax.all_gather(route_params, "member", axis=2, tiled=True).reshape(-1, members)
    anomaly = all_params - jnp.mean(all_params, axis=1, keepdims=True)
    columns = lax.dynamic_slice_in_dim(kalman_gain, col_start, members_dev, 1)
    increment = jnp.dot(anomaly, columns, precision=lax.Precision.HIGHEST)
    updated = route_params.reshape(-1, members_dev) + increment / jnp.sqrt(members - 1.0)
    return (
        flows.reshape(reach_count, members_dev, series_len),
        updated.reshape(route_params.shape),
    )


def solution(mesh):
    return jax.shard_map(
        per_device,
        mesh=mesh,
        in_specs=(
            P(("groups", "basin"), "member", None),
            P(None, ("groups", "basin"), "member"),
            P(),
            P(("groups", "basin")),
            P(("groups", "basin")),
            P(("groups", "basin")),
            P(("groups", "basin")),
            P(("groups", "basin"), None),
            P(("groups", "basin"), "member", None),
        ),
        out_specs=(P(("groups", "basin"), "member", None), P(None, ("groups", "basin"), "member")),
        check_vma=False,
    )
```

profile of v0, /device:TPU:0, one launch (start us, length us, event | category | flops | bytes accessed | tf_op | source)
XLA Modules:
  0.0 595.0 jit_solution(17505443768006794124)
XLA Ops:
  0.6 5.0 collective-permute-start
  5.9 0.4 fusion.23
  6.3 0.7 broadcast_compare_fusion.2
  7.0 0.8 copy.69
  8.2 430.4 %gather_fusion = f32[131072,3]{1,0:T(8,128)} fusion(f32[3,256]{0,1:T(8,128)S(1)} %copy.69, s32[131072]{0:T(1024)S(1)} %broadcast_clamp_fusion), kind=kCustom, calls=%fused_computation | custom fusion | bytes 3670016 | tf_op jit(solution)/shard_map/jit(_take)/gather | solution.py:22
  438.6 37.2 %copy.70 = f32[512,256,3]{0,1,2:T(8,128)S(1)} copy(f32[512,256,3]{2,1,0:T(8,128)} %bitcast.2) | data formatting | bytes 3145728 | tf_op jit(solution)/shard_map/jit(_take)/gather | solution.py:22
  476.9 0.4 fusion.1
  477.3 3.5 collective-permute-start.2
  480.8 3.5 collective-permute-start.1
  484.3 0.8 convert_reduce_fusion.16
  486.9 0.7 copy.100
  488.1 0.7 copy.101
  488.8 5.2 all_gather.9
  494.0 0.7 copy.81
  494.8 0.6 div.67
  495.4 1.2 iota_compare_fusion.18
  496.7 0.5 fusion.180
  497.2 1.3 iota_compare_fusion.14
  498.7 1.3 iota_compare_fusion.10
  500.1 1.2 iota_compare_fusion.6
  501.3 0.7 compare_and_fusion.2
  502.0 0.7 pad_add_fusion
  502.9 0.8 convert_reduce_fusion.15
  503.7 0.6 iota_compare_fusion.17
  504.2 0.7 iota_compare_fusion.15
  504.9 0.6 iota_compare_fusion.13
  505.5 0.6 iota_compare_fusion.11
  506.1 1.2 iota_compare_fusion.9
  507.3 1.2 iota_compare_fusion.7
  509.0 0.7 fusion.241
  509.7 1.1 iota_compare_fusion.5
  511.4 0.4 fusion.2
  511.8 1.9 collective-permute-start.3
  513.7 0.5 fusion.184
  514.2 1.4 collective-permute-done.3
  516.2 0.4 fusion.3
  516.6 4.3 collective-permute-start.4
  521.0 0.5 fusion.188
  521.4 1.4 collective-permute-done.4
  523.4 0.4 fusion.4
  523.8 4.3 collective-permute-start.5
  528.1 0.5 fusion.192
  528.6 1.4 collective-permute-done.5
  531.0 4.3 collective-permute-start.6
  535.3 0.5 fusion.196
  535.8 1.4 collective-permute-done.6
  538.2 4.3 collective-permute-start.7
  542.5 0.5 fusion.200
  542.9 1.4 collective-permute-done.7
  544.9 0.4 fusion.7
  545.3 4.4 collective-permute-start.8
  549.8 1.5 fusion.204
  551.5 1.5 convolution_convert_fusion
  553.1 1.1 fusion.8
  554.3 2.1 fusion
  556.4 0.9 copy.83
  558.1 5.2 all_gather.11
  563.3 5.2 all_gather.10
  568.8 17.9 %all-reduce.8 = (f32[32,32]{1,0:T(8,128)S(1)}, f32[32,32]{1,0:T(8,128)S(1)}) all-reduce(f32[32,32]{1,0:T(8,128)S(1)} %convolution_bitcast_fusion, f32[32,32]{1,0:T(8,128)S(1)} %convolution_bitcast_fusion.1), channel_id=1, replica_groups=mesh['groups'=2,'basin'=4,'member'=4] {'basin'}, use_global_device_ids=true, to_apply=%region_59.60 | all-reduce | flops 2048 | bytes 16384 | tf_op jit(solution)/shard_map/psum | solution.py:131
  586.8 2.9 cholesky.17
  589.8 0.7 compare_reduce_fusion
  590.5 0.7 fusion.98
  591.2 2.4 custom-call.10
  594.3 0.7 copy.102
  (149 shorter events, 11.7 us)
Async XLA Ops:
  0.6 502.1 %collective-permute-start = (s32[8]{0:T(128)}, s32[8]{0:T(128)S(1)}, u32[]{:S(2)}, u32[]{:S(2)}) collective-permute-start(s32[8]{0:T(128)} %param.12), channel_id=1, source_target_pairs={{0,4},{4,8},{8,12},{1,5},{5,9},{9,13},{2,6},{6,10},{10,14},{3,7},{... | collective-permute-start | bytes 104 | tf_op jit(solution)/shard_map/ppermute | solution.py:13
  438.6 37.3 %copy-start.6 = (f32[3,8,8]{2,1,0:T(8,128)S(1)}, f32[3,8,8]{2,1,0:T(8,128)}, u32[]{:S(2)}) copy-start(f32[3,8,8]{2,1,0:T(8,128)} %param.10) | copy-start | bytes 2308
  438.6 37.5 %copy-start.10 = (bf16[8,8,2048]{2,1,0:T(8,128)(2,1)S(1)}, bf16[8,8,2048]{2,1,0:T(8,128)(2,1)}, u32[]{:S(2)}) copy-start(bf16[8,8,2048]{2,1,0:T(8,128)(2,1)} %param.9) | copy-start | bytes 786436
  476.5 4.3 copy-start.25
  476.6 7.8 %copy-start.20 = (s32[8]{0:T(128)S(1)}, s32[8]{0:T(128)}, u32[]{:S(2)}) copy-start(s32[8]{0:T(128)} %param.12) | copy-start | bytes 100
  476.8 19.9 %copy-start.7 = (bf16[3,256,512,1]{2,1,0,3:T(8,128)(2,1)}, bf16[3,256,512,1]{2,1,0,3:T(8,128)(2,1)S(1)}, u32[]{:S(2)}) copy-start(bf16[3,256,512,1]{2,1,0,3:T(8,128)(2,1)S(1)} %fusion.10) | copy-start | bytes 2359300
  476.9 25.8 %copy-start.16 = (f32[2]{0:T(128)S(1)}, f32[2]{0:T(128)}, u32[]{:S(2)}) copy-start(f32[2]{0:T(128)} %param.15) | copy-start | bytes 28
  476.9 25.8 %copy-start.21 = (f32[2,64]{1,0:T(2,128)S(1)}, f32[2,64]{1,0:T(2,128)}, u32[]{:S(2)}) copy-start(f32[2,64]{1,0:T(2,128)} %param.16) | copy-start | bytes 1540
  477.3 33.5 %collective-permute-start.2 = (bf16[2,16384]{1,0:T(2,128)(2,1)S(1)}, bf16[2,16384]{1,0:T(2,128)(2,1)S(1)}, u32[]{:S(2)}, u32[]{:S(2)}) collective-permute-start(bf16[2,16384]{1,0:T(2,128)(2,1)S(1)} %convert_element_type.247), channel_id=1, source_target_pairs={{0,4},{4,8},{8,12},{1,5},{5,9},{9,13},{2,6},{6,10},{10,14},{3,7},{... | collective-permute-start | bytes 196616 | tf_op jit(solution)/shard_map/ppermute | solution.py:13
  480.8 28.1 %collective-permute-start.1 = (s32[8]{0:T(128)S(1)}, s32[8]{0:T(128)S(1)}, u32[]{:S(2)}, u32[]{:S(2)}) collective-permute-start(s32[8]{0:T(128)S(1)} %copy-done.25), channel_id=1, source_target_pairs={{0,4},{4,8},{8,12},{1,5},{5,9},{9,13},{2,6},{6,10},{10,14},{3,7},{... | collective-permute-start | bytes 104 | tf_op jit(solution)/shard_map/ppermute | solution.py:13
  496.7 14.7 %copy-start.8 = (bf16[3,256,512,1]{2,1,0,3:T(8,128)(2,1)S(1)}, bf16[3,256,512,1]{2,1,0,3:T(8,128)(2,1)}, u32[]{:S(2)}) copy-start(bf16[3,256,512,1]{2,1,0,3:T(8,128)(2,1)} %copy-done.7) | copy-start | bytes 2359300
  511.8 3.8 collective-permute-start.3
  513.7 2.4 copy-start.9
  514.2 1.7 copy-start
  516.6 6.2 %collective-permute-start.4 = (bf16[2,16384]{1,0:T(2,128)(2,1)S(1)}, bf16[2,16384]{1,0:T(2,128)(2,1)S(1)}, u32[]{:S(2)}, u32[]{:S(2)}) collective-permute-start(bf16[2,16384]{1,0:T(2,128)(2,1)S(1)} %convert_element_type.263), channel_id=1, source_target_pairs={{0,4},{4,8},{8,12},{1,5},{5,9},{9,13},{2,6},{6,10},{10,14},{3,7},{... | collective-permute-start | bytes 196616 | tf_op jit(solution)/shard_map/ppermute | solution.py:13
  521.4 1.7 copy-start.2
  523.8 6.2 %collective-permute-start.5 = (bf16[2,16384]{1,0:T(2,128)(2,1)S(1)}, bf16[2,16384]{1,0:T(2,128)(2,1)S(1)}, u32[]{:S(2)}, u32[]{:S(2)}) collective-permute-start(bf16[2,16384]{1,0:T(2,128)(2,1)S(1)} %convert_element_type.271), channel_id=1, source_target_pairs={{0,4},{4,8},{8,12},{1,5},{5,9},{9,13},{2,6},{6,10},{10,14},{3,7},{... | collective-permute-start | bytes 196616 | tf_op jit(solution)/shard_map/ppermute | solution.py:13
  528.6 1.7 copy-start.3
  530.3 6.9 %copy-start.19 = (s32[2]{0:T(128)S(1)}, s32[2]{0:T(128)}, u32[]{:S(2)}) copy-start(s32[2]{0:T(128)} %get-tuple-element.39) | copy-start | bytes 28
  530.3 6.9 %copy-start.24 = (pred[2]{0:T(512)(128)(4,1)S(1)}, pred[2]{0:T(512)(128)(4,1)}, u32[]{:S(2)}) copy-start(pred[2]{0:T(512)(128)(4,1)} %iota_compare_fusion.9) | copy-start | bytes 10
  531.0 6.2 %collective-permute-start.6 = (bf16[2,16384]{1,0:T(2,128)(2,1)S(1)}, bf16[2,16384]{1,0:T(2,128)(2,1)S(1)}, u32[]{:S(2)}, u32[]{:S(2)}) collective-permute-start(bf16[2,16384]{1,0:T(2,128)(2,1)S(1)} %convert_element_type.279), channel_id=1, source_target_pairs={{0,4},{4,8},{8,12},{1,5},{5,9},{9,13},{2,6},{6,10},{10,14},{3,7},{... | collective-permute-start | bytes 196616 | tf_op jit(solution)/shard_map/ppermute | solution.py:13
  535.8 1.7 copy-start.4
  537.5 6.9 %copy-start.18 = (s32[2]{0:T(128)S(1)}, s32[2]{0:T(128)}, u32[]{:S(2)}) copy-start(s32[2]{0:T(128)} %get-tuple-element.40) | copy-start | bytes 28
  537.5 6.9 %copy-start.23 = (pred[2]{0:T(512)(128)(4,1)S(1)}, pred[2]{0:T(512)(128)(4,1)}, u32[]{:S(2)}) copy-start(pred[2]{0:T(512)(128)(4,1)} %iota_compare_fusion.7) | copy-start | bytes 10
  538.2 6.2 %collective-permute-start.7 = (bf16[2,16384]{1,0:T(2,128)(2,1)S(1)}, bf16[2,16384]{1,0:T(2,128)(2,1)S(1)}, u32[]{:S(2)}, u32[]{:S(2)}) collective-permute-start(bf16[2,16384]{1,0:T(2,128)(2,1)S(1)} %convert_element_type.287), channel_id=1, source_target_pairs={{0,4},{4,8},{8,12},{1,5},{5,9},{9,13},{2,6},{6,10},{10,14},{3,7},{... | collective-permute-start | bytes 196616 | tf_op jit(solution)/shard_map/ppermute | solution.py:13
  542.9 1.7 copy-start.5
  544.3 5.5 copy-start.14
  544.4 5.5 copy-start.15
  545.3 6.2 %collective-permute-start.8 = (bf16[2,16384]{1,0:T(2,128)(2,1)S(1)}, bf16[2,16384]{1,0:T(2,128)(2,1)S(1)}, u32[]{:S(2)}, u32[]{:S(2)}) collective-permute-start(bf16[2,16384]{1,0:T(2,128)(2,1)S(1)} %convert_element_type.295), channel_id=1, source_target_pairs={{0,4},{4,8},{8,12},{1,5},{5,9},{9,13},{2,6},{6,10},{10,14},{3,7},{... | collective-permute-start | bytes 196616 | tf_op jit(solution)/shard_map/ppermute | solution.py:13
  551.3 3.0 copy-start.1
  554.3 3.0 copy-start.22
  556.3 1.6 copy-start.12
  556.4 1.6 copy-start.17
  556.4 37.7 %copy-start.11 = (f32[3,8,32]{2,1,0:T(8,128)S(1)}, f32[3,8,32]{2,1,0:T(8,128)}, u32[]{:S(2)}) copy-start(f32[3,8,32]{2,1,0:T(8,128)} %copy.81) | copy-start | bytes 9220
  556.4 37.7 %copy-start.13 = (f32[24,8]{0,1:T(8,128)S(1)}, f32[24,8]{0,1:T(8,128)}, u32[]{:S(2)}) copy-start(f32[24,8]{0,1:T(8,128)} %copy.101) | copy-start | bytes 2308
  556.4 37.7 %copy-start.26 = (f32[24]{0:T(128)S(1)}, f32[24]{0:T(128)}, u32[]{:S(2)}) copy-start(f32[24]{0:T(128)} %div.67) | copy-start | bytes 292
where the time goes:
time: 596 us; the launch traced here: 595 us
  local copies, waits for them, and re-layouts  475 us (80%)
  starting transfers between devices  35.4 us (6%)
  blocking collectives  33.5 us (6%)
  other arithmetic  25.5 us (4%)
  matrix products  17.2 us (3%)
  waiting for transfers between devices  7.24 us (1%)
    gather x2, local copies, waits for them, and re-layouts, kernel_table(): jnp.take(unit_shapes, jnp.clip(lag_index, 0, block_len - 1), axis=1)  468 us
    ppermute x9, starting transfers between devices, passed_along(): return lax.ppermute(x, axis, pairs)  35.4 us
    psum x1, blocking collectives, per_device(): gram_part, cross_part = lax.psum((gram_part, cross_part), 'basin')  17.9 us
  transfers between devices with their start and end apart: 9, of which 6 were waited for; matrix products, arithmetic and copies ran while one was open for 83% of the time, Pallas kernels for 0%

commit v1 on v0

--- a/solution.py
+++ b/solution.py
@@ -1,27 +1,548 @@
+import functools
+
 import jax
 import jax.numpy as jnp
 from jax import lax
+from jax.experimental import pallas as pl
+from jax.experimental.pallas import tpu as pltpu
 from jax.sharding import PartitionSpec as P
 
 LEVELS = 8
 WINDOWS = 64
+LANES = 128
+EXTRA = 16
+HIGHEST = lax.Precision.HIGHEST
+
+def vmem():
+    return pl.BlockSpec(memory_space=pltpu.VMEM)
+
+
+def smem():
+    return pl.BlockSpec(memory_space=pltpu.SMEM)
+
+
+def table_body(shapes_ref, table_ref):
+    shape_count, block_len = shapes_ref.shape
+    for s in range(shape_count):
+        lags = shapes_ref[s : s + 1, :] * (1.0 / block_len)
+        lags = jnp.concatenate([lags, jnp.zeros_like(lags)], axis=1)
+        skewed = pltpu.roll(
+            jnp.broadcast_to(lags, (block_len, 2 * block_len)), 0, 1, stride=1, stride_axis=0
+        ).astype(jnp.bfloat16)
+        cols = slice(s * block_len, (s + 1) * block_len)
+        table_ref[:block_len, cols] = skewed[:, :block_len]
+        table_ref[block_len:, cols] = skewed[:, block_len:]
+
+
+def kernel_table(unit_shapes):
+    shape_count, block_len = unit_shapes.shape
+    return pl.pallas_call(
+        table_body,
+        out_shape=jax.ShapeDtypeStruct((2 * block_len, shape_count * block_len), jnp.bfloat16),
+        in_specs=[vmem()],
+        out_specs=vmem(),
+        name="table",
+    )(unit_shapes)
+
+
+def split_two(x):
+    top = x.astype(jnp.bfloat16)
+    rest = x - top.astype(jnp.float32)
+    mid = rest.astype(jnp.bfloat16)
+    return top, mid, rest - mid.astype(jnp.float32)
+
+
+def pack_body(
+    level_ref,
+    down_ref,
+    gauge_ref,
+    sigma_ref,
+    runoff_ref,
+    params_ref,
+    observed_ref,
+    noise_ref,
+    *rest,
+):
+    out_refs, (stage_ref, extra_ref) = rest[:-2], rest[-2:]
+    reach_count, members_dev, series_len = runoff_ref.shape
+    shape_count = params_ref.shape[0]
+    gauge_count, windows = observed_ref.shape
+    block_len = out_refs[0].shape[1]
+    block_count = series_len // block_len
+    share = members_dev // len(out_refs)
+    rows = share * block_count
+    here = lax.axis_index("basin")
+    for r in range(reach_count):
+        series = runoff_ref[r].astype(jnp.float32)
+        for i in range(block_count):
+            at = (r * block_count + i) * members_dev
+            for h in range(block_len // LANES):
+                lane = i * block_len + h * LANES
+                stage_ref[h, at : at + members_dev, :] = series[:, lane : lane + LANES]
+    extra_ref[...] = jnp.zeros(extra_ref.shape, jnp.float32)
+    for g in range(gauge_count):
+        extra_ref[:members_dev, g * windows : (g + 1) * windows] = (
+            observed_ref[g : g + 1, :] / sigma_ref[g] + noise_ref[g]
+        )
+    lower = slice(members_dev, members_dev + reach_count)
+    for s in range(shape_count):
+        extra_ref[lower, s * members_dev : (s + 1) * members_dev] = params_ref[s]
+    at_row = lax.broadcasted_iota(jnp.int32, (reach_count, LANES), 0)
+    at_lane = lax.broadcasted_iota(jnp.int32, (reach_count, LANES), 1)
+    base = shape_count * members_dev
+    facts = extra_ref[lower, :]
+    for r in range(reach_count):
+        facts = jnp.where(
+            (at_row == r) & (at_lane == base), level_ref[r].astype(jnp.float32), facts
+        )
+        facts = jnp.where(
+            (at_row == r) & (at_lane == base + 1), down_ref[r].astype(jnp.float32), facts
+        )
+    for g in range(gauge_count):
+        facts = jnp.where(
+            (at_row == g) & (at_lane == base + 2), gauge_ref[g].astype(jnp.float32), facts
+        )
+        facts = jnp.where((at_row == g) & (at_lane == base + 3), sigma_ref[g], facts)
+    upper_top, upper_mid, _ = split_two(extra_ref[:members_dev, :])
+    lower_top, lower_mid, lower_low = split_two(facts)
+    half = LANES // 2
+    lower_top = jnp.where(
+        at_lane < half, lower_top.astype(jnp.float32), pltpu.roll(lower_low, half, 1)
+    )
+    tops = jnp.concatenate([upper_top.astype(jnp.float32), lower_top], axis=0)
+    mids = jnp.concatenate(
+        [upper_mid.astype(jnp.float32), lower_mid.astype(jnp.float32)], axis=0
+    )
+    extras = jnp.concatenate([tops, mids], axis=1).astype(jnp.bfloat16)
+    for k, out_ref in enumerate(out_refs):
+        to = here ^ k
+        for r in range(reach_count):
+            for h in range(block_len // LANES):
+                pieces = [
+                    stage_ref[
+                        h,
+                        pl.ds(
+                            r * block_count * members_dev + share * to + j,
+                            block_count,
+                            stride=members_dev,
+                        ),
+                        :,
+                    ]
+                    for j in range(share)
+                ]
+                out_ref[r * rows : (r + 1) * rows, h * LANES : (h + 1) * LANES] = jnp.concatenate(
+                    pieces, axis=0
+                ).astype(jnp.bfloat16)
+        out_ref[reach_count * rows :, :] = extras
+
+
+def route_body(table_ref, *rest, parts, reach_count, shape_count, gauge_count, members_dev):
+    in_refs, rest = rest[:parts], rest[parts:]
+    out_refs, rest = rest[:parts], rest[parts:]
+    base_ref, state_ref, flows_ref, left_ref, facts_ref, facts_smem, slot_ref, count_ref, sem = rest
+    block_len = table_ref.shape[0] // 2
+    rows = state_ref.shape[1]
+    share = members_dev // parts
+    block_count = rows // share
+    total = parts * reach_count
+    cap = slot_ref.shape[0] // (LEVELS * parts)
+    here = lax.axis_index("basin")
+    half = LANES // 2
+    base = shape_count * members_dev
+    at_lane = lax.broadcasted_iota(jnp.int32, (reach_count, LANES), 1)
+    facts_ref[total:, :] = jnp.zeros((facts_ref.shape[0] - total, LANES), jnp.float32)
+    for k, in_ref in enumerate(in_refs):
+        source = here ^ k
+        extras = in_ref[reach_count * rows :, :].astype(jnp.float32)
+        tops, mids = extras[:, :LANES], extras[:, LANES:]
+        base_ref[source] = tops[:members_dev] + mids[:members_dev]
+        low = pltpu.roll(tops[members_dev:], half, 1)
+        facts_ref[pl.ds(pl.multiple_of(source * reach_count, reach_count), reach_count), :] = jnp.where(
+            at_lane < half, tops[members_dev:] + (mids[members_dev:] + low), 0.0
+        )
+    copy = pltpu.make_async_copy(facts_ref, facts_smem, sem)
+    copy.start()
+    for k, in_ref in enumerate(in_refs):
+        source = here ^ k
+        for r in range(reach_count):
+            state_ref[source * reach_count + r] = in_ref[r * rows : (r + 1) * rows, :].astype(
+                jnp.float32
+            )
+    state_ref[total] = jnp.zeros(state_ref.shape[1:], jnp.float32)
+    state_ref[total + 1] = jnp.zeros(state_ref.shape[1:], jnp.float32)
+    copy.wait()
+
+    def clear(i, carry):
+        slot_ref[i] = total
+        return carry
+
+    lax.fori_loop(0, slot_ref.shape[0], clear, 0, unroll=True)
+
+    def clear_count(i, carry):
+        count_ref[i] = 0
+        return carry
+
+    lax.fori_loop(0, count_ref.shape[0], clear_count, 0, unroll=True)
+
+    def enlist(i, carry):
+        group = facts_smem[i, base].astype(jnp.int32) * parts + i // reach_count
+        taken = count_ref[group]
+        slot_ref[group * cap + jnp.minimum(taken, cap - 1)] = i
+        count_ref[group] = taken + 1
+        return carry
+
+    lax.fori_loop(0, total, enlist, 0)
+    first_row = lax.broadcasted_iota(jnp.int32, (block_count, block_len), 0) == 0
+    slots = parts * cap
+
+    def one_level(level_now, carry):
+        picked = [slot_ref[level_now * slots + c] for c in range(slots)]
+        for c in range(slots):
+            rows_now = state_ref[picked[c]]
+            left_ref[c * rows : (c + 1) * rows, :block_len] = rows_now.astype(jnp.bfloat16)
+            earlier = [
+                jnp.where(
+                    first_row,
+                    0.0,
+                    pltpu.roll(rows_now[j * block_count : (j + 1) * block_count], 1, 0),
+                )
+                for j in range(share)
+            ]
+            left_ref[c * rows : (c + 1) * rows, block_len:] = jnp.concatenate(
+                earlier, axis=0
+            ).astype(jnp.bfloat16)
+        left = left_ref[...]
+        mixed = [
+            jnp.dot(
+                left,
+                table_ref[:, s * block_len : (s + 1) * block_len],
+                preferred_element_type=jnp.float32,
+            )
+            for s in range(shape_count)
+        ]
+        for c in range(slots):
+            pieces = []
+            for j in range(share):
+                at = slice(c * rows + j * block_count, c * rows + (j + 1) * block_count)
+                piece = None
+                for s in range(shape_count):
+                    weight = facts_smem[picked[c], s * members_dev + share * here + j]
+                    term = mixed[s][at] * weight
+                    piece = term if piece is None else piece + term
+                pieces.append(piece)
+            routed = jnp.concatenate(pieces, axis=0).astype(jnp.bfloat16)
+            flows_ref[picked[c]] = routed
+            jump = facts_smem[picked[c], base + 1].astype(jnp.int32)
+            goal = (picked[c] // reach_count) * reach_count + jump
+            kept = (jump < 2 * reach_count) & (goal < total) & (picked[c] < total)
+            goal = jnp.where(kept, goal, total + 1)
+            state_ref[goal] = state_ref[goal] + routed.astype(jnp.float32)
+        return carry
+
+    lax.fori_loop(0, LEVELS, one_level, 0)
+
+    gauges = parts * gauge_count
+    span = block_count * block_len // WINDOWS
+    wide = gauges * WINDOWS
+    per_block = WINDOWS // block_count
+    lag_at = lax.broadcasted_iota(jnp.int32, (block_len, wide), 0)
+    col_at = lax.broadcasted_iota(jnp.int32, (block_len, wide), 1)
+    windowing = jnp.where(lag_at // span == col_at % per_block, 1.0 / span, 0.0).astype(
+        jnp.bfloat16
+    )
+    for g in range(gauges):
+        reach = (g // gauge_count) * reach_count + facts_smem[
+            (g // gauge_count) * reach_count + g % gauge_count, base + 2
+        ].astype(jnp.int32)
+        left_ref[g * rows : (g + 1) * rows, :block_len] = flows_ref[reach]
+    means = jnp.dot(
+        left_ref[: gauges * rows, :block_len], windowing, preferred_element_type=jnp.float32
+    )
+    row_at = lax.broadcasted_iota(jnp.int32, (block_count, wide), 0)
+    col_at = lax.broadcasted_iota(jnp.int32, (block_count, wide), 1)
+    sigma_row = jnp.zeros((1, wide), jnp.float32)
+    for g in range(gauges):
+        sigma = facts_smem[(g // gauge_count) * reach_count + g % gauge_count, base + 3]
+        sigma_row = jnp.where(col_at[:1] // WINDOWS == g, sigma, sigma_row)
+    scaled = []
+    for j in range(share):
+        merged = jnp.zeros((block_count, wide), jnp.float32)
+        for g in range(gauges):
+            at = g * rows + j * block_count
+            merged = jnp.where(
+                (col_at // per_block) == g * block_count + row_at,
+                means[at : at + block_count],
+                merged,
+            )
+        scaled.append(jnp.sum(merged, axis=0, keepdims=True) / sigma_row)
+    scaled = jnp.concatenate(scaled, axis=0)
+    top, mid, low = split_two(scaled)
+    chunks = []
+    for part in (top.astype(jnp.float32), mid.astype(jnp.float32), low):
+        chunks += [part[:, i * block_len : (i + 1) * block_len] for i in range(wide // block_len)]
+    used = len(chunks) * share
+    chunks.append(jnp.zeros((EXTRA - used, block_len), jnp.float32))
+    extras = jnp.concatenate(chunks, axis=0).astype(jnp.bfloat16)
+    for k, out_ref in enumerate(out_refs):
+        to = here ^ k
+        for r in range(reach_count):
+            out_ref[r * rows : (r + 1) * rows, :] = flows_ref[to * reach_count + r]
+        out_ref[reach_count * rows :, :] = extras
+
+
+def gather_body(params_ref, *rest, wide):
+    in_refs, (out_ref, tile_ref) = rest[:-2], rest[-2:]
+    parts = len(in_refs)
+    shape_count, reach_count, members_dev = params_ref.shape
+    share = members_dev // parts
+    block_len = in_refs[0].shape[1]
+    here = lax.axis_index("basin")
+    pieces = wide // block_len
+    at_row = lax.broadcasted_iota(jnp.int32, (members_dev, block_len), 0)
+    placed = [jnp.zeros((members_dev, block_len), jnp.float32)] * pieces
+    for k, in_ref in enumerate(in_refs):
+        extras = in_ref[...].astype(jnp.float32)
+        for i in range(pieces):
+            for j in range(share):
+                value = sum(
+                    extras[(p * pieces + i) * share + j : (p * pieces + i) * share + j + 1]
+                    for p in range(3)
+                )
+                placed[i] = jnp.where(at_row == share * (here ^ k) + j, value, placed[i])
+    for i in range(pieces):
+        out_ref[:, i * block_len : (i + 1) * block_len] = placed[i]
+    place_params(params_ref, tile_ref)
+    out_ref[:, wide:] = tile_ref[...]
+
+
+def place_params(params_ref, tile_ref):
+    shape_count, _, members_dev = params_ref.shape
+    members = members_dev * lax.axis_size("member")
+    tile_ref[...] = jnp.zeros(tile_ref.shape, jnp.float32)
+    for s in range(shape_count):
+        tile_ref[:, s * members : s * members + members_dev] = params_ref[s]
+    tile_ref[...] = pltpu.roll(tile_ref[...], lax.axis_index("member") * members_dev, 1)
+
+
+def unpack_body(*refs, parts, reach_count):
+    in_refs, (out_ref, stage_ref) = refs[:parts], refs[parts:]
+    members_dev = out_ref.shape[1]
+    block_len = in_refs[0].shape[1]
+    share = members_dev // parts
+    block_count = out_ref.shape[2] // block_len
+    rows = share * block_count
+    here = lax.axis_index("basin")
+    for k, in_ref in enumerate(in_refs):
+        source = here ^ k
+        for r in range(reach_count):
+            piece = in_ref[r * rows : (r + 1) * rows, :].astype(jnp.float32)
+            for j in range(share):
+                for h in range(block_len // LANES):
+                    stage_ref[
+                        h,
+                        pl.ds(
+                            r * block_count * members_dev + share * source + j,
+                            block_count,
+                            stride=members_dev,
+                        ),
+                        :,
+                    ] = piece[j * block_count : (j + 1) * block_count, h * LANES : (h + 1) * LANES]
+    for r in range(reach_count):
+        for i in range(block_count):
+            at = (r * block_count + i) * members_dev
+            for h in range(block_len // LANES):
+                lane = i * block_len + h * LANES
+                out_ref[r, :, lane : lane + LANES] = stage_ref[
+                    h, at : at + members_dev, :
+                ].astype(jnp.bfloat16)
+
+
+def solve_body(base_ref, params_ref, *rest):
+    in_refs, (out_ref, all_ref, right_ref) = rest[:-3], rest[-3:]
+    shape_count, reach_count, members_dev = params_ref.shape
+    groups = len(in_refs)
+    members = groups * members_dev
+    wide = all_ref.shape[1]
+    here = lax.axis_index("member")
+    tiles = None
+    for k, in_ref in enumerate(in_refs):
+        at = pl.multiple_of((here ^ k) * members_dev, members_dev)
+        all_ref[pl.ds(at, members_dev), :] = in_ref[:, :wide]
+        tile = in_ref[:, wide:]
+        tiles = tile if tiles is None else tiles + tile
+    scaled = all_ref[...]
+    root = jnp.sqrt(jnp.float32(members - 1))
+    spread = (scaled - jnp.mean(scaled, axis=0, keepdims=True)) / root
+    own = in_refs[0][:, :wide]
+    right_ref[:members, :] = spread
+    for n in range(base_ref.shape[0]):
+        cols = slice(n * base_ref.shape[2], (n + 1) * base_ref.shape[2])
+        right_ref[members : members + members_dev, cols] = base_ref[n] - own[:, cols]
+    right_ref[members + members_dev :, :] = jnp.zeros(
+        (right_ref.shape[0] - members - members_dev, wide), jnp.float32
+    )
+    system = lax.dot_general(
+        spread,
+        right_ref[...],
+        (((1,), (1,)), ((), ())),
+        precision=HIGHEST,
+        preferred_element_type=jnp.float32,
+    )
+    row_at = lax.broadcasted_iota(jnp.int32, system.shape, 0)
+    col_at = lax.broadcasted_iota(jnp.int32, system.shape, 1)
+    system = system + jnp.where(row_at == col_at, 1.0, 0.0)
+    for i in range(members):
+        pivot_row = system[i : i + 1, :] / system[i : i + 1, i : i + 1]
+        system = jnp.where(row_at == i, pivot_row, system - system[:, i : i + 1] * pivot_row)
+    gain = system[:, members : members + members_dev]
+    theta = jnp.concatenate(
+        [tiles[:, s * members : (s + 1) * members] for s in range(shape_count)], axis=0
+    )
+    anomaly = theta - jnp.mean(theta, axis=1, keepdims=True)
+    step = (
+        jnp.dot(anomaly, gain, precision=HIGHEST, preferred_element_type=jnp.float32) / root
+    )
+    for s in range(shape_count):
+        out_ref[s] = params_ref[s] + step[s * reach_count : (s + 1) * reach_count]
+
+
+def exchanged(x, axis, by):
+    length = lax.axis_size(axis)
+    return lax.ppermute(x, axis, [(i, i ^ by) for i in range(length)])
+
+
+def per_device_split(
+    runoff,
+    route_params,
+    unit_shapes,
+    level_map,
+    down_map,
+    gauge_reach,
+    gauge_sigma,
+    observed,
+    obs_noise,
+):
+    f32, bf16 = jnp.float32, jnp.bfloat16
+    parts, groups = lax.axis_size("basin"), lax.axis_size("member")
+    reach_count, members_dev, series_len = runoff.shape
+    shape_count, block_len = unit_shapes.shape
+    gauge_count = observed.shape[0]
+    block_count = series_len // block_len
+    share = members_dev // parts
+    rows = share * block_count
+    total = parts * reach_count
+    cap = reach_count // 4
+    wide = parts * gauge_count * WINDOWS
+    members = members_dev * groups
+    sent = jax.ShapeDtypeStruct((reach_count * rows + EXTRA, block_len), bf16)
+    packed = pl.pallas_call(
+        pack_body,
+        out_shape=[sent] * parts,
+        in_specs=[smem()] * 4 + [vmem()] * 4,
+        out_specs=[vmem()] * parts,
+        scratch_shapes=[
+            pltpu.VMEM((block_len // LANES, reach_count * members_dev * block_count, LANES), f32),
+            pltpu.VMEM((members_dev + reach_count, LANES), f32),
+        ],
+        name="pack",
+    )(level_map, down_map, gauge_reach, gauge_sigma, runoff, route_params, observed, obs_noise)
+    arrived = [packed[0]] + [exchanged(packed[k], "basin", k) for k in range(1, parts)]
+    conv_table = kernel_table(unit_shapes)
+    *routed, noise_base = pl.pallas_call(
+        functools.partial(
+            route_body,
+            parts=parts,
+            reach_count=reach_count,
+            shape_count=shape_count,
+            gauge_count=gauge_count,
+            members_dev=members_dev,
+        ),
+        out_shape=[sent] * parts
+        + [jax.ShapeDtypeStruct((parts, members_dev, gauge_count * WINDOWS), f32)],
+        in_specs=[vmem()] * (1 + parts),
+        out_specs=[vmem()] * (parts + 1),
+        scratch_shapes=[
+            pltpu.VMEM((total + 2, rows, block_len), f32),
+            pltpu.VMEM((total + 1, rows, block_len), bf16),
+            pltpu.VMEM((parts * max(cap, gauge_count) * rows, 2 * block_len), bf16),
+            pltpu.VMEM((total + 8, LANES), f32),
+            pltpu.SMEM((total + 8, LANES), f32),
+            pltpu.SMEM((LEVELS * parts * cap,), jnp.int32),
+            pltpu.SMEM((LEVELS * parts,), jnp.int32),
+            pltpu.SemaphoreType.DMA,
+        ],
+        name="route",
+    )(conv_table, *arrived)
+    returned = [routed[0]] + [exchanged(routed[k], "basin", k) for k in range(1, parts)]
+    last = (reach_count * rows) // EXTRA
+    local = pl.pallas_call(
+        functools.partial(gather_body, wide=wide),
+        grid=(1,),
+        out_shape=jax.ShapeDtypeStruct((members_dev, wide + LANES), f32),
+        in_specs=[pl.BlockSpec(route_params.shape, lambda i: (0, 0, 0))]
+        + [pl.BlockSpec((EXTRA, block_len), lambda i: (last, 0))] * parts,
+        out_specs=pl.BlockSpec((members_dev, wide + LANES), lambda i: (0, 0)),
+        scratch_shapes=[pltpu.VMEM((reach_count, LANES), f32)],
+        name="gather",
+    )(route_params, *returned)
+    everyone = [local] + [exchanged(local, "member", k) for k in range(1, groups)]
+    flows = pl.pallas_call(
+        functools.partial(unpack_body, parts=parts, reach_count=reach_count),
+        out_shape=jax.ShapeDtypeStruct(runoff.shape, bf16),
+        in_specs=[vmem()] * parts,
+        out_specs=vmem(),
+        scratch_shapes=[pltpu.VMEM((block_len // LANES, reach_count * members_dev * block_count, LANES), f32)],
+        name="unpack",
+    )(*returned)
+    updated = pl.pallas_call(
+        solve_body,
+        out_shape=jax.ShapeDtypeStruct(route_params.shape, f32),
+        in_specs=[vmem()] * (2 + groups),
+        out_specs=vmem(),
+        scratch_shapes=[pltpu.VMEM((members, wide), f32), pltpu.VMEM((LANES, wide), f32)],
+        name="solve",
+    )(noise_base, route_params, *everyone)
+    return flows, updated
+
+
+def power_of_two(x):
+    return x & (x - 1) == 0
+
+
+def per_device(*args):
+    runoff, route_params, unit_shapes, _, _, _, _, observed, _ = args
+    parts, groups = lax.axis_size("basin"), lax.axis_size("member")
+    reach_count, members_dev, series_len = runoff.shape
+    shape_count, block_len = unit_shapes.shape
+    block_count = series_len // block_len
+    gauge_count = observed.shape[0]
+    wide = parts * gauge_count * WINDOWS
+    share = max(members_dev // parts, 1)
+    fits = (
+        power_of_two(parts)
+        and power_of_two(groups)
+        and members_dev == share * parts
+        and reach_count == 8
+        and members_dev == 8
+        and block_count == 8
+        and series_len % block_len == 0
+        and block_len == 2 * LANES
+        and gauge_count * WINDOWS == LANES
+        and wide % block_len == 0
+        and 3 * share * (wide // block_len) <= EXTRA
+        and (shape_count * members_dev + 4) * 2 <= LANES
+        and shape_count * groups * members_dev <= LANES
+        and groups * members_dev + members_dev <= LANES
+    )
+    if fits:
+        return per_device_split(*args)
+    return per_device_chain(*args)
 
 
 def passed_along(x, axis, by):
     length = lax.axis_size(axis)
     pairs = [(i, i + by) for i in range(length) if 0 <= i + by < length]
     return lax.ppermute(x, axis, pairs)
-
-
-def kernel_table(unit_shapes):
-    block_len = unit_shapes.shape[1]
-    row_ids = jnp.arange(2 * block_len, dtype=jnp.int32)[:, None]
-    col_ids = jnp.arange(block_len, dtype=jnp.int32)[None, :]
-    lag_index = jnp.where(row_ids < block_len, col_ids - row_ids, 2 * block_len + col_ids - row_ids)
-    usable = (lag_index >= 0) & (lag_index < block_len)
-    shape_values = jnp.take(unit_shapes, jnp.clip(lag_index, 0, block_len - 1), axis=1)
-    shape_values = jnp.where(usable[None], shape_values, 0.0) / block_len
-    return jnp.transpose(shape_values, (1, 0, 2)).reshape(2 * block_len, -1).astype(jnp.bfloat16)
 
 
 def route_rows(inflow_rows, slot_weights, conv_table):
@@ -52,7 +573,7 @@
     return (select, slot_valid, slot_target)
 
 
-def per_device(
+def per_device_chain(
     runoff,
     route_params,
     unit_shapes,

time: 596 us -> 42.4 us (0.07)
  local copies, waits for them, and re-layouts: 475 us -> 1.88 us
  blocking collectives: 33.5 us -> 0 us
  other arithmetic: 25.5 us -> 0 us
  starting transfers between devices: 35.4 us -> 12 us
  Pallas kernels: 0 us -> 17.6 us
  matrix products: 17.2 us -> 0 us
    gather x2 -> x0, local copies, waits for them, and re-layouts: 468 us -> none  [kernel_table(): jnp.take(unit_shapes, jnp.clip(lag_index, 0, block_len - 1), axis=1)]
    ppermute x9, starting transfers between devices: 35.4 us -> 12 us  [exchanged(): return lax.ppermute(x, axis, [(i, i ^ by) for i in range(length)])]
    psum x1 -> x0, blocking collectives: 17.9 us -> none  [per_device(): gram_part, cross_part = lax.psum((gram_part, cross_part), 'basin')]
    pallas_call x0 -> x6, Pallas kernels: none -> 17.6 us  [the longest x1 6.17 us: per_device_split(): pl.pallas_call(functools.partial(route_body, parts=parts, reach_count=rea...]
    dot_general x42 -> x0, matrix products: 16.7 us -> none  [the longest x8 6.31 us: per_device(): jnp.dot(edge_matrix, routed, preferred_element_type=jnp.float32)]
    all_gather x3 -> x0, blocking collectives: 15.6 us -> none  [the longest x1 5.22 us: per_device(): lax.all_gather(route_params, 'member', axis=2, tiled=True)]
    lt x12 -> x0, other arithmetic: 10.9 us -> none  [the longest x11 10.9 us: level_select(): slot_valid = slot_ids < jnp.sum(in_level.astype(jnp.int32))]
    another operation x5 -> x0, other arithmetic: 6.8 us -> none  [the longest x3 3.67 us: per_device(): factor = jnp.linalg.cholesky(gram)]
  transfers between devices with their start and end apart: 9 -> 9, of which waited for: 6 -> 6; matrix products, arithmetic and copies ran while one was open for 83% -> 0% of each run, Pallas kernels for 0% -> 8%
where the time goes in v1:
time: 42.4 us; the launch traced here: 42.1 us
  Pallas kernels  17.6 us (42%)
  starting transfers between devices  12 us (28%)
  waiting for transfers between devices  9.94 us (23%)
  local copies, waits for them, and re-layouts  1.88 us (4%)
  between operations  0.66 us (2%)
    ppermute x9, starting transfers between devices, exchanged(): return lax.ppermute(x, axis, [(i, i ^ by) for i in range(length)])  12 us
    ppermute x9, waiting for transfers between devices, exchanged(): return lax.ppermute(x, axis, [(i, i ^ by) for i in range(length)])  9.94 us
    pallas_call x1, Pallas kernels, per_device_split(): pl.pallas_call(functools.partial(route_body, parts=parts, reach_count=rea...  6.17 us
    pallas_call x1, Pallas kernels, per_device_split(): pl.pallas_call(solve_body, out_shape=jax.ShapeDtypeStruct(route_params.sh...  4.53 us
    pallas_call x1, Pallas kernels, per_device_split(): pl.pallas_call(pack_body, out_shape=[sent] * parts, in_specs=[smem()] * 4...  1.9 us
    unnamed x18, local copies, waits for them, and re-layouts  1.88 us
    pallas_call x1, Pallas kernels, per_device_split(): pl.pallas_call(functools.partial(unpack_body, parts=parts, reach_count=re...  1.81 us
    pallas_call x1, Pallas kernels, kernel_table(): pl.pallas_call(table_body, out_shape=jax.ShapeDtypeStruct((2 * block_len,...  1.71 us
  transfers between devices with their start and end apart: 9, of which 6 were waited for; matrix products, arithmetic and copies ran while one was open for 0% of the time, Pallas kernels for 8%

profile of v1, /device:TPU:0, one launch (start us, length us, event | category | flops | bytes accessed | tf_op | source)
XLA Modules:
  0.0 42.1 jit_solution(681435764913601696)
XLA Ops:
  0.6 1.9 %pack.1 = (bf16[144,256]{1,0:T(8,128)(2,1)}, bf16[144,256]{1,0:T(8,128)(2,1)}, bf16[144,256]{1,0:T(8,128)(2,1)}, bf16[144,256]{1,0:T(8,128)(2,1)}) custom-call(s32[8]{0:T(128)} %level_ref.1, s32[8]{0:T(128)} %down_ref.1, s32[2]{0:T(128)} %gauge_ref.1, f32[2]{0:T(128)} %sigma_ref.1, bf16[8,8,2048]{2,1,0:T(8,128)(2,1)} %runoff_ref.1, f32[3,8,8]{2,1,0:T(8,128)} %params_ref.5, ...), custom_call_target="tpu_custom_call" | custom-call | tf_op jit(solution)/shard_map/pack/pallas_call | solution.py:438
  2.5 3.1 %collective-permute-start = (bf16[144,256]{1,0:T(8,128)(2,1)}, bf16[144,256]{1,0:T(8,128)(2,1)S(1)}, u32[]{:S(2)}, u32[]{:S(2)}) collective-permute-start(bf16[144,256]{1,0:T(8,128)(2,1)} %get-tuple-element.12), channel_id=1, source_target_pairs={{0,4},{4,0},{8,12},{12,8},{1,5},{5,1},{9,13},{13,9},{2,6},{6,2},{1... | collective-permute-start | bytes 221192 | tf_op jit(solution)/shard_map/ppermute | solution.py:411
  5.6 2.6 %collective-permute-start.1 = (bf16[144,256]{1,0:T(8,128)(2,1)}, bf16[144,256]{1,0:T(8,128)(2,1)S(1)}, u32[]{:S(2)}, u32[]{:S(2)}) collective-permute-start(bf16[144,256]{1,0:T(8,128)(2,1)} %get-tuple-element.13), channel_id=1, source_target_pairs={{0,8},{4,12},{8,0},{12,4},{1,9},{5,13},{9,1},{13,5},{2,10},{6,14},... | collective-permute-start | bytes 221192 | tf_op jit(solution)/shard_map/ppermute | solution.py:411
  8.2 0.0 collective-permute-start.2
  8.2 1.7 %table.1.table_ref = bf16[512,768]{1,0:T(8,128)(2,1)} custom-call(f32[3,256]{1,0:T(4,128)} %shapes_ref.1), custom_call_target="tpu_custom_call" | custom-call | tf_op jit(solution)/shard_map/table/pallas_call | solution.py:39
  9.9 0.0 collective-permute-done.rest_1_
  9.9 0.0 copy-start.3
  9.9 3.7 %collective-permute-done.1.rest_2_ = bf16[144,256]{1,0:T(8,128)(2,1)S(1)} collective-permute-done((bf16[144,256]{1,0:T(8,128)(2,1)}, bf16[144,256]{1,0:T(8,128)(2,1)S(1)}, u32[]{:S(2)}, u32[]{:S(2)}) %collective-permute-start.1) | collective-permute-done | bytes 73760 | tf_op jit(solution)/shard_map/ppermute | solution.py:411
  13.6 0.0 copy-start.4
  13.6 1.1 %collective-permute-done.2.rest_3_ = bf16[144,256]{1,0:T(8,128)(2,1)S(1)} collective-permute-done((bf16[144,256]{1,0:T(8,128)(2,1)}, bf16[144,256]{1,0:T(8,128)(2,1)S(1)}, u32[]{:S(2)}, u32[]{:S(2)}) %collective-permute-start.2) | collective-permute-done | bytes 73760 | tf_op jit(solution)/shard_map/ppermute | solution.py:411
  14.6 0.0 copy-start.5
  14.6 0.0 copy-done.3
  14.6 0.0 copy-done.4
  14.6 0.6 %copy-done.5 = bf16[144,256]{1,0:T(8,128)(2,1)} copy-done((bf16[144,256]{1,0:T(8,128)(2,1)}, bf16[144,256]{1,0:T(8,128)(2,1)S(1)}, u32[]{:S(2)}) %copy-start.5) | copy-done | bytes 73752
  15.3 6.2 %route.1 = (bf16[144,256]{1,0:T(8,128)(2,1)}, bf16[144,256]{1,0:T(8,128)(2,1)}, bf16[144,256]{1,0:T(8,128)(2,1)}, bf16[144,256]{1,0:T(8,128)(2,1)}, f32[4,8,128]{2,1,0:T(8,128)}) custom-call(bf16[512,768]{1,0:T(8,128)(2,1)} %table.1.table_ref, bf16[144,256]{1,0:T(8,128)(2,1)} %get-tuple-element.11.rest_0_, bf16[144,256]{1,0:T(8,128)(2,1)} %copy-done.3, ...), custom_call_target="tpu_custom_call" | custom-call | tf_op jit(solution)/shard_map/route/pallas_call | solution.py:451
  21.4 1.2 %collective-permute-start.3 = (bf16[144,256]{1,0:T(8,128)(2,1)}, bf16[144,256]{1,0:T(8,128)(2,1)S(1)}, u32[]{:S(2)}, u32[]{:S(2)}) collective-permute-start(bf16[144,256]{1,0:T(8,128)(2,1)} %get-tuple-element.16), channel_id=1, source_target_pairs={{0,4},{4,0},{8,12},{12,8},{1,5},{5,1},{9,13},{13,9},{2,6},{6,2},{1... | collective-permute-start | bytes 221192 | tf_op jit(solution)/shard_map/ppermute | solution.py:411
  22.6 1.7 %collective-permute-start.4 = (bf16[144,256]{1,0:T(8,128)(2,1)}, bf16[144,256]{1,0:T(8,128)(2,1)S(1)}, u32[]{:S(2)}, u32[]{:S(2)}) collective-permute-start(bf16[144,256]{1,0:T(8,128)(2,1)} %get-tuple-element.17), channel_id=1, source_target_pairs={{0,8},{4,12},{8,0},{12,4},{1,9},{5,13},{9,1},{13,5},{2,10},{6,14},... | collective-permute-start | bytes 221192 | tf_op jit(solution)/shard_map/ppermute | solution.py:411
  24.3 1.6 %collective-permute-start.5 = (bf16[144,256]{1,0:T(8,128)(2,1)}, bf16[144,256]{1,0:T(8,128)(2,1)S(1)}, u32[]{:S(2)}, u32[]{:S(2)}) collective-permute-start(bf16[144,256]{1,0:T(8,128)(2,1)} %get-tuple-element.18), channel_id=1, source_target_pairs={{0,12},{4,8},{8,4},{12,0},{1,13},{5,9},{9,5},{13,1},{2,14},{6,10},... | collective-permute-start | bytes 221192 | tf_op jit(solution)/shard_map/ppermute | solution.py:411
  25.9 0.2 collective-permute-done.3.refs_1_.rest_1_
  26.1 0.0 copy-start
  26.1 3.2 %collective-permute-done.4.refs_2_.rest_2_ = bf16[144,256]{1,0:T(8,128)(2,1)S(1)} collective-permute-done((bf16[144,256]{1,0:T(8,128)(2,1)}, bf16[144,256]{1,0:T(8,128)(2,1)S(1)}, u32[]{:S(2)}, u32[]{:S(2)}) %collective-permute-start.4) | collective-permute-done | bytes 73760 | tf_op jit(solution)/shard_map/ppermute | solution.py:411
  29.3 0.0 copy-start.1
  29.3 1.5 %collective-permute-done.5.refs_3_.rest_3_ = bf16[144,256]{1,0:T(8,128)(2,1)S(1)} collective-permute-done((bf16[144,256]{1,0:T(8,128)(2,1)}, bf16[144,256]{1,0:T(8,128)(2,1)S(1)}, u32[]{:S(2)}, u32[]{:S(2)}) %collective-permute-start.5) | collective-permute-done | bytes 73760 | tf_op jit(solution)/shard_map/ppermute | solution.py:411
  30.8 0.0 copy-start.2
  30.8 0.0 copy-done
  30.8 0.0 copy-done.1
  30.8 0.6 %copy-done.2 = bf16[144,256]{1,0:T(8,128)(2,1)} copy-done((bf16[144,256]{1,0:T(8,128)(2,1)}, bf16[144,256]{1,0:T(8,128)(2,1)S(1)}, u32[]{:S(2)}) %copy-start.2) | copy-done | bytes 73752
  31.4 1.5 %gather.1.rest_0_ = f32[8,640]{1,0:T(8,128)} custom-call(f32[3,8,8]{2,1,0:T(8,128)} %params_ref.5, bf16[144,256]{1,0:T(8,128)(2,1)} %get-tuple-element.15.refs_0_.rest_0_, bf16[144,256]{1,0:T(8,128)(2,1)} %copy-done, bf16[144,256]{1,0:T(8,128)(2,1)} %copy-done.1, bf16[144,256]{1,0:T(8,128)(2,1)} %copy-done.2), custom_call_target="tpu_custom_call" | custom-call | tf_op jit(solution)/shard_map/gather/pallas_call | solution.py:478
  32.9 0.0 collective-permute-start.8
  32.9 1.5 %collective-permute-start.7 = (f32[8,640]{1,0:T(8,128)}, f32[8,640]{1,0:T(8,128)S(1)}, u32[]{:S(2)}, u32[]{:S(2)}) collective-permute-start(f32[8,640]{1,0:T(8,128)} %gather.1.rest_0_), channel_id=1, source_target_pairs={{0,2},{1,3},{2,0},{3,1},{4,6},{5,7},{6,4},{7,5},{8,10},{9,11},{10,... | collective-permute-start | bytes 61448 | tf_op jit(solution)/shard_map/ppermute | solution.py:411
  34.4 0.4 collective-permute-start.6
  34.8 1.8 %unpack.1 = bf16[8,8,2048]{2,1,0:T(8,128)(2,1)} custom-call(bf16[144,256]{1,0:T(8,128)(2,1)} %get-tuple-element.15.refs_0_.rest_0_, bf16[144,256]{1,0:T(8,128)(2,1)} %copy-done, bf16[144,256]{1,0:T(8,128)(2,1)} %copy-done.1, bf16[144,256]{1,0:T(8,128)(2,1)} %copy-done.2), custom_call_target="tpu_custom_call" | custom-call | tf_op jit(solution)/shard_map/unpack/pallas_call | solution.py:489
  36.6 0.0 collective-permute-done.8.rest_3_
  36.6 0.0 copy-start.6
  36.6 0.3 collective-permute-done.7.rest_2_
  36.9 0.0 copy-start.7
  36.9 0.0 collective-permute-done.6.rest_1_
  36.9 0.0 copy-start.8
  36.9 0.3 copy-done.6
  37.2 0.3 copy-done.7
  37.5 0.0 copy-done.8
  37.5 4.5 %solve.1 = f32[3,8,8]{2,1,0:T(8,128)} custom-call(f32[4,8,128]{2,1,0:T(8,128)} %get-tuple-element.19.base_ref, f32[3,8,8]{2,1,0:T(8,128)} %params_ref.5, f32[8,640]{1,0:T(8,128)} %gather.1.rest_0_, f32[8,640]{1,0:T(8,128)} %copy-done.8, f32[8,640]{1,0:T(8,128)} %copy-done.7, f32[8,640]{1,0:T(8,128)} %copy-done.6), custom_call_target="tpu_custom_call" | custom-call | tf_op jit(solution)/shard_map/solve/pallas_call | solution.py:497
Async XLA Ops:
  2.5 7.4 %collective-permute-start = (bf16[144,256]{1,0:T(8,128)(2,1)}, bf16[144,256]{1,0:T(8,128)(2,1)S(1)}, u32[]{:S(2)}, u32[]{:S(2)}) collective-permute-start(bf16[144,256]{1,0:T(8,128)(2,1)} %get-tuple-element.12), channel_id=1, source_target_pairs={{0,4},{4,0},{8,12},{12,8},{1,5},{5,1},{9,13},{13,9},{2,6},{6,2},{1... | collective-permute-start | bytes 221192 | tf_op jit(solution)/shard_map/ppermute | solution.py:411
  5.6 8.0 %collective-permute-start.1 = (bf16[144,256]{1,0:T(8,128)(2,1)}, bf16[144,256]{1,0:T(8,128)(2,1)S(1)}, u32[]{:S(2)}, u32[]{:S(2)}) collective-permute-start(bf16[144,256]{1,0:T(8,128)(2,1)} %get-tuple-element.13), channel_id=1, source_target_pairs={{0,8},{4,12},{8,0},{12,4},{1,9},{5,13},{9,1},{13,5},{2,10},{6,14},... | collective-permute-start | bytes 221192 | tf_op jit(solution)/shard_map/ppermute | solution.py:411
  8.2 6.5 %collective-permute-start.2 = (bf16[144,256]{1,0:T(8,128)(2,1)}, bf16[144,256]{1,0:T(8,128)(2,1)S(1)}, u32[]{:S(2)}, u32[]{:S(2)}) collective-permute-start(bf16[144,256]{1,0:T(8,128)(2,1)} %get-tuple-element.14), channel_id=1, source_target_pairs={{0,12},{4,8},{8,4},{12,0},{1,13},{5,9},{9,5},{13,1},{2,14},{6,10},... | collective-permute-start | bytes 221192 | tf_op jit(solution)/shard_map/ppermute | solution.py:411
  9.9 4.7 %copy-start.3 = (bf16[144,256]{1,0:T(8,128)(2,1)}, bf16[144,256]{1,0:T(8,128)(2,1)S(1)}, u32[]{:S(2)}) copy-start(bf16[144,256]{1,0:T(8,128)(2,1)S(1)} %collective-permute-done.rest_1_) | copy-start | bytes 221188
  13.6 1.1 %copy-start.4 = (bf16[144,256]{1,0:T(8,128)(2,1)}, bf16[144,256]{1,0:T(8,128)(2,1)S(1)}, u32[]{:S(2)}) copy-start(bf16[144,256]{1,0:T(8,128)(2,1)S(1)} %collective-permute-done.1.rest_2_) | copy-start | bytes 221188
  14.6 0.6 %copy-start.5 = (bf16[144,256]{1,0:T(8,128)(2,1)}, bf16[144,256]{1,0:T(8,128)(2,1)S(1)}, u32[]{:S(2)}) copy-start(bf16[144,256]{1,0:T(8,128)(2,1)S(1)} %collective-permute-done.2.rest_3_) | copy-start | bytes 221188
  21.4 4.6 %collective-permute-start.3 = (bf16[144,256]{1,0:T(8,128)(2,1)}, bf16[144,256]{1,0:T(8,128)(2,1)S(1)}, u32[]{:S(2)}, u32[]{:S(2)}) collective-permute-start(bf16[144,256]{1,0:T(8,128)(2,1)} %get-tuple-element.16), channel_id=1, source_target_pairs={{0,4},{4,0},{8,12},{12,8},{1,5},{5,1},{9,13},{13,9},{2,6},{6,2},{1... | collective-permute-start | bytes 221192 | tf_op jit(solution)/shard_map/ppermute | solution.py:411
  22.6 6.7 %collective-permute-start.4 = (bf16[144,256]{1,0:T(8,128)(2,1)}, bf16[144,256]{1,0:T(8,128)(2,1)S(1)}, u32[]{:S(2)}, u32[]{:S(2)}) collective-permute-start(bf16[144,256]{1,0:T(8,128)(2,1)} %get-tuple-element.17), channel_id=1, source_target_pairs={{0,8},{4,12},{8,0},{12,4},{1,9},{5,13},{9,1},{13,5},{2,10},{6,14},... | collective-permute-start | bytes 221192 | tf_op jit(solution)/shard_map/ppermute | solution.py:411
  24.3 6.5 %collective-permute-start.5 = (bf16[144,256]{1,0:T(8,128)(2,1)}, bf16[144,256]{1,0:T(8,128)(2,1)S(1)}, u32[]{:S(2)}, u32[]{:S(2)}) collective-permute-start(bf16[144,256]{1,0:T(8,128)(2,1)} %get-tuple-element.18), channel_id=1, source_target_pairs={{0,12},{4,8},{8,4},{12,0},{1,13},{5,9},{9,5},{13,1},{2,14},{6,10},... | collective-permute-start | bytes 221192 | tf_op jit(solution)/shard_map/ppermute | solution.py:411
  26.1 4.7 %copy-start = (bf16[144,256]{1,0:T(8,128)(2,1)}, bf16[144,256]{1,0:T(8,128)(2,1)S(1)}, u32[]{:S(2)}) copy-start(bf16[144,256]{1,0:T(8,128)(2,1)S(1)} %collective-permute-done.3.refs_1_.rest_1_) | copy-start | bytes 221188
  29.3 1.5 %copy-start.1 = (bf16[144,256]{1,0:T(8,128)(2,1)}, bf16[144,256]{1,0:T(8,128)(2,1)S(1)}, u32[]{:S(2)}) copy-start(bf16[144,256]{1,0:T(8,128)(2,1)S(1)} %collective-permute-done.4.refs_2_.rest_2_) | copy-start | bytes 221188
  30.8 0.6 %copy-start.2 = (bf16[144,256]{1,0:T(8,128)(2,1)}, bf16[144,256]{1,0:T(8,128)(2,1)S(1)}, u32[]{:S(2)}) copy-start(bf16[144,256]{1,0:T(8,128)(2,1)S(1)} %collective-permute-done.5.refs_3_.rest_3_) | copy-start | bytes 221188
  32.9 3.7 %collective-permute-start.8 = (f32[8,640]{1,0:T(8,128)}, f32[8,640]{1,0:T(8,128)S(1)}, u32[]{:S(2)}, u32[]{:S(2)}) collective-permute-start(f32[8,640]{1,0:T(8,128)} %gather.1.rest_0_), channel_id=1, source_target_pairs={{0,3},{1,2},{2,1},{3,0},{4,7},{5,6},{6,5},{7,4},{8,11},{9,10},{10,... | collective-permute-start | bytes 61448 | tf_op jit(solution)/shard_map/ppermute | solution.py:411
  32.9 4.0 %collective-permute-start.7 = (f32[8,640]{1,0:T(8,128)}, f32[8,640]{1,0:T(8,128)S(1)}, u32[]{:S(2)}, u32[]{:S(2)}) collective-permute-start(f32[8,640]{1,0:T(8,128)} %gather.1.rest_0_), channel_id=1, source_target_pairs={{0,2},{1,3},{2,0},{3,1},{4,6},{5,7},{6,4},{7,5},{8,10},{9,11},{10,... | collective-permute-start | bytes 61448 | tf_op jit(solution)/shard_map/ppermute | solution.py:411
  34.4 2.5 %collective-permute-start.6 = (f32[8,640]{1,0:T(8,128)}, f32[8,640]{1,0:T(8,128)S(1)}, u32[]{:S(2)}, u32[]{:S(2)}) collective-permute-start(f32[8,640]{1,0:T(8,128)} %gather.1.rest_0_), channel_id=1, source_target_pairs={{0,1},{1,0},{2,3},{3,2},{4,5},{5,4},{6,7},{7,6},{8,9},{9,8},{10,11... | collective-permute-start | bytes 61448 | tf_op jit(solution)/shard_map/ppermute | solution.py:411
  36.6 0.6 %copy-start.6 = (f32[8,640]{1,0:T(8,128)}, f32[8,640]{1,0:T(8,128)S(1)}, u32[]{:S(2)}) copy-start(f32[8,640]{1,0:T(8,128)S(1)} %collective-permute-done.8.rest_3_) | copy-start | bytes 61444
  36.9 0.6 %copy-start.7 = (f32[8,640]{1,0:T(8,128)}, f32[8,640]{1,0:T(8,128)S(1)}, u32[]{:S(2)}) copy-start(f32[8,640]{1,0:T(8,128)S(1)} %collective-permute-done.7.rest_2_) | copy-start | bytes 61444
  36.9 0.6 %copy-start.8 = (f32[8,640]{1,0:T(8,128)}, f32[8,640]{1,0:T(8,128)S(1)}, u32[]{:S(2)}) copy-start(f32[8,640]{1,0:T(8,128)S(1)} %collective-permute-done.6.rest_1_) | copy-start | bytes 61444

commit v2 on v1

--- a/solution.py
+++ b/solution.py
@@ -19,6 +19,10 @@
 
 def smem():
     return pl.BlockSpec(memory_space=pltpu.SMEM)
+
+
+def kept(x):
+    return pltpu.with_memory_space_constraint(x, pltpu.VMEM)
 
 
 def table_body(shapes_ref, table_ref):
@@ -38,7 +42,7 @@
     shape_count, block_len = unit_shapes.shape
     return pl.pallas_call(
         table_body,
-        out_shape=jax.ShapeDtypeStruct((2 * block_len, shape_count * block_len), jnp.bfloat16),
+        out_shape=pltpu.VMEM((2 * block_len, shape_count * block_len), jnp.bfloat16),
         in_specs=[vmem()],
         out_specs=vmem(),
         name="table",
@@ -301,7 +305,7 @@
     at_row = lax.broadcasted_iota(jnp.int32, (members_dev, block_len), 0)
     placed = [jnp.zeros((members_dev, block_len), jnp.float32)] * pieces
     for k, in_ref in enumerate(in_refs):
-        extras = in_ref[...].astype(jnp.float32)
+        extras = in_ref[in_ref.shape[0] - EXTRA :, :].astype(jnp.float32)
         for i in range(pieces):
             for j in range(share):
                 value = sum(
@@ -434,7 +438,7 @@
     cap = reach_count // 4
     wide = parts * gauge_count * WINDOWS
     members = members_dev * groups
-    sent = jax.ShapeDtypeStruct((reach_count * rows + EXTRA, block_len), bf16)
+    sent = pltpu.VMEM((reach_count * rows + EXTRA, block_len), bf16)
     packed = pl.pallas_call(
         pack_body,
         out_shape=[sent] * parts,
@@ -458,7 +462,7 @@
             members_dev=members_dev,
         ),
         out_shape=[sent] * parts
-        + [jax.ShapeDtypeStruct((parts, members_dev, gauge_count * WINDOWS), f32)],
+        + [pltpu.VMEM((parts, members_dev, gauge_count * WINDOWS), f32)],
         in_specs=[vmem()] * (1 + parts),
         out_specs=[vmem()] * (parts + 1),
         scratch_shapes=[
@@ -472,19 +476,16 @@
             pltpu.SemaphoreType.DMA,
         ],
         name="route",
-    )(conv_table, *arrived)
+    )(kept(conv_table), *map(kept, arrived))
     returned = [routed[0]] + [exchanged(routed[k], "basin", k) for k in range(1, parts)]
-    last = (reach_count * rows) // EXTRA
     local = pl.pallas_call(
         functools.partial(gather_body, wide=wide),
-        grid=(1,),
-        out_shape=jax.ShapeDtypeStruct((members_dev, wide + LANES), f32),
-        in_specs=[pl.BlockSpec(route_params.shape, lambda i: (0, 0, 0))]
-        + [pl.BlockSpec((EXTRA, block_len), lambda i: (last, 0))] * parts,
-        out_specs=pl.BlockSpec((members_dev, wide + LANES), lambda i: (0, 0)),
+        out_shape=pltpu.VMEM((members_dev, wide + LANES), f32),
+        in_specs=[vmem()] * (1 + parts),
+        out_specs=vmem(),
         scratch_shapes=[pltpu.VMEM((reach_count, LANES), f32)],
         name="gather",
-    )(route_params, *returned)
+    )(route_params, *map(kept, returned))
     everyone = [local] + [exchanged(local, "member", k) for k in range(1, groups)]
     flows = pl.pallas_call(
         functools.partial(unpack_body, parts=parts, reach_count=reach_count),
@@ -493,7 +494,7 @@
         out_specs=vmem(),
         scratch_shapes=[pltpu.VMEM((block_len // LANES, reach_count * members_dev * block_count, LANES), f32)],
         name="unpack",
-    )(*returned)
+    )(*map(kept, returned))
     updated = pl.pallas_call(
         solve_body,
         out_shape=jax.ShapeDtypeStruct(route_params.shape, f32),
@@ -501,7 +502,7 @@
         out_specs=vmem(),
         scratch_shapes=[pltpu.VMEM((members, wide), f32), pltpu.VMEM((LANES, wide), f32)],
         name="solve",
-    )(noise_base, route_params, *everyone)
+    )(kept(noise_base), route_params, *map(kept, everyone))
     return flows, updated
 
 

time: 42.4 us -> 36.6 us (0.86)
  Pallas kernels: 17.6 us -> 12.4 us
  local copies, waits for them, and re-layouts: 1.88 us -> 0 us
  waiting for transfers between devices: 9.94 us -> 11.2 us
    pallas_call x1, Pallas kernels: 6.17 us -> 4.26 us  [per_device_split(): pl.pallas_call(functools.partial(route_body, parts=parts, reach_count=rea...]
    unnamed x18 -> x0, local copies, waits for them, and re-layouts: 1.88 us -> none
    pallas_call x2, Pallas kernels: 3.22 us -> 1.68 us  [the longest x1 0.85 us: per_device_split(): pl.pallas_call(functools.partial(gather_body, wide=wide), out_shape=pltpu...]
    ppermute x9, waiting for transfers between devices: 9.94 us -> 11.2 us  [exchanged(): return lax.ppermute(x, axis, [(i, i ^ by) for i in range(length)])]
    pallas_call x1, Pallas kernels: 1.81 us -> 0.82 us  [per_device_split(): pl.pallas_call(functools.partial(unpack_body, parts=parts, reach_count=re...]
    pallas_call x1, Pallas kernels: 1.9 us -> 1.22 us  [per_device_split(): pl.pallas_call(pack_body, out_shape=[sent] * parts, in_specs=[smem()] * 4...]
  transfers between devices with their start and end apart: 9 -> 9, of which waited for: 6 -> 6; matrix products, arithmetic and copies ran while one was open for 0% -> 0% of each run, Pallas kernels for 8% -> 5%
where the time goes in v2:
time: 36.6 us; the launch traced here: 36.3 us
  Pallas kernels  12.4 us (34%)
  starting transfers between devices  12 us (33%)
  waiting for transfers between devices  11.2 us (31%)
  between operations  0.67 us (2%)
    ppermute x9, starting transfers between devices, exchanged(): return lax.ppermute(x, axis, [(i, i ^ by) for i in range(length)])  12 us
    ppermute x9, waiting for transfers between devices, exchanged(): return lax.ppermute(x, axis, [(i, i ^ by) for i in range(length)])  11.2 us
    pallas_call x1, Pallas kernels, per_device_split(): pl.pallas_call(solve_body, out_shape=jax.ShapeDtypeStruct(route_params.sh...  4.43 us
    pallas_call x1, Pallas kernels, per_device_split(): pl.pallas_call(functools.partial(route_body, parts=parts, reach_count=rea...  4.26 us
    pallas_call x1, Pallas kernels, per_device_split(): pl.pallas_call(pack_body, out_shape=[sent] * parts, in_specs=[smem()] * 4...  1.22 us
    pallas_call x1, Pallas kernels, per_device_split(): pl.pallas_call(functools.partial(gather_body, wide=wide), out_shape=pltpu...  0.85 us
    pallas_call x1, Pallas kernels, kernel_table(): pl.pallas_call(table_body, out_shape=pltpu.VMEM((2 * block_len, shape_cou...  0.83 us
    pallas_call x1, Pallas kernels, per_device_split(): pl.pallas_call(functools.partial(unpack_body, parts=parts, reach_count=re...  0.82 us
  transfers between devices with their start and end apart: 9, of which 6 were waited for; matrix products, arithmetic and copies ran while one was open for 0% of the time, Pallas kernels for 5%

profile of v2, /device:TPU:0, one launch (start us, length us, event | category | flops | bytes accessed | tf_op | source)
XLA Modules:
  0.0 36.3 jit_solution(1124292942849559509)
XLA Ops:
  0.6 1.2 %pack.1 = (bf16[144,256]{1,0:T(8,128)(2,1)S(1)}, bf16[144,256]{1,0:T(8,128)(2,1)S(1)}, bf16[144,256]{1,0:T(8,128)(2,1)S(1)}, bf16[144,256]{1,0:T(8,128)(2,1)S(1)}) custom-call(s32[8]{0:T(128)} %level_ref.1, s32[8]{0:T(128)} %down_ref.1, s32[2]{0:T(128)} %gauge_ref.1, f32[2]{0:T(128)} %sigma_ref.1, bf16[8,8,2048]{2,1,0:T(8,128)(2,1)} %runoff_ref.1, ...), custom_call_target="tpu_custom_call" | custom-call | tf_op jit(solution)/shard_map/pack/pallas_call | solution.py:442
  1.9 3.1 %collective-permute-start = (bf16[144,256]{1,0:T(8,128)(2,1)S(1)}, bf16[144,256]{1,0:T(8,128)(2,1)S(1)}, u32[]{:S(2)}, u32[]{:S(2)}) collective-permute-start(bf16[144,256]{1,0:T(8,128)(2,1)S(1)} %get-tuple-element.12), channel_id=1, source_target_pairs={{0,4},{4,0},{8,12},{12,8},{1,5},{5,1},{9,13},{13,9},{2,6},{6,2},{1... | collective-permute-start | bytes 221192 | tf_op jit(solution)/shard_map/ppermute | solution.py:415
  5.0 2.6 %collective-permute-start.1 = (bf16[144,256]{1,0:T(8,128)(2,1)S(1)}, bf16[144,256]{1,0:T(8,128)(2,1)S(1)}, u32[]{:S(2)}, u32[]{:S(2)}) collective-permute-start(bf16[144,256]{1,0:T(8,128)(2,1)S(1)} %get-tuple-element.13), channel_id=1, source_target_pairs={{0,8},{4,12},{8,0},{12,4},{1,9},{5,13},{9,1},{13,5},{2,10},{6,14},... | collective-permute-start | bytes 221192 | tf_op jit(solution)/shard_map/ppermute | solution.py:415
  7.6 0.0 collective-permute-start.2
  7.6 0.8 %table.1.table_ref = bf16[512,768]{1,0:T(8,128)(2,1)S(1)} custom-call(f32[3,256]{1,0:T(4,128)} %shapes_ref.1), custom_call_target="tpu_custom_call" | custom-call | tf_op jit(solution)/shard_map/table/pallas_call | solution.py:43
  8.4 0.0 collective-permute-done.rest_1_
  8.4 4.3 %collective-permute-done.1.rest_2_ = bf16[144,256]{1,0:T(8,128)(2,1)S(1)} collective-permute-done((bf16[144,256]{1,0:T(8,128)(2,1)S(1)}, bf16[144,256]{1,0:T(8,128)(2,1)S(1)}, u32[]{:S(2)}, u32[]{:S(2)}) %collective-permute-start.1) | collective-permute-done | bytes 73760 | tf_op jit(solution)/shard_map/ppermute | solution.py:415
  12.8 1.1 %collective-permute-done.2.rest_3_ = bf16[144,256]{1,0:T(8,128)(2,1)S(1)} collective-permute-done((bf16[144,256]{1,0:T(8,128)(2,1)S(1)}, bf16[144,256]{1,0:T(8,128)(2,1)S(1)}, u32[]{:S(2)}, u32[]{:S(2)}) %collective-permute-start.2) | collective-permute-done | bytes 73760 | tf_op jit(solution)/shard_map/ppermute | solution.py:415
  13.8 4.3 %route.1 = (bf16[144,256]{1,0:T(8,128)(2,1)S(1)}, bf16[144,256]{1,0:T(8,128)(2,1)S(1)}, bf16[144,256]{1,0:T(8,128)(2,1)S(1)}, bf16[144,256]{1,0:T(8,128)(2,1)S(1)}, f32[4,8,128]{2,1,0:T(8,128)S(1)}) custom-call(bf16[512,768]{1,0:T(8,128)(2,1)S(1)} %table.1.table_ref, bf16[144,256]{1,0:T(8,128)(2,1)S(1)} %get-tuple-element.11.rest_0_, ...), custom_call_target="tpu_custom_call" | custom-call | tf_op jit(solution)/shard_map/route/pallas_call | solution.py:455
  18.1 1.2 %collective-permute-start.3 = (bf16[144,256]{1,0:T(8,128)(2,1)S(1)}, bf16[144,256]{1,0:T(8,128)(2,1)S(1)}, u32[]{:S(2)}, u32[]{:S(2)}) collective-permute-start(bf16[144,256]{1,0:T(8,128)(2,1)S(1)} %get-tuple-element.16), channel_id=1, source_target_pairs={{0,4},{4,0},{8,12},{12,8},{1,5},{5,1},{9,13},{13,9},{2,6},{6,2},{1... | collective-permute-start | bytes 221192 | tf_op jit(solution)/shard_map/ppermute | solution.py:415
  19.2 1.7 %collective-permute-start.4 = (bf16[144,256]{1,0:T(8,128)(2,1)S(1)}, bf16[144,256]{1,0:T(8,128)(2,1)S(1)}, u32[]{:S(2)}, u32[]{:S(2)}) collective-permute-start(bf16[144,256]{1,0:T(8,128)(2,1)S(1)} %get-tuple-element.17), channel_id=1, source_target_pairs={{0,8},{4,12},{8,0},{12,4},{1,9},{5,13},{9,1},{13,5},{2,10},{6,14},... | collective-permute-start | bytes 221192 | tf_op jit(solution)/shard_map/ppermute | solution.py:415
  20.9 1.6 %collective-permute-start.5 = (bf16[144,256]{1,0:T(8,128)(2,1)S(1)}, bf16[144,256]{1,0:T(8,128)(2,1)S(1)}, u32[]{:S(2)}, u32[]{:S(2)}) collective-permute-start(bf16[144,256]{1,0:T(8,128)(2,1)S(1)} %get-tuple-element.18), channel_id=1, source_target_pairs={{0,12},{4,8},{8,4},{12,0},{1,13},{5,9},{9,5},{13,1},{2,14},{6,10},... | collective-permute-start | bytes 221192 | tf_op jit(solution)/shard_map/ppermute | solution.py:415
  22.5 0.0 collective-permute-done.3.refs_1_.rest_1_
  22.5 3.2 %collective-permute-done.4.refs_2_.rest_2_ = bf16[144,256]{1,0:T(8,128)(2,1)S(1)} collective-permute-done((bf16[144,256]{1,0:T(8,128)(2,1)S(1)}, bf16[144,256]{1,0:T(8,128)(2,1)S(1)}, u32[]{:S(2)}, u32[]{:S(2)}) %collective-permute-start.4) | collective-permute-done | bytes 73760 | tf_op jit(solution)/shard_map/ppermute | solution.py:415
  25.7 1.4 %collective-permute-done.5.refs_3_.rest_3_ = bf16[144,256]{1,0:T(8,128)(2,1)S(1)} collective-permute-done((bf16[144,256]{1,0:T(8,128)(2,1)S(1)}, bf16[144,256]{1,0:T(8,128)(2,1)S(1)}, u32[]{:S(2)}, u32[]{:S(2)}) %collective-permute-start.5) | collective-permute-done | bytes 73760 | tf_op jit(solution)/shard_map/ppermute | solution.py:415
  27.2 0.9 %gather.1.rest_0_ = f32[8,640]{1,0:T(8,128)S(1)} custom-call(f32[3,8,8]{2,1,0:T(8,128)} %params_ref.5, bf16[144,256]{1,0:T(8,128)(2,1)S(1)} %get-tuple-element.15.refs_0_.rest_0_, bf16[144,256]{1,0:T(8,128)(2,1)S(1)} %collective-permute-done.3.refs_1_.rest_1_, bf16[144,256]{1,0:T(8,128)(2,1)S(1)} %collective-permute-done.4.refs_2_.rest_2_, ...), custom_call_target="tpu_custom_call" | custom-call | tf_op jit(solution)/shard_map/gather/pallas_call | solution.py:481
  28.0 0.0 collective-permute-start.8
  28.0 1.5 %collective-permute-start.7 = (f32[8,640]{1,0:T(8,128)S(1)}, f32[8,640]{1,0:T(8,128)S(1)}, u32[]{:S(2)}, u32[]{:S(2)}) collective-permute-start(f32[8,640]{1,0:T(8,128)S(1)} %gather.1.rest_0_), channel_id=1, source_target_pairs={{0,2},{1,3},{2,0},{3,1},{4,6},{5,7},{6,4},{7,5},{8,10},{9,11},{10,... | collective-permute-start | bytes 61448 | tf_op jit(solution)/shard_map/ppermute | solution.py:415
  29.5 0.3 collective-permute-start.6
  29.9 0.8 %unpack.1 = bf16[8,8,2048]{2,1,0:T(8,128)(2,1)} custom-call(bf16[144,256]{1,0:T(8,128)(2,1)S(1)} %get-tuple-element.15.refs_0_.rest_0_, bf16[144,256]{1,0:T(8,128)(2,1)S(1)} %collective-permute-done.3.refs_1_.rest_1_, bf16[144,256]{1,0:T(8,128)(2,1)S(1)} %collective-permute-done.4.refs_2_.rest_2_, bf16[144,256]{1,0:T(8,128)(2,1)S(1)} %collective-permute-done.5.refs_3_.rest_3_), custom_call_target="tpu_custom_call" | custom-call | tf_op jit(solution)/shard_map/unpack/pallas_call | solution.py:490
  30.7 0.7 %collective-permute-done.8.rest_3_ = f32[8,640]{1,0:T(8,128)S(1)} collective-permute-done((f32[8,640]{1,0:T(8,128)S(1)}, f32[8,640]{1,0:T(8,128)S(1)}, u32[]{:S(2)}, u32[]{:S(2)}) %collective-permute-start.8) | collective-permute-done | bytes 20512 | tf_op jit(solution)/shard_map/ppermute | solution.py:415
  31.4 0.4 %collective-permute-done.7.rest_2_ = f32[8,640]{1,0:T(8,128)S(1)} collective-permute-done((f32[8,640]{1,0:T(8,128)S(1)}, f32[8,640]{1,0:T(8,128)S(1)}, u32[]{:S(2)}, u32[]{:S(2)}) %collective-permute-start.7) | collective-permute-done | bytes 20512 | tf_op jit(solution)/shard_map/ppermute | solution.py:415
  31.8 0.0 collective-permute-done.6.rest_1_
  31.8 4.4 %solve.1 = f32[3,8,8]{2,1,0:T(8,128)} custom-call(f32[4,8,128]{2,1,0:T(8,128)S(1)} %get-tuple-element.19.base_ref, f32[3,8,8]{2,1,0:T(8,128)} %params_ref.5, f32[8,640]{1,0:T(8,128)S(1)} %gather.1.rest_0_, f32[8,640]{1,0:T(8,128)S(1)} %collective-permute-done.6.rest_1_, f32[8,640]{1,0:T(8,128)S(1)} %collective-permute-done.7.rest_2_, ...), custom_call_target="tpu_custom_call" | custom-call | tf_op jit(solution)/shard_map/solve/pallas_call | solution.py:498
Async XLA Ops:
  1.9 6.6 %collective-permute-start = (bf16[144,256]{1,0:T(8,128)(2,1)S(1)}, bf16[144,256]{1,0:T(8,128)(2,1)S(1)}, u32[]{:S(2)}, u32[]{:S(2)}) collective-permute-start(bf16[144,256]{1,0:T(8,128)(2,1)S(1)} %get-tuple-element.12), channel_id=1, source_target_pairs={{0,4},{4,0},{8,12},{12,8},{1,5},{5,1},{9,13},{13,9},{2,6},{6,2},{1... | collective-permute-start | bytes 221192 | tf_op jit(solution)/shard_map/ppermute | solution.py:415
  5.0 7.8 %collective-permute-start.1 = (bf16[144,256]{1,0:T(8,128)(2,1)S(1)}, bf16[144,256]{1,0:T(8,128)(2,1)S(1)}, u32[]{:S(2)}, u32[]{:S(2)}) collective-permute-start(bf16[144,256]{1,0:T(8,128)(2,1)S(1)} %get-tuple-element.13), channel_id=1, source_target_pairs={{0,8},{4,12},{8,0},{12,4},{1,9},{5,13},{9,1},{13,5},{2,10},{6,14},... | collective-permute-start | bytes 221192 | tf_op jit(solution)/shard_map/ppermute | solution.py:415
  7.6 6.3 %collective-permute-start.2 = (bf16[144,256]{1,0:T(8,128)(2,1)S(1)}, bf16[144,256]{1,0:T(8,128)(2,1)S(1)}, u32[]{:S(2)}, u32[]{:S(2)}) collective-permute-start(bf16[144,256]{1,0:T(8,128)(2,1)S(1)} %get-tuple-element.14), channel_id=1, source_target_pairs={{0,12},{4,8},{8,4},{12,0},{1,13},{5,9},{9,5},{13,1},{2,14},{6,10},... | collective-permute-start | bytes 221192 | tf_op jit(solution)/shard_map/ppermute | solution.py:415
  18.1 4.5 %collective-permute-start.3 = (bf16[144,256]{1,0:T(8,128)(2,1)S(1)}, bf16[144,256]{1,0:T(8,128)(2,1)S(1)}, u32[]{:S(2)}, u32[]{:S(2)}) collective-permute-start(bf16[144,256]{1,0:T(8,128)(2,1)S(1)} %get-tuple-element.16), channel_id=1, source_target_pairs={{0,4},{4,0},{8,12},{12,8},{1,5},{5,1},{9,13},{13,9},{2,6},{6,2},{1... | collective-permute-start | bytes 221192 | tf_op jit(solution)/shard_map/ppermute | solution.py:415
  19.2 6.5 %collective-permute-start.4 = (bf16[144,256]{1,0:T(8,128)(2,1)S(1)}, bf16[144,256]{1,0:T(8,128)(2,1)S(1)}, u32[]{:S(2)}, u32[]{:S(2)}) collective-permute-start(bf16[144,256]{1,0:T(8,128)(2,1)S(1)} %get-tuple-element.17), channel_id=1, source_target_pairs={{0,8},{4,12},{8,0},{12,4},{1,9},{5,13},{9,1},{13,5},{2,10},{6,14},... | collective-permute-start | bytes 221192 | tf_op jit(solution)/shard_map/ppermute | solution.py:415
  20.9 6.3 %collective-permute-start.5 = (bf16[144,256]{1,0:T(8,128)(2,1)S(1)}, bf16[144,256]{1,0:T(8,128)(2,1)S(1)}, u32[]{:S(2)}, u32[]{:S(2)}) collective-permute-start(bf16[144,256]{1,0:T(8,128)(2,1)S(1)} %get-tuple-element.18), channel_id=1, source_target_pairs={{0,12},{4,8},{8,4},{12,0},{1,13},{5,9},{9,5},{13,1},{2,14},{6,10},... | collective-permute-start | bytes 221192 | tf_op jit(solution)/shard_map/ppermute | solution.py:415
  28.0 3.4 %collective-permute-start.8 = (f32[8,640]{1,0:T(8,128)S(1)}, f32[8,640]{1,0:T(8,128)S(1)}, u32[]{:S(2)}, u32[]{:S(2)}) collective-permute-start(f32[8,640]{1,0:T(8,128)S(1)} %gather.1.rest_0_), channel_id=1, source_target_pairs={{0,3},{1,2},{2,1},{3,0},{4,7},{5,6},{6,5},{7,4},{8,11},{9,10},{10,... | collective-permute-start | bytes 61448 | tf_op jit(solution)/shard_map/ppermute | solution.py:415
  28.0 3.8 %collective-permute-start.7 = (f32[8,640]{1,0:T(8,128)S(1)}, f32[8,640]{1,0:T(8,128)S(1)}, u32[]{:S(2)}, u32[]{:S(2)}) collective-permute-start(f32[8,640]{1,0:T(8,128)S(1)} %gather.1.rest_0_), channel_id=1, source_target_pairs={{0,2},{1,3},{2,0},{3,1},{4,6},{5,7},{6,4},{7,5},{8,10},{9,11},{10,... | collective-permute-start | bytes 61448 | tf_op jit(solution)/shard_map/ppermute | solution.py:415
  29.5 2.3 %collective-permute-start.6 = (f32[8,640]{1,0:T(8,128)S(1)}, f32[8,640]{1,0:T(8,128)S(1)}, u32[]{:S(2)}, u32[]{:S(2)}) collective-permute-start(f32[8,640]{1,0:T(8,128)S(1)} %gather.1.rest_0_), channel_id=1, source_target_pairs={{0,1},{1,0},{2,3},{3,2},{4,5},{5,4},{6,7},{7,6},{8,9},{9,8},{10,11... | collective-permute-start | bytes 61448 | tf_op jit(solution)/shard_map/ppermute | solution.py:415

commit v3 on v2

--- a/solution.py
+++ b/solution.py
@@ -19,6 +19,9 @@
 
 def smem():
     return pl.BlockSpec(memory_space=pltpu.SMEM)
+
+
+AHEAD = 8
 
 
 def kept(x):
@@ -67,7 +70,7 @@
     noise_ref,
     *rest,
 ):
-    out_refs, (stage_ref, extra_ref) = rest[:-2], rest[-2:]
+    out_refs, (own_ref, tile_ref, stage_ref, extra_ref) = rest[:-4], rest[-4:]
     reach_count, members_dev, series_len = runoff_ref.shape
     shape_count = params_ref.shape[0]
     gauge_count, windows = observed_ref.shape
@@ -95,18 +98,21 @@
     at_lane = lax.broadcasted_iota(jnp.int32, (reach_count, LANES), 1)
     base = shape_count * members_dev
     facts = extra_ref[lower, :]
+    cap = reach_count // 4
+    facts = jnp.where(at_lane // cap == base // cap, jnp.float32(reach_count), facts)
     for r in range(reach_count):
-        facts = jnp.where(
-            (at_row == r) & (at_lane == base), level_ref[r].astype(jnp.float32), facts
-        )
-        facts = jnp.where(
-            (at_row == r) & (at_lane == base + 1), down_ref[r].astype(jnp.float32), facts
-        )
+        rank = jnp.int32(0)
+        for q in range(r):
+            rank = rank + (level_ref[q] == level_ref[r]).astype(jnp.int32)
+        here_slot = (at_row == level_ref[r]) & (at_lane == base + rank)
+        facts = jnp.where(here_slot, jnp.float32(r), facts)
+        goal_slot = (at_row == level_ref[r]) & (at_lane == base + cap + rank)
+        facts = jnp.where(goal_slot, down_ref[r].astype(jnp.float32), facts)
     for g in range(gauge_count):
         facts = jnp.where(
-            (at_row == g) & (at_lane == base + 2), gauge_ref[g].astype(jnp.float32), facts
+            (at_row == g) & (at_lane == base + 2 * cap), gauge_ref[g].astype(jnp.float32), facts
         )
-        facts = jnp.where((at_row == g) & (at_lane == base + 3), sigma_ref[g], facts)
+        facts = jnp.where((at_row == g) & (at_lane == base + 2 * cap + 1), sigma_ref[g], facts)
     upper_top, upper_mid, _ = split_two(extra_ref[:members_dev, :])
     lower_top, lower_mid, lower_low = split_two(facts)
     half = LANES // 2
@@ -138,18 +144,20 @@
                     pieces, axis=0
                 ).astype(jnp.bfloat16)
         out_ref[reach_count * rows :, :] = extras
+    own_ref[...] = params_ref[...]
+    place_params(params_ref, tile_ref)
 
 
 def route_body(table_ref, *rest, parts, reach_count, shape_count, gauge_count, members_dev):
     in_refs, rest = rest[:parts], rest[parts:]
     out_refs, rest = rest[:parts], rest[parts:]
-    base_ref, state_ref, flows_ref, left_ref, facts_ref, facts_smem, slot_ref, count_ref, sem = rest
+    base_ref, state_ref, flows_ref, left_ref, facts_ref, facts_smem, sem = rest
     block_len = table_ref.shape[0] // 2
     rows = state_ref.shape[1]
     share = members_dev // parts
     block_count = rows // share
     total = parts * reach_count
-    cap = slot_ref.shape[0] // (LEVELS * parts)
+    cap = reach_count // 4
     here = lax.axis_index("basin")
     half = LANES // 2
     base = shape_count * members_dev
@@ -176,31 +184,20 @@
     state_ref[total + 1] = jnp.zeros(state_ref.shape[1:], jnp.float32)
     copy.wait()
 
-    def clear(i, carry):
-        slot_ref[i] = total
-        return carry
-
-    lax.fori_loop(0, slot_ref.shape[0], clear, 0, unroll=True)
-
-    def clear_count(i, carry):
-        count_ref[i] = 0
-        return carry
-
-    lax.fori_loop(0, count_ref.shape[0], clear_count, 0, unroll=True)
-
-    def enlist(i, carry):
-        group = facts_smem[i, base].astype(jnp.int32) * parts + i // reach_count
-        taken = count_ref[group]
-        slot_ref[group * cap + jnp.minimum(taken, cap - 1)] = i
-        count_ref[group] = taken + 1
-        return carry
-
-    lax.fori_loop(0, total, enlist, 0)
     first_row = lax.broadcasted_iota(jnp.int32, (block_count, block_len), 0) == 0
     slots = parts * cap
 
     def one_level(level_now, carry):
-        picked = [slot_ref[level_now * slots + c] for c in range(slots)]
+        picked, goals = [], []
+        for c in range(slots):
+            at = (c // cap) * reach_count + level_now
+            lane = base + c % cap
+            reach = facts_smem[at, lane].astype(jnp.int32)
+            goal = (c // cap) * reach_count + facts_smem[at, lane + cap].astype(jnp.int32)
+            real = reach < reach_count
+            kept_goal = (goal < (c // cap + 2) * reach_count) & (goal < total) & real
+            picked.append(jnp.where(real, (c // cap) * reach_count + reach, total))
+            goals.append(jnp.where(kept_goal, goal, total + 1))
         for c in range(slots):
             rows_now = state_ref[picked[c]]
             left_ref[c * rows : (c + 1) * rows, :block_len] = rows_now.astype(jnp.bfloat16)
@@ -236,11 +233,7 @@
                 pieces.append(piece)
             routed = jnp.concatenate(pieces, axis=0).astype(jnp.bfloat16)
             flows_ref[picked[c]] = routed
-            jump = facts_smem[picked[c], base + 1].astype(jnp.int32)
-            goal = (picked[c] // reach_count) * reach_count + jump
-            kept = (jump < 2 * reach_count) & (goal < total) & (picked[c] < total)
-            goal = jnp.where(kept, goal, total + 1)
-            state_ref[goal] = state_ref[goal] + routed.astype(jnp.float32)
+            state_ref[goals[c]] = state_ref[goals[c]] + routed.astype(jnp.float32)
         return carry
 
     lax.fori_loop(0, LEVELS, one_level, 0)
@@ -256,7 +249,7 @@
     )
     for g in range(gauges):
         reach = (g // gauge_count) * reach_count + facts_smem[
-            (g // gauge_count) * reach_count + g % gauge_count, base + 2
+            (g // gauge_count) * reach_count + g % gauge_count, base + 2 * cap
         ].astype(jnp.int32)
         left_ref[g * rows : (g + 1) * rows, :block_len] = flows_ref[reach]
     means = jnp.dot(
@@ -266,7 +259,7 @@
     col_at = lax.broadcasted_iota(jnp.int32, (block_count, wide), 1)
     sigma_row = jnp.zeros((1, wide), jnp.float32)
     for g in range(gauges):
-        sigma = facts_smem[(g // gauge_count) * reach_count + g % gauge_count, base + 3]
+        sigma = facts_smem[(g // gauge_count) * reach_count + g % gauge_count, base + 2 * cap + 1]
         sigma_row = jnp.where(col_at[:1] // WINDOWS == g, sigma, sigma_row)
     scaled = []
     for j in range(share):
@@ -294,10 +287,10 @@
         out_ref[reach_count * rows :, :] = extras
 
 
-def gather_body(params_ref, *rest, wide):
-    in_refs, (out_ref, tile_ref) = rest[:-2], rest[-2:]
+def gather_body(tile_ref, *rest, wide):
+    in_refs, out_ref = rest[:-1], rest[-1]
     parts = len(in_refs)
-    shape_count, reach_count, members_dev = params_ref.shape
+    members_dev = out_ref.shape[0]
     share = members_dev // parts
     block_len = in_refs[0].shape[1]
     here = lax.axis_index("basin")
@@ -315,7 +308,6 @@
                 placed[i] = jnp.where(at_row == share * (here ^ k) + j, value, placed[i])
     for i in range(pieces):
         out_ref[:, i * block_len : (i + 1) * block_len] = placed[i]
-    place_params(params_ref, tile_ref)
     out_ref[:, wide:] = tile_ref[...]
 
 
@@ -395,9 +387,20 @@
     row_at = lax.broadcasted_iota(jnp.int32, system.shape, 0)
     col_at = lax.broadcasted_iota(jnp.int32, system.shape, 1)
     system = system + jnp.where(row_at == col_at, 1.0, 0.0)
-    for i in range(members):
-        pivot_row = system[i : i + 1, :] / system[i : i + 1, i : i + 1]
-        system = jnp.where(row_at == i, pivot_row, system - system[:, i : i + 1] * pivot_row)
+    for first in range(0, members, AHEAD):
+        cols = [
+            jnp.broadcast_to(system[:, i : i + 1], system.shape)
+            for i in range(first, first + AHEAD)
+        ]
+        for t in range(AHEAD):
+            i = first + t
+            own_row = row_at == i
+            inverse = 1.0 / cols[t][i : i + 1, :]
+            pivot_row = system[i : i + 1, :] * inverse
+            system = jnp.where(own_row, pivot_row, system - cols[t] * pivot_row)
+            for u in range(t + 1, AHEAD):
+                pivot_row = cols[u][i : i + 1, :] * inverse
+                cols[u] = jnp.where(own_row, pivot_row, cols[u] - cols[t] * pivot_row)
     gain = system[:, members : members + members_dev]
     theta = jnp.concatenate(
         [tiles[:, s * members : (s + 1) * members] for s in range(shape_count)], axis=0
@@ -439,11 +442,12 @@
     wide = parts * gauge_count * WINDOWS
     members = members_dev * groups
     sent = pltpu.VMEM((reach_count * rows + EXTRA, block_len), bf16)
-    packed = pl.pallas_call(
+    *packed, own_params, tile = pl.pallas_call(
         pack_body,
-        out_shape=[sent] * parts,
+        out_shape=[sent] * parts
+        + [pltpu.VMEM(route_params.shape, f32), pltpu.VMEM((reach_count, LANES), f32)],
         in_specs=[smem()] * 4 + [vmem()] * 4,
-        out_specs=[vmem()] * parts,
+        out_specs=[vmem()] * (parts + 2),
         scratch_shapes=[
             pltpu.VMEM((block_len // LANES, reach_count * members_dev * block_count, LANES), f32),
             pltpu.VMEM((members_dev + reach_count, LANES), f32),
@@ -471,8 +475,6 @@
             pltpu.VMEM((parts * max(cap, gauge_count) * rows, 2 * block_len), bf16),
             pltpu.VMEM((total + 8, LANES), f32),
             pltpu.SMEM((total + 8, LANES), f32),
-            pltpu.SMEM((LEVELS * parts * cap,), jnp.int32),
-            pltpu.SMEM((LEVELS * parts,), jnp.int32),
             pltpu.SemaphoreType.DMA,
         ],
         name="route",
@@ -483,9 +485,8 @@
         out_shape=pltpu.VMEM((members_dev, wide + LANES), f32),
         in_specs=[vmem()] * (1 + parts),
         out_specs=vmem(),
-        scratch_shapes=[pltpu.VMEM((reach_count, LANES), f32)],
         name="gather",
-    )(route_params, *map(kept, returned))
+    )(kept(tile), *map(kept, returned))
     everyone = [local] + [exchanged(local, "member", k) for k in range(1, groups)]
     flows = pl.pallas_call(
         functools.partial(unpack_body, parts=parts, reach_count=reach_count),
@@ -502,7 +503,7 @@
         out_specs=vmem(),
         scratch_shapes=[pltpu.VMEM((members, wide), f32), pltpu.VMEM((LANES, wide), f32)],
         name="solve",
-    )(kept(noise_base), route_params, *map(kept, everyone))
+    )(kept(noise_base), kept(own_params), *map(kept, everyone))
     return flows, updated
 
 
@@ -531,7 +532,8 @@
         and gauge_count * WINDOWS == LANES
         and wide % block_len == 0
         and 3 * share * (wide // block_len) <= EXTRA
-        and (shape_count * members_dev + 4) * 2 <= LANES
+        and (shape_count * members_dev + 8) * 2 <= LANES
+        and reach_count == LEVELS
         and shape_count * groups * members_dev <= LANES
         and groups * members_dev + members_dev <= LANES
     )

time: 36.6 us -> 32.5 us (0.89)
  Pallas kernels: 12.4 us -> 8.28 us
    pallas_call x1, Pallas kernels: 4.43 us -> 1.84 us  [per_device_split(): pl.pallas_call(solve_body, out_shape=jax.ShapeDtypeStruct(route_params.sh...]
    pallas_call x1, Pallas kernels: 0.85 us -> 0.02 us  [per_device_split(): pl.pallas_call(functools.partial(gather_body, wide=wide), out_shape=pltpu...]
    pallas_call x1, Pallas kernels: 4.26 us -> 3.55 us  [per_device_split(): pl.pallas_call(functools.partial(route_body, parts=parts, reach_count=rea...]
where the time goes in v3:
time: 32.5 us; the launch traced here: 32.3 us
  starting transfers between devices  12.1 us (37%)
  waiting for transfers between devices  11.2 us (34%)
  Pallas kernels  8.28 us (25%)
  between operations  0.68 us (2%)
    ppermute x9, starting transfers between devices, exchanged(): return lax.ppermute(x, axis, [(i, i ^ by) for i in range(length)])  12.1 us
    ppermute x9, waiting for transfers between devices, exchanged(): return lax.ppermute(x, axis, [(i, i ^ by) for i in range(length)])  11.2 us
    pallas_call x1, Pallas kernels, per_device_split(): pl.pallas_call(functools.partial(route_body, parts=parts, reach_count=rea...  3.55 us
    pallas_call x1, Pallas kernels, per_device_split(): pl.pallas_call(solve_body, out_shape=jax.ShapeDtypeStruct(route_params.sh...  1.84 us
    pallas_call x1, Pallas kernels, per_device_split(): pl.pallas_call(pack_body, out_shape=[sent] * parts + [pltpu.VMEM(route_pa...  1.22 us
    pallas_call x1, Pallas kernels, kernel_table(): pl.pallas_call(table_body, out_shape=pltpu.VMEM((2 * block_len, shape_cou...  0.83 us
    pallas_call x1, Pallas kernels, per_device_split(): pl.pallas_call(functools.partial(unpack_body, parts=parts, reach_count=re...  0.82 us
  transfers between devices with their start and end apart: 9, of which 6 were waited for; matrix products, arithmetic and copies ran while one was open for 0% of the time, Pallas kernels for 5%

profile of v3, /device:TPU:0, one launch (start us, length us, event | category | flops | bytes accessed | tf_op | source)
XLA Modules:
  0.0 32.3 jit_solution(6597623098345731530)
XLA Ops:
  0.6 1.2 %pack.1 = (bf16[144,256]{1,0:T(8,128)(2,1)S(1)}, bf16[144,256]{1,0:T(8,128)(2,1)S(1)}, bf16[144,256]{1,0:T(8,128)(2,1)S(1)}, bf16[144,256]{1,0:T(8,128)(2,1)S(1)...) custom-call(s32[8]{0:T(128)} %level_ref.1, s32[8]{0:T(128)} %down_ref.1, s32[2]{0:T(128)} %gauge_ref.1, f32[2]{0:T(128)} %sigma_ref.1, ...), custom_call_target="tpu_custom_call" | custom-call | tf_op jit(solution)/shard_map/pack/pallas_call | solution.py:445
  1.9 3.1 %collective-permute-start = (bf16[144,256]{1,0:T(8,128)(2,1)S(1)}, bf16[144,256]{1,0:T(8,128)(2,1)S(1)}, u32[]{:S(2)}, u32[]{:S(2)}) collective-permute-start(bf16[144,256]{1,0:T(8,128)(2,1)S(1)} %get-tuple-element.14), channel_id=1, source_target_pairs={{0,4},{4,0},{8,12},{12,8},{1,5},{5,1},{9,13},{13,9},{2,6},{6,2},{1... | collective-permute-start | bytes 221192 | tf_op jit(solution)/shard_map/ppermute | solution.py:418
  5.0 2.6 %collective-permute-start.1 = (bf16[144,256]{1,0:T(8,128)(2,1)S(1)}, bf16[144,256]{1,0:T(8,128)(2,1)S(1)}, u32[]{:S(2)}, u32[]{:S(2)}) collective-permute-start(bf16[144,256]{1,0:T(8,128)(2,1)S(1)} %get-tuple-element.15), channel_id=1, source_target_pairs={{0,8},{4,12},{8,0},{12,4},{1,9},{5,13},{9,1},{13,5},{2,10},{6,14},... | collective-permute-start | bytes 221192 | tf_op jit(solution)/shard_map/ppermute | solution.py:418
  7.6 0.0 collective-permute-start.2
  7.6 0.8 %table.1.table_ref = bf16[512,768]{1,0:T(8,128)(2,1)S(1)} custom-call(f32[3,256]{1,0:T(4,128)} %shapes_ref.1), custom_call_target="tpu_custom_call" | custom-call | tf_op jit(solution)/shard_map/table/pallas_call | solution.py:46
  8.4 0.0 collective-permute-done.rest_1_
  8.4 4.3 %collective-permute-done.1.rest_2_ = bf16[144,256]{1,0:T(8,128)(2,1)S(1)} collective-permute-done((bf16[144,256]{1,0:T(8,128)(2,1)S(1)}, bf16[144,256]{1,0:T(8,128)(2,1)S(1)}, u32[]{:S(2)}, u32[]{:S(2)}) %collective-permute-start.1) | collective-permute-done | bytes 73760 | tf_op jit(solution)/shard_map/ppermute | solution.py:418
  12.8 1.1 %collective-permute-done.2.rest_3_ = bf16[144,256]{1,0:T(8,128)(2,1)S(1)} collective-permute-done((bf16[144,256]{1,0:T(8,128)(2,1)S(1)}, bf16[144,256]{1,0:T(8,128)(2,1)S(1)}, u32[]{:S(2)}, u32[]{:S(2)}) %collective-permute-start.2) | collective-permute-done | bytes 73760 | tf_op jit(solution)/shard_map/ppermute | solution.py:418
  13.8 3.5 %route.1 = (bf16[144,256]{1,0:T(8,128)(2,1)S(1)}, bf16[144,256]{1,0:T(8,128)(2,1)S(1)}, bf16[144,256]{1,0:T(8,128)(2,1)S(1)}, bf16[144,256]{1,0:T(8,128)(2,1)S(1)}, f32[4,8,128]{2,1,0:T(8,128)S(1)}) custom-call(bf16[512,768]{1,0:T(8,128)(2,1)S(1)} %table.1.table_ref, bf16[144,256]{1,0:T(8,128)(2,1)S(1)} %get-tuple-element.13.rest_0_, ...), custom_call_target="tpu_custom_call" | custom-call | tf_op jit(solution)/shard_map/route/pallas_call | solution.py:459
  17.4 1.2 %collective-permute-start.3 = (bf16[144,256]{1,0:T(8,128)(2,1)S(1)}, bf16[144,256]{1,0:T(8,128)(2,1)S(1)}, u32[]{:S(2)}, u32[]{:S(2)}) collective-permute-start(bf16[144,256]{1,0:T(8,128)(2,1)S(1)} %get-tuple-element.18), channel_id=1, source_target_pairs={{0,4},{4,0},{8,12},{12,8},{1,5},{5,1},{9,13},{13,9},{2,6},{6,2},{1... | collective-permute-start | bytes 221192 | tf_op jit(solution)/shard_map/ppermute | solution.py:418
  18.5 1.7 %collective-permute-start.4 = (bf16[144,256]{1,0:T(8,128)(2,1)S(1)}, bf16[144,256]{1,0:T(8,128)(2,1)S(1)}, u32[]{:S(2)}, u32[]{:S(2)}) collective-permute-start(bf16[144,256]{1,0:T(8,128)(2,1)S(1)} %get-tuple-element.19), channel_id=1, source_target_pairs={{0,8},{4,12},{8,0},{12,4},{1,9},{5,13},{9,1},{13,5},{2,10},{6,14},... | collective-permute-start | bytes 221192 | tf_op jit(solution)/shard_map/ppermute | solution.py:418
  20.2 1.6 %collective-permute-start.5 = (bf16[144,256]{1,0:T(8,128)(2,1)S(1)}, bf16[144,256]{1,0:T(8,128)(2,1)S(1)}, u32[]{:S(2)}, u32[]{:S(2)}) collective-permute-start(bf16[144,256]{1,0:T(8,128)(2,1)S(1)} %get-tuple-element.20), channel_id=1, source_target_pairs={{0,12},{4,8},{8,4},{12,0},{1,13},{5,9},{9,5},{13,1},{2,14},{6,10},... | collective-permute-start | bytes 221192 | tf_op jit(solution)/shard_map/ppermute | solution.py:418
  21.8 0.0 collective-permute-done.3.refs_1_.rest_1_
  21.8 3.2 %collective-permute-done.4.refs_2_.rest_2_ = bf16[144,256]{1,0:T(8,128)(2,1)S(1)} collective-permute-done((bf16[144,256]{1,0:T(8,128)(2,1)S(1)}, bf16[144,256]{1,0:T(8,128)(2,1)S(1)}, u32[]{:S(2)}, u32[]{:S(2)}) %collective-permute-start.4) | collective-permute-done | bytes 73760 | tf_op jit(solution)/shard_map/ppermute | solution.py:418
  25.0 1.4 %collective-permute-done.5.refs_3_.rest_3_ = bf16[144,256]{1,0:T(8,128)(2,1)S(1)} collective-permute-done((bf16[144,256]{1,0:T(8,128)(2,1)S(1)}, bf16[144,256]{1,0:T(8,128)(2,1)S(1)}, u32[]{:S(2)}, u32[]{:S(2)}) %collective-permute-start.5) | collective-permute-done | bytes 73760 | tf_op jit(solution)/shard_map/ppermute | solution.py:418
  26.5 0.1 collective-permute-start.8
  26.6 1.6 %collective-permute-start.7 = (f32[8,640]{1,0:T(8,128)S(1)}, f32[8,640]{1,0:T(8,128)S(1)}, u32[]{:S(2)}, u32[]{:S(2)}) collective-permute-start(f32[8,640]{1,0:T(8,128)S(1)} %gather.1.rest_0_), channel_id=1, source_target_pairs={{0,2},{1,3},{2,0},{3,1},{4,6},{5,7},{6,4},{7,5},{8,10},{9,11},{10,... | collective-permute-start | bytes 61448 | tf_op jit(solution)/shard_map/ppermute | solution.py:418
  28.1 0.3 collective-permute-start.6
  28.4 0.8 %unpack.1 = bf16[8,8,2048]{2,1,0:T(8,128)(2,1)} custom-call(bf16[144,256]{1,0:T(8,128)(2,1)S(1)} %get-tuple-element.17.refs_0_.rest_0_, bf16[144,256]{1,0:T(8,128)(2,1)S(1)} %collective-permute-done.3.refs_1_.rest_1_, bf16[144,256]{1,0:T(8,128)(2,1)S(1)} %collective-permute-done.4.refs_2_.rest_2_, bf16[144,256]{1,0:T(8,128)(2,1)S(1)} %collective-permute-done.5.refs_3_.rest_3_), custom_call_target="tpu_custom_call" | custom-call | tf_op jit(solution)/shard_map/unpack/pallas_call | solution.py:491
  29.2 0.7 %collective-permute-done.8.rest_3_ = f32[8,640]{1,0:T(8,128)S(1)} collective-permute-done((f32[8,640]{1,0:T(8,128)S(1)}, f32[8,640]{1,0:T(8,128)S(1)}, u32[]{:S(2)}, u32[]{:S(2)}) %collective-permute-start.8) | collective-permute-done | bytes 20512 | tf_op jit(solution)/shard_map/ppermute | solution.py:418
  29.9 0.5 %collective-permute-done.7.rest_2_ = f32[8,640]{1,0:T(8,128)S(1)} collective-permute-done((f32[8,640]{1,0:T(8,128)S(1)}, f32[8,640]{1,0:T(8,128)S(1)}, u32[]{:S(2)}, u32[]{:S(2)}) %collective-permute-start.7) | collective-permute-done | bytes 20512 | tf_op jit(solution)/shard_map/ppermute | solution.py:418
  30.4 0.0 collective-permute-done.6.rest_1_
  30.4 1.8 %solve.1 = f32[3,8,8]{2,1,0:T(8,128)} custom-call(f32[4,8,128]{2,1,0:T(8,128)S(1)} %get-tuple-element.21.base_ref, f32[3,8,8]{2,1,0:T(8,128)S(1)} %get-tuple-element.22.params_ref, f32[8,640]{1,0:T(8,128)S(1)} %gather.1.rest_0_, f32[8,640]{1,0:T(8,128)S(1)} %collective-permute-done.6.rest_1_, f32[8,640]{1,0:T(8,128)S(1)} %collective-permute-done.7.rest_2_, ...), custom_call_target="tpu_custom_call" | custom-call | tf_op jit(solution)/shard_map/solve/pallas_call | solution.py:499
  (1 shorter events, 0.0 us)
Async XLA Ops:
  1.9 6.6 %collective-permute-start = (bf16[144,256]{1,0:T(8,128)(2,1)S(1)}, bf16[144,256]{1,0:T(8,128)(2,1)S(1)}, u32[]{:S(2)}, u32[]{:S(2)}) collective-permute-start(bf16[144,256]{1,0:T(8,128)(2,1)S(1)} %get-tuple-element.14), channel_id=1, source_target_pairs={{0,4},{4,0},{8,12},{12,8},{1,5},{5,1},{9,13},{13,9},{2,6},{6,2},{1... | collective-permute-start | bytes 221192 | tf_op jit(solution)/shard_map/ppermute | solution.py:418
  5.0 7.8 %collective-permute-start.1 = (bf16[144,256]{1,0:T(8,128)(2,1)S(1)}, bf16[144,256]{1,0:T(8,128)(2,1)S(1)}, u32[]{:S(2)}, u32[]{:S(2)}) collective-permute-start(bf16[144,256]{1,0:T(8,128)(2,1)S(1)} %get-tuple-element.15), channel_id=1, source_target_pairs={{0,8},{4,12},{8,0},{12,4},{1,9},{5,13},{9,1},{13,5},{2,10},{6,14},... | collective-permute-start | bytes 221192 | tf_op jit(solution)/shard_map/ppermute | solution.py:418
  7.6 6.3 %collective-permute-start.2 = (bf16[144,256]{1,0:T(8,128)(2,1)S(1)}, bf16[144,256]{1,0:T(8,128)(2,1)S(1)}, u32[]{:S(2)}, u32[]{:S(2)}) collective-permute-start(bf16[144,256]{1,0:T(8,128)(2,1)S(1)} %get-tuple-element.16), channel_id=1, source_target_pairs={{0,12},{4,8},{8,4},{12,0},{1,13},{5,9},{9,5},{13,1},{2,14},{6,10},... | collective-permute-start | bytes 221192 | tf_op jit(solution)/shard_map/ppermute | solution.py:418
  17.4 4.5 %collective-permute-start.3 = (bf16[144,256]{1,0:T(8,128)(2,1)S(1)}, bf16[144,256]{1,0:T(8,128)(2,1)S(1)}, u32[]{:S(2)}, u32[]{:S(2)}) collective-permute-start(bf16[144,256]{1,0:T(8,128)(2,1)S(1)} %get-tuple-element.18), channel_id=1, source_target_pairs={{0,4},{4,0},{8,12},{12,8},{1,5},{5,1},{9,13},{13,9},{2,6},{6,2},{1... | collective-permute-start | bytes 221192 | tf_op jit(solution)/shard_map/ppermute | solution.py:418
  18.5 6.5 %collective-permute-start.4 = (bf16[144,256]{1,0:T(8,128)(2,1)S(1)}, bf16[144,256]{1,0:T(8,128)(2,1)S(1)}, u32[]{:S(2)}, u32[]{:S(2)}) collective-permute-start(bf16[144,256]{1,0:T(8,128)(2,1)S(1)} %get-tuple-element.19), channel_id=1, source_target_pairs={{0,8},{4,12},{8,0},{12,4},{1,9},{5,13},{9,1},{13,5},{2,10},{6,14},... | collective-permute-start | bytes 221192 | tf_op jit(solution)/shard_map/ppermute | solution.py:418
  20.2 6.3 %collective-permute-start.5 = (bf16[144,256]{1,0:T(8,128)(2,1)S(1)}, bf16[144,256]{1,0:T(8,128)(2,1)S(1)}, u32[]{:S(2)}, u32[]{:S(2)}) collective-permute-start(bf16[144,256]{1,0:T(8,128)(2,1)S(1)} %get-tuple-element.20), channel_id=1, source_target_pairs={{0,12},{4,8},{8,4},{12,0},{1,13},{5,9},{9,5},{13,1},{2,14},{6,10},... | collective-permute-start | bytes 221192 | tf_op jit(solution)/shard_map/ppermute | solution.py:418
  26.5 3.4 %collective-permute-start.8 = (f32[8,640]{1,0:T(8,128)S(1)}, f32[8,640]{1,0:T(8,128)S(1)}, u32[]{:S(2)}, u32[]{:S(2)}) collective-permute-start(f32[8,640]{1,0:T(8,128)S(1)} %gather.1.rest_0_), channel_id=1, source_target_pairs={{0,3},{1,2},{2,1},{3,0},{4,7},{5,6},{6,5},{7,4},{8,11},{9,10},{10,... | collective-permute-start | bytes 61448 | tf_op jit(solution)/shard_map/ppermute | solution.py:418
  26.6 3.8 %collective-permute-start.7 = (f32[8,640]{1,0:T(8,128)S(1)}, f32[8,640]{1,0:T(8,128)S(1)}, u32[]{:S(2)}, u32[]{:S(2)}) collective-permute-start(f32[8,640]{1,0:T(8,128)S(1)} %gather.1.rest_0_), channel_id=1, source_target_pairs={{0,2},{1,3},{2,0},{3,1},{4,6},{5,7},{6,4},{7,5},{8,10},{9,11},{10,... | collective-permute-start | bytes 61448 | tf_op jit(solution)/shard_map/ppermute | solution.py:418
  28.1 2.3 %collective-permute-start.6 = (f32[8,640]{1,0:T(8,128)S(1)}, f32[8,640]{1,0:T(8,128)S(1)}, u32[]{:S(2)}, u32[]{:S(2)}) collective-permute-start(f32[8,640]{1,0:T(8,128)S(1)} %gather.1.rest_0_), channel_id=1, source_target_pairs={{0,1},{1,0},{2,3},{3,2},{4,5},{5,4},{6,7},{7,6},{8,9},{9,8},{10,11... | collective-permute-start | bytes 61448 | tf_op jit(solution)/shard_map/ppermute | solution.py:418

commit v4 on v3

--- a/solution.py
+++ b/solution.py
@@ -22,6 +22,13 @@
 
 
 AHEAD = 8
+
+
+ORDERS = {"basin": (3, 1, 2), "back": (3, 1, 2), "member": (1, 2, 3)}
+
+
+def partners(length, axis):
+    return [0] + list(ORDERS[axis])
 
 
 def kept(x):
@@ -124,7 +131,7 @@
         [upper_mid.astype(jnp.float32), lower_mid.astype(jnp.float32)], axis=0
     )
     extras = jnp.concatenate([tops, mids], axis=1).astype(jnp.bfloat16)
-    for k, out_ref in enumerate(out_refs):
+    for k, out_ref in zip(partners(len(out_refs), "basin"), out_refs):
         to = here ^ k
         for r in range(reach_count):
             for h in range(block_len // LANES):
@@ -163,7 +170,7 @@
     base = shape_count * members_dev
     at_lane = lax.broadcasted_iota(jnp.int32, (reach_count, LANES), 1)
     facts_ref[total:, :] = jnp.zeros((facts_ref.shape[0] - total, LANES), jnp.float32)
-    for k, in_ref in enumerate(in_refs):
+    for k, in_ref in zip(partners(len(in_refs), "basin"), in_refs):
         source = here ^ k
         extras = in_ref[reach_count * rows :, :].astype(jnp.float32)
         tops, mids = extras[:, :LANES], extras[:, LANES:]
@@ -174,7 +181,7 @@
         )
     copy = pltpu.make_async_copy(facts_ref, facts_smem, sem)
     copy.start()
-    for k, in_ref in enumerate(in_refs):
+    for k, in_ref in zip(partners(len(in_refs), "basin"), in_refs):
         source = here ^ k
         for r in range(reach_count):
             state_ref[source * reach_count + r] = in_ref[r * rows : (r + 1) * rows, :].astype(
@@ -280,7 +287,7 @@
     used = len(chunks) * share
     chunks.append(jnp.zeros((EXTRA - used, block_len), jnp.float32))
     extras = jnp.concatenate(chunks, axis=0).astype(jnp.bfloat16)
-    for k, out_ref in enumerate(out_refs):
+    for k, out_ref in zip(partners(len(out_refs), "back"), out_refs):
         to = here ^ k
         for r in range(reach_count):
             out_ref[r * rows : (r + 1) * rows, :] = flows_ref[to * reach_count + r]
@@ -297,7 +304,7 @@
     pieces = wide // block_len
     at_row = lax.broadcasted_iota(jnp.int32, (members_dev, block_len), 0)
     placed = [jnp.zeros((members_dev, block_len), jnp.float32)] * pieces
-    for k, in_ref in enumerate(in_refs):
+    for k, in_ref in zip(partners(len(in_refs), "back"), in_refs):
         extras = in_ref[in_ref.shape[0] - EXTRA :, :].astype(jnp.float32)
         for i in range(pieces):
             for j in range(share):
@@ -328,7 +335,7 @@
     block_count = out_ref.shape[2] // block_len
     rows = share * block_count
     here = lax.axis_index("basin")
-    for k, in_ref in enumerate(in_refs):
+    for k, in_ref in zip(partners(len(in_refs), "back"), in_refs):
         source = here ^ k
         for r in range(reach_count):
             piece = in_ref[r * rows : (r + 1) * rows, :].astype(jnp.float32)
@@ -361,7 +368,7 @@
     wide = all_ref.shape[1]
     here = lax.axis_index("member")
     tiles = None
-    for k, in_ref in enumerate(in_refs):
+    for k, in_ref in zip(partners(len(in_refs), "member"), in_refs):
         at = pl.multiple_of((here ^ k) * members_dev, members_dev)
         all_ref[pl.ds(at, members_dev), :] = in_ref[:, :wide]
         tile = in_ref[:, wide:]
@@ -416,6 +423,12 @@
 def exchanged(x, axis, by):
     length = lax.axis_size(axis)
     return lax.ppermute(x, axis, [(i, i ^ by) for i in range(length)])
+
+
+def swapped(pieces, axis, order):
+    return [pieces[0]] + [
+        exchanged(piece, axis, by) for piece, by in zip(pieces[1:], partners(len(pieces), order)[1:])
+    ]
 
 
 def per_device_split(
@@ -454,7 +467,7 @@
         ],
         name="pack",
     )(level_map, down_map, gauge_reach, gauge_sigma, runoff, route_params, observed, obs_noise)
-    arrived = [packed[0]] + [exchanged(packed[k], "basin", k) for k in range(1, parts)]
+    arrived = swapped(packed, "basin", "basin")
     conv_table = kernel_table(unit_shapes)
     *routed, noise_base = pl.pallas_call(
         functools.partial(
@@ -479,7 +492,7 @@
         ],
         name="route",
     )(kept(conv_table), *map(kept, arrived))
-    returned = [routed[0]] + [exchanged(routed[k], "basin", k) for k in range(1, parts)]
+    returned = swapped(routed, "basin", "back")
     local = pl.pallas_call(
         functools.partial(gather_body, wide=wide),
         out_shape=pltpu.VMEM((members_dev, wide + LANES), f32),
@@ -487,7 +500,7 @@
         out_specs=vmem(),
         name="gather",
     )(kept(tile), *map(kept, returned))
-    everyone = [local] + [exchanged(local, "member", k) for k in range(1, groups)]
+    everyone = swapped([local] * groups, "member", "member")
     flows = pl.pallas_call(
         functools.partial(unpack_body, parts=parts, reach_count=reach_count),
         out_shape=jax.ShapeDtypeStruct(runoff.shape, bf16),

time: 32.5 us -> 31.2 us (0.960)
  waiting for transfers between devices: 11.2 us -> 9.85 us
    ppermute x9, waiting for transfers between devices: 11.2 us -> 9.85 us  [exchanged(): return lax.ppermute(x, axis, [(i, i ^ by) for i in range(length)])]
  transfers between devices with their start and end apart: 9 -> 9, of which waited for: 6 -> 7; matrix products, arithmetic and copies ran while one was open for 0% -> 0% of each run, Pallas kernels for 5% -> 5%
where the time goes in v4:
time: 31.2 us; the launch traced here: 31 us
  starting transfers between devices  12.2 us (39%)
  waiting for transfers between devices  9.85 us (32%)
  Pallas kernels  8.29 us (27%)
  between operations  0.67 us (2%)
    ppermute x9, starting transfers between devices, exchanged(): return lax.ppermute(x, axis, [(i, i ^ by) for i in range(length)])  12.2 us
    ppermute x9, waiting for transfers between devices, exchanged(): return lax.ppermute(x, axis, [(i, i ^ by) for i in range(length)])  9.85 us
    pallas_call x1, Pallas kernels, per_device_split(): pl.pallas_call(functools.partial(route_body, parts=parts, reach_count=rea...  3.56 us
    pallas_call x1, Pallas kernels, per_device_split(): pl.pallas_call(solve_body, out_shape=jax.ShapeDtypeStruct(route_params.sh...  1.84 us
    pallas_call x1, Pallas kernels, per_device_split(): pl.pallas_call(pack_body, out_shape=[sent] * parts + [pltpu.VMEM(route_pa...  1.22 us
    pallas_call x1, Pallas kernels, kernel_table(): pl.pallas_call(table_body, out_shape=pltpu.VMEM((2 * block_len, shape_cou...  0.83 us
    pallas_call x1, Pallas kernels, per_device_split(): pl.pallas_call(functools.partial(unpack_body, parts=parts, reach_count=re...  0.82 us
  transfers between devices with their start and end apart: 9, of which 7 were waited for; matrix products, arithmetic and copies ran while one was open for 0% of the time, Pallas kernels for 5%

profile of v4, /device:TPU:0, one launch (start us, length us, event | category | flops | bytes accessed | tf_op | source)
XLA Modules:
  0.0 31.0 jit_solution(3983650292045471776)
XLA Ops:
  0.6 1.2 %pack.1 = (bf16[144,256]{1,0:T(8,128)(2,1)S(1)}, bf16[144,256]{1,0:T(8,128)(2,1)S(1)}, bf16[144,256]{1,0:T(8,128)(2,1)S(1)}, bf16[144,256]{1,0:T(8,128)(2,1)S(1)...) custom-call(s32[8]{0:T(128)} %level_ref.1, s32[8]{0:T(128)} %down_ref.1, s32[2]{0:T(128)} %gauge_ref.1, f32[2]{0:T(128)} %sigma_ref.1, ...), custom_call_target="tpu_custom_call" | custom-call | tf_op jit(solution)/shard_map/pack/pallas_call | solution.py:458
  1.9 5.1 %collective-permute-start = (bf16[144,256]{1,0:T(8,128)(2,1)S(1)}, bf16[144,256]{1,0:T(8,128)(2,1)S(1)}, u32[]{:S(2)}, u32[]{:S(2)}) collective-permute-start(bf16[144,256]{1,0:T(8,128)(2,1)S(1)} %get-tuple-element.14), channel_id=1, source_target_pairs={{0,12},{4,8},{8,4},{12,0},{1,13},{5,9},{9,5},{13,1},{2,14},{6,10},... | collective-permute-start | bytes 221192 | tf_op jit(solution)/shard_map/ppermute | solution.py:425
  7.0 0.0 collective-permute-start.1
  7.0 0.6 %collective-permute-start.2 = (bf16[144,256]{1,0:T(8,128)(2,1)S(1)}, bf16[144,256]{1,0:T(8,128)(2,1)S(1)}, u32[]{:S(2)}, u32[]{:S(2)}) collective-permute-start(bf16[144,256]{1,0:T(8,128)(2,1)S(1)} %get-tuple-element.16), channel_id=1, source_target_pairs={{0,8},{4,12},{8,0},{12,4},{1,9},{5,13},{9,1},{13,5},{2,10},{6,14},... | collective-permute-start | bytes 221192 | tf_op jit(solution)/shard_map/ppermute | solution.py:425
  7.6 0.8 %table.1.table_ref = bf16[512,768]{1,0:T(8,128)(2,1)S(1)} custom-call(f32[3,256]{1,0:T(4,128)} %shapes_ref.1), custom_call_target="tpu_custom_call" | custom-call | tf_op jit(solution)/shard_map/table/pallas_call | solution.py:53
  8.5 1.7 %collective-permute-done.rest_1_ = bf16[144,256]{1,0:T(8,128)(2,1)S(1)} collective-permute-done((bf16[144,256]{1,0:T(8,128)(2,1)S(1)}, bf16[144,256]{1,0:T(8,128)(2,1)S(1)}, u32[]{:S(2)}, u32[]{:S(2)}) %collective-permute-start) | collective-permute-done | bytes 73760 | tf_op jit(solution)/shard_map/ppermute | solution.py:425
  10.2 1.9 %collective-permute-done.1.rest_2_ = bf16[144,256]{1,0:T(8,128)(2,1)S(1)} collective-permute-done((bf16[144,256]{1,0:T(8,128)(2,1)S(1)}, bf16[144,256]{1,0:T(8,128)(2,1)S(1)}, u32[]{:S(2)}, u32[]{:S(2)}) %collective-permute-start.1) | collective-permute-done | bytes 73760 | tf_op jit(solution)/shard_map/ppermute | solution.py:425
  12.1 0.7 %collective-permute-done.2.rest_3_ = bf16[144,256]{1,0:T(8,128)(2,1)S(1)} collective-permute-done((bf16[144,256]{1,0:T(8,128)(2,1)S(1)}, bf16[144,256]{1,0:T(8,128)(2,1)S(1)}, u32[]{:S(2)}, u32[]{:S(2)}) %collective-permute-start.2) | collective-permute-done | bytes 73760 | tf_op jit(solution)/shard_map/ppermute | solution.py:425
  12.8 3.6 %route.1 = (bf16[144,256]{1,0:T(8,128)(2,1)S(1)}, bf16[144,256]{1,0:T(8,128)(2,1)S(1)}, bf16[144,256]{1,0:T(8,128)(2,1)S(1)}, bf16[144,256]{1,0:T(8,128)(2,1)S(1)}, f32[4,8,128]{2,1,0:T(8,128)S(1)}) custom-call(bf16[512,768]{1,0:T(8,128)(2,1)S(1)} %table.1.table_ref, bf16[144,256]{1,0:T(8,128)(2,1)S(1)} %get-tuple-element.13.rest_0_, ...), custom_call_target="tpu_custom_call" | custom-call | tf_op jit(solution)/shard_map/route/pallas_call | solution.py:472
  16.4 3.3 %collective-permute-start.3 = (bf16[144,256]{1,0:T(8,128)(2,1)S(1)}, bf16[144,256]{1,0:T(8,128)(2,1)S(1)}, u32[]{:S(2)}, u32[]{:S(2)}) collective-permute-start(bf16[144,256]{1,0:T(8,128)(2,1)S(1)} %get-tuple-element.18), channel_id=1, source_target_pairs={{0,12},{4,8},{8,4},{12,0},{1,13},{5,9},{9,5},{13,1},{2,14},{6,10},... | collective-permute-start | bytes 221192 | tf_op jit(solution)/shard_map/ppermute | solution.py:425
  19.6 0.0 collective-permute-start.4
  19.6 1.2 %collective-permute-start.5 = (bf16[144,256]{1,0:T(8,128)(2,1)S(1)}, bf16[144,256]{1,0:T(8,128)(2,1)S(1)}, u32[]{:S(2)}, u32[]{:S(2)}) collective-permute-start(bf16[144,256]{1,0:T(8,128)(2,1)S(1)} %get-tuple-element.20), channel_id=1, source_target_pairs={{0,8},{4,12},{8,0},{12,4},{1,9},{5,13},{9,1},{13,5},{2,10},{6,14},... | collective-permute-start | bytes 221192 | tf_op jit(solution)/shard_map/ppermute | solution.py:425
  20.8 1.9 %collective-permute-done.3.refs_1_.rest_1_ = bf16[144,256]{1,0:T(8,128)(2,1)S(1)} collective-permute-done((bf16[144,256]{1,0:T(8,128)(2,1)S(1)}, bf16[144,256]{1,0:T(8,128)(2,1)S(1)}, u32[]{:S(2)}, u32[]{:S(2)}) %collective-permute-start.3) | collective-permute-done | bytes 73760 | tf_op jit(solution)/shard_map/ppermute | solution.py:425
  22.7 2.5 %collective-permute-done.4.refs_2_.rest_2_ = bf16[144,256]{1,0:T(8,128)(2,1)S(1)} collective-permute-done((bf16[144,256]{1,0:T(8,128)(2,1)S(1)}, bf16[144,256]{1,0:T(8,128)(2,1)S(1)}, u32[]{:S(2)}, u32[]{:S(2)}) %collective-permute-start.4) | collective-permute-done | bytes 73760 | tf_op jit(solution)/shard_map/ppermute | solution.py:425
  25.2 0.0 collective-permute-done.5.refs_3_.rest_3_
  25.2 0.1 collective-permute-start.8
  25.3 1.6 %collective-permute-start.7 = (f32[8,640]{1,0:T(8,128)S(1)}, f32[8,640]{1,0:T(8,128)S(1)}, u32[]{:S(2)}, u32[]{:S(2)}) collective-permute-start(f32[8,640]{1,0:T(8,128)S(1)} %gather.1.rest_0_), channel_id=1, source_target_pairs={{0,2},{1,3},{2,0},{3,1},{4,6},{5,7},{6,4},{7,5},{8,10},{9,11},{10,... | collective-permute-start | bytes 61448 | tf_op jit(solution)/shard_map/ppermute | solution.py:425
  26.8 0.3 collective-permute-start.6
  27.1 0.8 %unpack.1 = bf16[8,8,2048]{2,1,0:T(8,128)(2,1)} custom-call(bf16[144,256]{1,0:T(8,128)(2,1)S(1)} %get-tuple-element.17.refs_0_.rest_0_, bf16[144,256]{1,0:T(8,128)(2,1)S(1)} %collective-permute-done.3.refs_1_.rest_1_, bf16[144,256]{1,0:T(8,128)(2,1)S(1)} %collective-permute-done.4.refs_2_.rest_2_, bf16[144,256]{1,0:T(8,128)(2,1)S(1)} %collective-permute-done.5.refs_3_.rest_3_), custom_call_target="tpu_custom_call" | custom-call | tf_op jit(solution)/shard_map/unpack/pallas_call | solution.py:504
  27.9 0.7 %collective-permute-done.8.rest_3_ = f32[8,640]{1,0:T(8,128)S(1)} collective-permute-done((f32[8,640]{1,0:T(8,128)S(1)}, f32[8,640]{1,0:T(8,128)S(1)}, u32[]{:S(2)}, u32[]{:S(2)}) %collective-permute-start.8) | collective-permute-done | bytes 20512 | tf_op jit(solution)/shard_map/ppermute | solution.py:425
  28.6 0.5 %collective-permute-done.7.rest_2_ = f32[8,640]{1,0:T(8,128)S(1)} collective-permute-done((f32[8,640]{1,0:T(8,128)S(1)}, f32[8,640]{1,0:T(8,128)S(1)}, u32[]{:S(2)}, u32[]{:S(2)}) %collective-permute-start.7) | collective-permute-done | bytes 20512 | tf_op jit(solution)/shard_map/ppermute | solution.py:425
  29.1 0.0 collective-permute-done.6.rest_1_
  29.1 1.8 %solve.1 = f32[3,8,8]{2,1,0:T(8,128)} custom-call(f32[4,8,128]{2,1,0:T(8,128)S(1)} %get-tuple-element.21.base_ref, f32[3,8,8]{2,1,0:T(8,128)S(1)} %get-tuple-element.22.params_ref, f32[8,640]{1,0:T(8,128)S(1)} %gather.1.rest_0_, f32[8,640]{1,0:T(8,128)S(1)} %collective-permute-done.6.rest_1_, f32[8,640]{1,0:T(8,128)S(1)} %collective-permute-done.7.rest_2_, ...), custom_call_target="tpu_custom_call" | custom-call | tf_op jit(solution)/shard_map/solve/pallas_call | solution.py:512
  (1 shorter events, 0.0 us)
Async XLA Ops:
  1.9 8.3 %collective-permute-start = (bf16[144,256]{1,0:T(8,128)(2,1)S(1)}, bf16[144,256]{1,0:T(8,128)(2,1)S(1)}, u32[]{:S(2)}, u32[]{:S(2)}) collective-permute-start(bf16[144,256]{1,0:T(8,128)(2,1)S(1)} %get-tuple-element.14), channel_id=1, source_target_pairs={{0,12},{4,8},{8,4},{12,0},{1,13},{5,9},{9,5},{13,1},{2,14},{6,10},... | collective-permute-start | bytes 221192 | tf_op jit(solution)/shard_map/ppermute | solution.py:425
  7.0 5.1 %collective-permute-start.1 = (bf16[144,256]{1,0:T(8,128)(2,1)S(1)}, bf16[144,256]{1,0:T(8,128)(2,1)S(1)}, u32[]{:S(2)}, u32[]{:S(2)}) collective-permute-start(bf16[144,256]{1,0:T(8,128)(2,1)S(1)} %get-tuple-element.15), channel_id=1, source_target_pairs={{0,4},{4,0},{8,12},{12,8},{1,5},{5,1},{9,13},{13,9},{2,6},{6,2},{1... | collective-permute-start | bytes 221192 | tf_op jit(solution)/shard_map/ppermute | solution.py:425
  7.0 5.8 %collective-permute-start.2 = (bf16[144,256]{1,0:T(8,128)(2,1)S(1)}, bf16[144,256]{1,0:T(8,128)(2,1)S(1)}, u32[]{:S(2)}, u32[]{:S(2)}) collective-permute-start(bf16[144,256]{1,0:T(8,128)(2,1)S(1)} %get-tuple-element.16), channel_id=1, source_target_pairs={{0,8},{4,12},{8,0},{12,4},{1,9},{5,13},{9,1},{13,5},{2,10},{6,14},... | collective-permute-start | bytes 221192 | tf_op jit(solution)/shard_map/ppermute | solution.py:425
  16.4 6.3 %collective-permute-start.3 = (bf16[144,256]{1,0:T(8,128)(2,1)S(1)}, bf16[144,256]{1,0:T(8,128)(2,1)S(1)}, u32[]{:S(2)}, u32[]{:S(2)}) collective-permute-start(bf16[144,256]{1,0:T(8,128)(2,1)S(1)} %get-tuple-element.18), channel_id=1, source_target_pairs={{0,12},{4,8},{8,4},{12,0},{1,13},{5,9},{9,5},{13,1},{2,14},{6,10},... | collective-permute-start | bytes 221192 | tf_op jit(solution)/shard_map/ppermute | solution.py:425
  19.6 5.5 %collective-permute-start.4 = (bf16[144,256]{1,0:T(8,128)(2,1)S(1)}, bf16[144,256]{1,0:T(8,128)(2,1)S(1)}, u32[]{:S(2)}, u32[]{:S(2)}) collective-permute-start(bf16[144,256]{1,0:T(8,128)(2,1)S(1)} %get-tuple-element.19), channel_id=1, source_target_pairs={{0,4},{4,0},{8,12},{12,8},{1,5},{5,1},{9,13},{13,9},{2,6},{6,2},{1... | collective-permute-start | bytes 221192 | tf_op jit(solution)/shard_map/ppermute | solution.py:425
  19.6 5.5 %collective-permute-start.5 = (bf16[144,256]{1,0:T(8,128)(2,1)S(1)}, bf16[144,256]{1,0:T(8,128)(2,1)S(1)}, u32[]{:S(2)}, u32[]{:S(2)}) collective-permute-start(bf16[144,256]{1,0:T(8,128)(2,1)S(1)} %get-tuple-element.20), channel_id=1, source_target_pairs={{0,8},{4,12},{8,0},{12,4},{1,9},{5,13},{9,1},{13,5},{2,10},{6,14},... | collective-permute-start | bytes 221192 | tf_op jit(solution)/shard_map/ppermute | solution.py:425
  25.2 3.4 %collective-permute-start.8 = (f32[8,640]{1,0:T(8,128)S(1)}, f32[8,640]{1,0:T(8,128)S(1)}, u32[]{:S(2)}, u32[]{:S(2)}) collective-permute-start(f32[8,640]{1,0:T(8,128)S(1)} %gather.1.rest_0_), channel_id=1, source_target_pairs={{0,3},{1,2},{2,1},{3,0},{4,7},{5,6},{6,5},{7,4},{8,11},{9,10},{10,... | collective-permute-start | bytes 61448 | tf_op jit(solution)/shard_map/ppermute | solution.py:425
  25.3 3.8 %collective-permute-start.7 = (f32[8,640]{1,0:T(8,128)S(1)}, f32[8,640]{1,0:T(8,128)S(1)}, u32[]{:S(2)}, u32[]{:S(2)}) collective-permute-start(f32[8,640]{1,0:T(8,128)S(1)} %gather.1.rest_0_), channel_id=1, source_target_pairs={{0,2},{1,3},{2,0},{3,1},{4,6},{5,7},{6,4},{7,5},{8,10},{9,11},{10,... | collective-permute-start | bytes 61448 | tf_op jit(solution)/shard_map/ppermute | solution.py:425
  26.8 2.3 %collective-permute-start.6 = (f32[8,640]{1,0:T(8,128)S(1)}, f32[8,640]{1,0:T(8,128)S(1)}, u32[]{:S(2)}, u32[]{:S(2)}) collective-permute-start(f32[8,640]{1,0:T(8,128)S(1)} %gather.1.rest_0_), channel_id=1, source_target_pairs={{0,1},{1,0},{2,3},{3,2},{4,5},{5,4},{6,7},{7,6},{8,9},{9,8},{10,11... | collective-permute-start | bytes 61448 | tf_op jit(solution)/shard_map/ppermute | solution.py:425

commit v5 on v4

--- a/solution.py
+++ b/solution.py
@@ -21,7 +21,8 @@
     return pl.BlockSpec(memory_space=pltpu.SMEM)
 
 
-AHEAD = 8
+AHEAD = 16
+CODE = 64
 
 
 ORDERS = {"basin": (3, 1, 2), "back": (3, 1, 2), "member": (1, 2, 3)}
@@ -35,7 +36,7 @@
     return pltpu.with_memory_space_constraint(x, pltpu.VMEM)
 
 
-def table_body(shapes_ref, table_ref):
+def table_body(shapes_ref, table_ref, window_ref, *, span):
     shape_count, block_len = shapes_ref.shape
     for s in range(shape_count):
         lags = shapes_ref[s : s + 1, :] * (1.0 / block_len)
@@ -46,15 +47,23 @@
         cols = slice(s * block_len, (s + 1) * block_len)
         table_ref[:block_len, cols] = skewed[:, :block_len]
         table_ref[block_len:, cols] = skewed[:, block_len:]
-
-
-def kernel_table(unit_shapes):
+    lag_at = lax.broadcasted_iota(jnp.int32, window_ref.shape, 0)
+    col_at = lax.broadcasted_iota(jnp.int32, window_ref.shape, 1)
+    window_ref[...] = jnp.where(
+        lag_at // span == col_at % (block_len // span), 1.0 / span, 0.0
+    ).astype(jnp.bfloat16)
+
+
+def kernel_table(unit_shapes, span, wide):
     shape_count, block_len = unit_shapes.shape
     return pl.pallas_call(
-        table_body,
-        out_shape=pltpu.VMEM((2 * block_len, shape_count * block_len), jnp.bfloat16),
+        functools.partial(table_body, span=span),
+        out_shape=[
+            pltpu.VMEM((2 * block_len, shape_count * block_len), jnp.bfloat16),
+            pltpu.VMEM((block_len, wide), jnp.bfloat16),
+        ],
         in_specs=[vmem()],
-        out_specs=vmem(),
+        out_specs=[vmem()] * 2,
         name="table",
     )(unit_shapes)
 
@@ -106,20 +115,20 @@
     base = shape_count * members_dev
     facts = extra_ref[lower, :]
     cap = reach_count // 4
-    facts = jnp.where(at_lane // cap == base // cap, jnp.float32(reach_count), facts)
+    facts = jnp.where(
+        (at_lane >= base) & (at_lane < base + cap), jnp.float32(reach_count * CODE), facts
+    )
     for r in range(reach_count):
         rank = jnp.int32(0)
         for q in range(r):
             rank = rank + (level_ref[q] == level_ref[r]).astype(jnp.int32)
         here_slot = (at_row == level_ref[r]) & (at_lane == base + rank)
-        facts = jnp.where(here_slot, jnp.float32(r), facts)
-        goal_slot = (at_row == level_ref[r]) & (at_lane == base + cap + rank)
-        facts = jnp.where(goal_slot, down_ref[r].astype(jnp.float32), facts)
+        facts = jnp.where(here_slot, (down_ref[r] + r * CODE).astype(jnp.float32), facts)
     for g in range(gauge_count):
         facts = jnp.where(
-            (at_row == g) & (at_lane == base + 2 * cap), gauge_ref[g].astype(jnp.float32), facts
+            (at_row == g) & (at_lane == base + cap), gauge_ref[g].astype(jnp.float32), facts
         )
-        facts = jnp.where((at_row == g) & (at_lane == base + 2 * cap + 1), sigma_ref[g], facts)
+        facts = jnp.where((at_row == g) & (at_lane == base + cap + 1), sigma_ref[g], facts)
     upper_top, upper_mid, _ = split_two(extra_ref[:members_dev, :])
     lower_top, lower_mid, lower_low = split_two(facts)
     half = LANES // 2
@@ -155,10 +164,10 @@
     place_params(params_ref, tile_ref)
 
 
-def route_body(table_ref, *rest, parts, reach_count, shape_count, gauge_count, members_dev):
+def route_body(table_ref, window_ref, *rest, parts, reach_count, shape_count, gauge_count, members_dev):
     in_refs, rest = rest[:parts], rest[parts:]
     out_refs, rest = rest[:parts], rest[parts:]
-    base_ref, state_ref, flows_ref, left_ref, facts_ref, facts_smem, sem = rest
+    base_ref, state_ref, flows_ref, left_ref, weight_ref, code_ref = rest
     block_len = table_ref.shape[0] // 2
     rows = state_ref.shape[1]
     share = members_dev // parts
@@ -168,19 +177,31 @@
     here = lax.axis_index("basin")
     half = LANES // 2
     base = shape_count * members_dev
+    span = LANES // parts
     at_lane = lax.broadcasted_iota(jnp.int32, (reach_count, LANES), 1)
-    facts_ref[total:, :] = jnp.zeros((facts_ref.shape[0] - total, LANES), jnp.float32)
+    facts = jnp.zeros((reach_count, LANES), jnp.float32)
     for k, in_ref in zip(partners(len(in_refs), "basin"), in_refs):
         source = here ^ k
         extras = in_ref[reach_count * rows :, :].astype(jnp.float32)
         tops, mids = extras[:, :LANES], extras[:, LANES:]
         base_ref[source] = tops[:members_dev] + mids[:members_dev]
         low = pltpu.roll(tops[members_dev:], half, 1)
-        facts_ref[pl.ds(pl.multiple_of(source * reach_count, reach_count), reach_count), :] = jnp.where(
-            at_lane < half, tops[members_dev:] + (mids[members_dev:] + low), 0.0
-        )
-    copy = pltpu.make_async_copy(facts_ref, facts_smem, sem)
-    copy.start()
+        part = jnp.where(at_lane < span, tops[members_dev:] + (mids[members_dev:] + low), 0.0)
+        facts = facts + pltpu.roll(part, source * span, 1)
+    whole = facts.astype(jnp.int32)
+    for level_now in range(LEVELS):
+        for c in range(parts * cap):
+            code_ref[level_now * parts * cap + c] = whole[
+                level_now, (c // cap) * span + base + c % cap
+            ]
+    mine = pltpu.roll(facts, LANES - share * here, 1)
+    for n in range(parts):
+        for s in range(shape_count):
+            for j in range(share):
+                lane = n * span + s * members_dev + j
+                weight_ref[s * share + j, n * reach_count : (n + 1) * reach_count, :] = (
+                    jnp.broadcast_to(mine[:, lane : lane + 1], (reach_count, LANES))
+                )
     for k, in_ref in zip(partners(len(in_refs), "basin"), in_refs):
         source = here ^ k
         for r in range(reach_count):
@@ -189,20 +210,19 @@
             )
     state_ref[total] = jnp.zeros(state_ref.shape[1:], jnp.float32)
     state_ref[total + 1] = jnp.zeros(state_ref.shape[1:], jnp.float32)
-    copy.wait()
 
     first_row = lax.broadcasted_iota(jnp.int32, (block_count, block_len), 0) == 0
     slots = parts * cap
 
     def one_level(level_now, carry):
-        picked, goals = [], []
+        picked, goals, sources = [], [], []
         for c in range(slots):
-            at = (c // cap) * reach_count + level_now
-            lane = base + c % cap
-            reach = facts_smem[at, lane].astype(jnp.int32)
-            goal = (c // cap) * reach_count + facts_smem[at, lane + cap].astype(jnp.int32)
+            code = code_ref[level_now * slots + c]
+            reach = code // CODE
+            goal = (c // cap) * reach_count + code % CODE
             real = reach < reach_count
             kept_goal = (goal < (c // cap + 2) * reach_count) & (goal < total) & real
+            sources.append((c // cap) * reach_count + jnp.where(real, reach, 0))
             picked.append(jnp.where(real, (c // cap) * reach_count + reach, total))
             goals.append(jnp.where(kept_goal, goal, total + 1))
         for c in range(slots):
@@ -234,7 +254,8 @@
                 at = slice(c * rows + j * block_count, c * rows + (j + 1) * block_count)
                 piece = None
                 for s in range(shape_count):
-                    weight = facts_smem[picked[c], s * members_dev + share * here + j]
+                    weight = weight_ref[s * share + j, pl.ds(sources[c], 1), :]
+                    weight = jnp.concatenate([weight] * (block_len // LANES), axis=1)
                     term = mixed[s][at] * weight
                     piece = term if piece is None else piece + term
                 pieces.append(piece)
@@ -246,27 +267,21 @@
     lax.fori_loop(0, LEVELS, one_level, 0)
 
     gauges = parts * gauge_count
-    span = block_count * block_len // WINDOWS
     wide = gauges * WINDOWS
     per_block = WINDOWS // block_count
-    lag_at = lax.broadcasted_iota(jnp.int32, (block_len, wide), 0)
-    col_at = lax.broadcasted_iota(jnp.int32, (block_len, wide), 1)
-    windowing = jnp.where(lag_at // span == col_at % per_block, 1.0 / span, 0.0).astype(
-        jnp.bfloat16
-    )
     for g in range(gauges):
-        reach = (g // gauge_count) * reach_count + facts_smem[
-            (g // gauge_count) * reach_count + g % gauge_count, base + 2 * cap
-        ].astype(jnp.int32)
+        reach = (g // gauge_count) * reach_count + whole[
+            g % gauge_count, (g // gauge_count) * span + base + cap
+        ]
         left_ref[g * rows : (g + 1) * rows, :block_len] = flows_ref[reach]
     means = jnp.dot(
-        left_ref[: gauges * rows, :block_len], windowing, preferred_element_type=jnp.float32
+        left_ref[: gauges * rows, :block_len], window_ref[...], preferred_element_type=jnp.float32
     )
     row_at = lax.broadcasted_iota(jnp.int32, (block_count, wide), 0)
     col_at = lax.broadcasted_iota(jnp.int32, (block_count, wide), 1)
     sigma_row = jnp.zeros((1, wide), jnp.float32)
     for g in range(gauges):
-        sigma = facts_smem[(g // gauge_count) * reach_count + g % gauge_count, base + 2 * cap + 1]
+        sigma = facts[g % gauge_count, (g // gauge_count) * span + base + cap + 1]
         sigma_row = jnp.where(col_at[:1] // WINDOWS == g, sigma, sigma_row)
     scaled = []
     for j in range(share):
@@ -468,7 +483,7 @@
         name="pack",
     )(level_map, down_map, gauge_reach, gauge_sigma, runoff, route_params, observed, obs_noise)
     arrived = swapped(packed, "basin", "basin")
-    conv_table = kernel_table(unit_shapes)
+    conv_table, window_table = kernel_table(unit_shapes, series_len // WINDOWS, wide)
     *routed, noise_base = pl.pallas_call(
         functools.partial(
             route_body,
@@ -480,18 +495,17 @@
         ),
         out_shape=[sent] * parts
         + [pltpu.VMEM((parts, members_dev, gauge_count * WINDOWS), f32)],
-        in_specs=[vmem()] * (1 + parts),
+        in_specs=[vmem()] * (2 + parts),
         out_specs=[vmem()] * (parts + 1),
         scratch_shapes=[
             pltpu.VMEM((total + 2, rows, block_len), f32),
             pltpu.VMEM((total + 1, rows, block_len), bf16),
             pltpu.VMEM((parts * max(cap, gauge_count) * rows, 2 * block_len), bf16),
-            pltpu.VMEM((total + 8, LANES), f32),
-            pltpu.SMEM((total + 8, LANES), f32),
-            pltpu.SemaphoreType.DMA,
+            pltpu.VMEM((shape_count * share, total, LANES), f32),
+            pltpu.SMEM((LEVELS * parts * cap,), jnp.int32),
         ],
         name="route",
-    )(kept(conv_table), *map(kept, arrived))
+    )(kept(conv_table), kept(window_table), *map(kept, arrived))
     returned = swapped(routed, "basin", "back")
     local = pl.pallas_call(
         functools.partial(gather_body, wide=wide),
@@ -545,7 +559,9 @@
         and gauge_count * WINDOWS == LANES
         and wide % block_len == 0
         and 3 * share * (wide // block_len) <= EXTRA
-        and (shape_count * members_dev + 8) * 2 <= LANES
+        and shape_count * members_dev + reach_count // 4 + 2 <= LANES // parts
+        and 2 * reach_count < CODE
+        and parts >= 2
         and reach_count == LEVELS
         and shape_count * groups * members_dev <= LANES
         and groups * members_dev + members_dev <= LANES
@@ -600,7 +616,7 @@
     observed,
     obs_noise,
 ):
-    conv_table = kernel_table(unit_shapes)
+    conv_table, _ = kernel_table(unit_shapes, runoff.shape[2] // WINDOWS, LANES)
     reach_count, members_dev, series_len = runoff.shape
     flat_len = members_dev * series_len
     slot_count = reach_count // 4

time: 31.2 us -> 30.4 us (0.974)
  Pallas kernels: 8.29 us -> 7.53 us
    pallas_call x1, Pallas kernels: 3.56 us -> 2.96 us  [per_device_split(): pl.pallas_call(functools.partial(route_body, parts=parts, reach_count=rea...]
where the time goes in v5:
time: 30.4 us; the launch traced here: 30.2 us
  starting transfers between devices  12.2 us (40%)
  waiting for transfers between devices  9.85 us (32%)
  Pallas kernels  7.53 us (25%)
  between operations  0.67 us (2%)
    ppermute x9, starting transfers between devices, exchanged(): return lax.ppermute(x, axis, [(i, i ^ by) for i in range(length)])  12.2 us
    ppermute x9, waiting for transfers between devices, exchanged(): return lax.ppermute(x, axis, [(i, i ^ by) for i in range(length)])  9.85 us
    pallas_call x1, Pallas kernels, per_device_split(): pl.pallas_call(functools.partial(route_body, parts=parts, reach_count=rea...  2.96 us
    pallas_call x1, Pallas kernels, per_device_split(): pl.pallas_call(solve_body, out_shape=jax.ShapeDtypeStruct(route_params.sh...  1.69 us
    pallas_call x1, Pallas kernels, per_device_split(): pl.pallas_call(pack_body, out_shape=[sent] * parts + [pltpu.VMEM(route_pa...  1.22 us
    pallas_call x1, Pallas kernels, kernel_table(): pl.pallas_call(functools.partial(table_body, span=span), out_shape=[pltpu...  0.83 us
    pallas_call x1, Pallas kernels, per_device_split(): pl.pallas_call(functools.partial(unpack_body, parts=parts, reach_count=re...  0.82 us
  transfers between devices with their start and end apart: 9, of which 7 were waited for; matrix products, arithmetic and copies ran while one was open for 0% of the time, Pallas kernels for 5%

profile of v5, /device:TPU:0, one launch (start us, length us, event | category | flops | bytes accessed | tf_op | source)
XLA Modules:
  0.0 30.2 jit_solution(7098034988020172001)
XLA Ops:
  0.6 1.2 %pack.1 = (bf16[144,256]{1,0:T(8,128)(2,1)S(1)}, bf16[144,256]{1,0:T(8,128)(2,1)S(1)}, bf16[144,256]{1,0:T(8,128)(2,1)S(1)}, bf16[144,256]{1,0:T(8,128)(2,1)S(1)...) custom-call(s32[8]{0:T(128)} %level_ref.1, s32[8]{0:T(128)} %down_ref.1, s32[2]{0:T(128)} %gauge_ref.1, f32[2]{0:T(128)} %sigma_ref.1, ...), custom_call_target="tpu_custom_call" | custom-call | tf_op jit(solution)/shard_map/pack/pallas_call | solution.py:473
  1.9 5.1 %collective-permute-start = (bf16[144,256]{1,0:T(8,128)(2,1)S(1)}, bf16[144,256]{1,0:T(8,128)(2,1)S(1)}, u32[]{:S(2)}, u32[]{:S(2)}) collective-permute-start(bf16[144,256]{1,0:T(8,128)(2,1)S(1)} %get-tuple-element.18), channel_id=1, source_target_pairs={{0,12},{4,8},{8,4},{12,0},{1,13},{5,9},{9,5},{13,1},{2,14},{6,10},... | collective-permute-start | bytes 221192 | tf_op jit(solution)/shard_map/ppermute | solution.py:440
  7.0 0.0 collective-permute-start.1
  7.0 0.6 %collective-permute-start.2 = (bf16[144,256]{1,0:T(8,128)(2,1)S(1)}, bf16[144,256]{1,0:T(8,128)(2,1)S(1)}, u32[]{:S(2)}, u32[]{:S(2)}) collective-permute-start(bf16[144,256]{1,0:T(8,128)(2,1)S(1)} %get-tuple-element.20), channel_id=1, source_target_pairs={{0,8},{4,12},{8,0},{12,4},{1,9},{5,13},{9,1},{13,5},{2,10},{6,14},... | collective-permute-start | bytes 221192 | tf_op jit(solution)/shard_map/ppermute | solution.py:440
  7.6 0.8 %table.1 = (bf16[512,768]{1,0:T(8,128)(2,1)S(1)}, bf16[256,512]{1,0:T(8,128)(2,1)S(1)}) custom-call(f32[3,256]{1,0:T(4,128)} %shapes_ref.1), custom_call_target="tpu_custom_call" | custom-call | tf_op jit(solution)/shard_map/table/pallas_call | solution.py:59
  8.5 1.7 %collective-permute-done.rest_1_ = bf16[144,256]{1,0:T(8,128)(2,1)S(1)} collective-permute-done((bf16[144,256]{1,0:T(8,128)(2,1)S(1)}, bf16[144,256]{1,0:T(8,128)(2,1)S(1)}, u32[]{:S(2)}, u32[]{:S(2)}) %collective-permute-start) | collective-permute-done | bytes 73760 | tf_op jit(solution)/shard_map/ppermute | solution.py:440
  10.2 1.9 %collective-permute-done.1.rest_2_ = bf16[144,256]{1,0:T(8,128)(2,1)S(1)} collective-permute-done((bf16[144,256]{1,0:T(8,128)(2,1)S(1)}, bf16[144,256]{1,0:T(8,128)(2,1)S(1)}, u32[]{:S(2)}, u32[]{:S(2)}) %collective-permute-start.1) | collective-permute-done | bytes 73760 | tf_op jit(solution)/shard_map/ppermute | solution.py:440
  12.1 0.7 %collective-permute-done.2.rest_3_ = bf16[144,256]{1,0:T(8,128)(2,1)S(1)} collective-permute-done((bf16[144,256]{1,0:T(8,128)(2,1)S(1)}, bf16[144,256]{1,0:T(8,128)(2,1)S(1)}, u32[]{:S(2)}, u32[]{:S(2)}) %collective-permute-start.2) | collective-permute-done | bytes 73760 | tf_op jit(solution)/shard_map/ppermute | solution.py:440
  12.8 3.0 %route.1 = (bf16[144,256]{1,0:T(8,128)(2,1)S(1)}, bf16[144,256]{1,0:T(8,128)(2,1)S(1)}, bf16[144,256]{1,0:T(8,128)(2,1)S(1)}, bf16[144,256]{1,0:T(8,128)(2,1)S(1)}, f32[4,8,128]{2,1,0:T(8,128)S(1)}) custom-call(bf16[512,768]{1,0:T(8,128)(2,1)S(1)} %get-tuple-element.15.table_ref, bf16[256,512]{1,0:T(8,128)(2,1)S(1)} %get-tuple-element.16.window_ref, ...), custom_call_target="tpu_custom_call" | custom-call | tf_op jit(solution)/shard_map/route/pallas_call | solution.py:487
  15.8 3.3 %collective-permute-start.3 = (bf16[144,256]{1,0:T(8,128)(2,1)S(1)}, bf16[144,256]{1,0:T(8,128)(2,1)S(1)}, u32[]{:S(2)}, u32[]{:S(2)}) collective-permute-start(bf16[144,256]{1,0:T(8,128)(2,1)S(1)} %get-tuple-element.22), channel_id=1, source_target_pairs={{0,12},{4,8},{8,4},{12,0},{1,13},{5,9},{9,5},{13,1},{2,14},{6,10},... | collective-permute-start | bytes 221192 | tf_op jit(solution)/shard_map/ppermute | solution.py:440
  19.0 0.0 collective-permute-start.4
  19.0 1.2 %collective-permute-start.5 = (bf16[144,256]{1,0:T(8,128)(2,1)S(1)}, bf16[144,256]{1,0:T(8,128)(2,1)S(1)}, u32[]{:S(2)}, u32[]{:S(2)}) collective-permute-start(bf16[144,256]{1,0:T(8,128)(2,1)S(1)} %get-tuple-element.24), channel_id=1, source_target_pairs={{0,8},{4,12},{8,0},{12,4},{1,9},{5,13},{9,1},{13,5},{2,10},{6,14},... | collective-permute-start | bytes 221192 | tf_op jit(solution)/shard_map/ppermute | solution.py:440
  20.2 1.9 %collective-permute-done.3.refs_1_.rest_1_ = bf16[144,256]{1,0:T(8,128)(2,1)S(1)} collective-permute-done((bf16[144,256]{1,0:T(8,128)(2,1)S(1)}, bf16[144,256]{1,0:T(8,128)(2,1)S(1)}, u32[]{:S(2)}, u32[]{:S(2)}) %collective-permute-start.3) | collective-permute-done | bytes 73760 | tf_op jit(solution)/shard_map/ppermute | solution.py:440
  22.1 2.5 %collective-permute-done.4.refs_2_.rest_2_ = bf16[144,256]{1,0:T(8,128)(2,1)S(1)} collective-permute-done((bf16[144,256]{1,0:T(8,128)(2,1)S(1)}, bf16[144,256]{1,0:T(8,128)(2,1)S(1)}, u32[]{:S(2)}, u32[]{:S(2)}) %collective-permute-start.4) | collective-permute-done | bytes 73760 | tf_op jit(solution)/shard_map/ppermute | solution.py:440
  24.6 0.0 collective-permute-done.5.refs_3_.rest_3_
  24.6 0.1 collective-permute-start.8
  24.7 1.6 %collective-permute-start.7 = (f32[8,640]{1,0:T(8,128)S(1)}, f32[8,640]{1,0:T(8,128)S(1)}, u32[]{:S(2)}, u32[]{:S(2)}) collective-permute-start(f32[8,640]{1,0:T(8,128)S(1)} %gather.1.rest_0_), channel_id=1, source_target_pairs={{0,2},{1,3},{2,0},{3,1},{4,6},{5,7},{6,4},{7,5},{8,10},{9,11},{10,... | collective-permute-start | bytes 61448 | tf_op jit(solution)/shard_map/ppermute | solution.py:440
  26.2 0.3 collective-permute-start.6
  26.5 0.8 %unpack.1 = bf16[8,8,2048]{2,1,0:T(8,128)(2,1)} custom-call(bf16[144,256]{1,0:T(8,128)(2,1)S(1)} %get-tuple-element.21.refs_0_.rest_0_, bf16[144,256]{1,0:T(8,128)(2,1)S(1)} %collective-permute-done.3.refs_1_.rest_1_, bf16[144,256]{1,0:T(8,128)(2,1)S(1)} %collective-permute-done.4.refs_2_.rest_2_, bf16[144,256]{1,0:T(8,128)(2,1)S(1)} %collective-permute-done.5.refs_3_.rest_3_), custom_call_target="tpu_custom_call" | custom-call | tf_op jit(solution)/shard_map/unpack/pallas_call | solution.py:518
  27.3 0.7 %collective-permute-done.8.rest_3_ = f32[8,640]{1,0:T(8,128)S(1)} collective-permute-done((f32[8,640]{1,0:T(8,128)S(1)}, f32[8,640]{1,0:T(8,128)S(1)}, u32[]{:S(2)}, u32[]{:S(2)}) %collective-permute-start.8) | collective-permute-done | bytes 20512 | tf_op jit(solution)/shard_map/ppermute | solution.py:440
  28.0 0.5 %collective-permute-done.7.rest_2_ = f32[8,640]{1,0:T(8,128)S(1)} collective-permute-done((f32[8,640]{1,0:T(8,128)S(1)}, f32[8,640]{1,0:T(8,128)S(1)}, u32[]{:S(2)}, u32[]{:S(2)}) %collective-permute-start.7) | collective-permute-done | bytes 20512 | tf_op jit(solution)/shard_map/ppermute | solution.py:440
  28.5 0.0 collective-permute-done.6.rest_1_
  28.5 1.7 %solve.1 = f32[3,8,8]{2,1,0:T(8,128)} custom-call(f32[4,8,128]{2,1,0:T(8,128)S(1)} %get-tuple-element.25.base_ref, f32[3,8,8]{2,1,0:T(8,128)S(1)} %get-tuple-element.26.params_ref, f32[8,640]{1,0:T(8,128)S(1)} %gather.1.rest_0_, f32[8,640]{1,0:T(8,128)S(1)} %collective-permute-done.6.rest_1_, f32[8,640]{1,0:T(8,128)S(1)} %collective-permute-done.7.rest_2_, ...), custom_call_target="tpu_custom_call" | custom-call | tf_op jit(solution)/shard_map/solve/pallas_call | solution.py:526
  (1 shorter events, 0.0 us)
Async XLA Ops:
  1.9 8.3 %collective-permute-start = (bf16[144,256]{1,0:T(8,128)(2,1)S(1)}, bf16[144,256]{1,0:T(8,128)(2,1)S(1)}, u32[]{:S(2)}, u32[]{:S(2)}) collective-permute-start(bf16[144,256]{1,0:T(8,128)(2,1)S(1)} %get-tuple-element.18), channel_id=1, source_target_pairs={{0,12},{4,8},{8,4},{12,0},{1,13},{5,9},{9,5},{13,1},{2,14},{6,10},... | collective-permute-start | bytes 221192 | tf_op jit(solution)/shard_map/ppermute | solution.py:440
  7.0 5.1 %collective-permute-start.1 = (bf16[144,256]{1,0:T(8,128)(2,1)S(1)}, bf16[144,256]{1,0:T(8,128)(2,1)S(1)}, u32[]{:S(2)}, u32[]{:S(2)}) collective-permute-start(bf16[144,256]{1,0:T(8,128)(2,1)S(1)} %get-tuple-element.19), channel_id=1, source_target_pairs={{0,4},{4,0},{8,12},{12,8},{1,5},{5,1},{9,13},{13,9},{2,6},{6,2},{1... | collective-permute-start | bytes 221192 | tf_op jit(solution)/shard_map/ppermute | solution.py:440
  7.0 5.8 %collective-permute-start.2 = (bf16[144,256]{1,0:T(8,128)(2,1)S(1)}, bf16[144,256]{1,0:T(8,128)(2,1)S(1)}, u32[]{:S(2)}, u32[]{:S(2)}) collective-permute-start(bf16[144,256]{1,0:T(8,128)(2,1)S(1)} %get-tuple-element.20), channel_id=1, source_target_pairs={{0,8},{4,12},{8,0},{12,4},{1,9},{5,13},{9,1},{13,5},{2,10},{6,14},... | collective-permute-start | bytes 221192 | tf_op jit(solution)/shard_map/ppermute | solution.py:440
  15.8 6.3 %collective-permute-start.3 = (bf16[144,256]{1,0:T(8,128)(2,1)S(1)}, bf16[144,256]{1,0:T(8,128)(2,1)S(1)}, u32[]{:S(2)}, u32[]{:S(2)}) collective-permute-start(bf16[144,256]{1,0:T(8,128)(2,1)S(1)} %get-tuple-element.22), channel_id=1, source_target_pairs={{0,12},{4,8},{8,4},{12,0},{1,13},{5,9},{9,5},{13,1},{2,14},{6,10},... | collective-permute-start | bytes 221192 | tf_op jit(solution)/shard_map/ppermute | solution.py:440
  19.0 5.5 %collective-permute-start.4 = (bf16[144,256]{1,0:T(8,128)(2,1)S(1)}, bf16[144,256]{1,0:T(8,128)(2,1)S(1)}, u32[]{:S(2)}, u32[]{:S(2)}) collective-permute-start(bf16[144,256]{1,0:T(8,128)(2,1)S(1)} %get-tuple-element.23), channel_id=1, source_target_pairs={{0,4},{4,0},{8,12},{12,8},{1,5},{5,1},{9,13},{13,9},{2,6},{6,2},{1... | collective-permute-start | bytes 221192 | tf_op jit(solution)/shard_map/ppermute | solution.py:440
  19.0 5.5 %collective-permute-start.5 = (bf16[144,256]{1,0:T(8,128)(2,1)S(1)}, bf16[144,256]{1,0:T(8,128)(2,1)S(1)}, u32[]{:S(2)}, u32[]{:S(2)}) collective-permute-start(bf16[144,256]{1,0:T(8,128)(2,1)S(1)} %get-tuple-element.24), channel_id=1, source_target_pairs={{0,8},{4,12},{8,0},{12,4},{1,9},{5,13},{9,1},{13,5},{2,10},{6,14},... | collective-permute-start | bytes 221192 | tf_op jit(solution)/shard_map/ppermute | solution.py:440
  24.6 3.4 %collective-permute-start.8 = (f32[8,640]{1,0:T(8,128)S(1)}, f32[8,640]{1,0:T(8,128)S(1)}, u32[]{:S(2)}, u32[]{:S(2)}) collective-permute-start(f32[8,640]{1,0:T(8,128)S(1)} %gather.1.rest_0_), channel_id=1, source_target_pairs={{0,3},{1,2},{2,1},{3,0},{4,7},{5,6},{6,5},{7,4},{8,11},{9,10},{10,... | collective-permute-start | bytes 61448 | tf_op jit(solution)/shard_map/ppermute | solution.py:440
  24.7 3.8 %collective-permute-start.7 = (f32[8,640]{1,0:T(8,128)S(1)}, f32[8,640]{1,0:T(8,128)S(1)}, u32[]{:S(2)}, u32[]{:S(2)}) collective-permute-start(f32[8,640]{1,0:T(8,128)S(1)} %gather.1.rest_0_), channel_id=1, source_target_pairs={{0,2},{1,3},{2,0},{3,1},{4,6},{5,7},{6,4},{7,5},{8,10},{9,11},{10,... | collective-permute-start | bytes 61448 | tf_op jit(solution)/shard_map/ppermute | solution.py:440
  26.2 2.3 %collective-permute-start.6 = (f32[8,640]{1,0:T(8,128)S(1)}, f32[8,640]{1,0:T(8,128)S(1)}, u32[]{:S(2)}, u32[]{:S(2)}) collective-permute-start(f32[8,640]{1,0:T(8,128)S(1)} %gather.1.rest_0_), channel_id=1, source_target_pairs={{0,1},{1,0},{2,3},{3,2},{4,5},{5,4},{6,7},{7,6},{8,9},{9,8},{10,11... | collective-permute-start | bytes 61448 | tf_op jit(solution)/shard_map/ppermute | solution.py:440

commit v6 on v5

--- a/solution.py
+++ b/solution.py
@@ -25,11 +25,19 @@
 CODE = 64
 
 
-ORDERS = {"basin": (3, 1, 2), "back": (3, 1, 2), "member": (1, 2, 3)}
-
-
-def partners(length, axis):
-    return [0] + list(ORDERS[axis])
+ORDERS = {
+    "basin": ((3, 1, 2), (3, 1, 2)),
+    "back": ((3, 1, 2), (2, 3, 1)),
+    "member": ((1, 2, 3), (1, 2, 3)),
+}
+
+
+def partners(length, step):
+    even, odd = ORDERS[step]
+    if even == odd:
+        return [0] + list(even)
+    side = lax.axis_index("member") % 2
+    return [0] + [jnp.where(side == 0, a, b) for a, b in zip(even, odd)]
 
 
 def kept(x):
@@ -435,15 +443,21 @@
         out_ref[s] = params_ref[s] + step[s * reach_count : (s + 1) * reach_count]
 
 
-def exchanged(x, axis, by):
-    length = lax.axis_size(axis)
-    return lax.ppermute(x, axis, [(i, i ^ by) for i in range(length)])
-
-
-def swapped(pieces, axis, order):
-    return [pieces[0]] + [
-        exchanged(piece, axis, by) for piece, by in zip(pieces[1:], partners(len(pieces), order)[1:])
-    ]
+def swapped(pieces, axis, step):
+    results = [pieces[0]]
+    groups = lax.axis_size("member")
+    for piece, *by in zip(pieces[1:], *ORDERS[step]):
+        if axis == "member":
+            pairs = [(m, m ^ by[m % 2]) for m in range(groups)]
+            results.append(lax.ppermute(piece, axis, pairs))
+        else:
+            pairs = [
+                (b * groups + m, (b ^ by[m % 2]) * groups + m)
+                for b in range(lax.axis_size(axis))
+                for m in range(groups)
+            ]
+            results.append(lax.ppermute(piece, (axis, "member"), pairs))
+    return results
 
 
 def per_device_split(
@@ -534,10 +548,6 @@
     return flows, updated
 
 
-def power_of_two(x):
-    return x & (x - 1) == 0
-
-
 def per_device(*args):
     runoff, route_params, unit_shapes, _, _, _, _, observed, _ = args
     parts, groups = lax.axis_size("basin"), lax.axis_size("member")
@@ -548,8 +558,8 @@
     wide = parts * gauge_count * WINDOWS
     share = max(members_dev // parts, 1)
     fits = (
-        power_of_two(parts)
-        and power_of_two(groups)
+        parts == 4
+        and groups == 4
         and members_dev == share * parts
         and reach_count == 8
         and members_dev == 8

time: 30.4 us -> 30.1 us (level)
  transfers between devices with their start and end apart: 9 -> 9, of which waited for: 7 -> 8; matrix products, arithmetic and copies ran while one was open for 0% -> 0% of each run, Pallas kernels for 5% -> 6%
where the time goes in v6:
time: 30.1 us; the launch traced here: 29.9 us
  starting transfers between devices  12.2 us (41%)
  waiting for transfers between devices  9.58 us (32%)
  Pallas kernels  7.52 us (25%)
  between operations  0.67 us (2%)
    ppermute x6, starting transfers between devices, swapped(): results.append(lax.ppermute(piece, (axis, 'member'), pairs))  10.2 us
    ppermute x6, waiting for transfers between devices, swapped(): results.append(lax.ppermute(piece, (axis, 'member'), pairs))  8.4 us
    pallas_call x1, Pallas kernels, per_device_split(): pl.pallas_call(functools.partial(route_body, parts=parts, reach_count=rea...  2.95 us
    ppermute x3, starting transfers between devices, swapped(): results.append(lax.ppermute(piece, axis, pairs))  1.92 us
    pallas_call x1, Pallas kernels, per_device_split(): pl.pallas_call(solve_body, out_shape=jax.ShapeDtypeStruct(route_params.sh...  1.69 us
    pallas_call x1, Pallas kernels, per_device_split(): pl.pallas_call(pack_body, out_shape=[sent] * parts + [pltpu.VMEM(route_pa...  1.22 us
    ppermute x3, waiting for transfers between devices, swapped(): results.append(lax.ppermute(piece, axis, pairs))  1.18 us
    pallas_call x1, Pallas kernels, kernel_table(): pl.pallas_call(functools.partial(table_body, span=span), out_shape=[pltpu...  0.83 us
  transfers between devices with their start and end apart: 9, of which 8 were waited for; matrix products, arithmetic and copies ran while one was open for 0% of the time, Pallas kernels for 6%

profile of v6, /device:TPU:0, one launch (start us, length us, event | category | flops | bytes accessed | tf_op | source)
XLA Modules:
  0.0 29.9 jit_solution(14748588104407170930)
XLA Ops:
  0.6 1.2 %pack.1 = (bf16[144,256]{1,0:T(8,128)(2,1)S(1)}, bf16[144,256]{1,0:T(8,128)(2,1)S(1)}, bf16[144,256]{1,0:T(8,128)(2,1)S(1)}, bf16[144,256]{1,0:T(8,128)(2,1)S(1)...) custom-call(s32[8]{0:T(128)} %level_ref.1, s32[8]{0:T(128)} %down_ref.1, s32[2]{0:T(128)} %gauge_ref.1, f32[2]{0:T(128)} %sigma_ref.1, ...), custom_call_target="tpu_custom_call" | custom-call | tf_op jit(solution)/shard_map/pack/pallas_call | solution.py:487
  1.9 5.1 %collective-permute-start = (bf16[144,256]{1,0:T(8,128)(2,1)S(1)}, bf16[144,256]{1,0:T(8,128)(2,1)S(1)}, u32[]{:S(2)}, u32[]{:S(2)}) collective-permute-start(bf16[144,256]{1,0:T(8,128)(2,1)S(1)} %get-tuple-element.18), channel_id=1, source_target_pairs={{0,12},{1,13},{2,14},{3,15},{4,8},{5,9},{6,10},{7,11},{8,4},{9,5},... | collective-permute-start | bytes 221192 | tf_op jit(solution)/shard_map/ppermute | solution.py:459
  7.0 0.0 collective-permute-start.1
  7.0 0.6 %collective-permute-start.2 = (bf16[144,256]{1,0:T(8,128)(2,1)S(1)}, bf16[144,256]{1,0:T(8,128)(2,1)S(1)}, u32[]{:S(2)}, u32[]{:S(2)}) collective-permute-start(bf16[144,256]{1,0:T(8,128)(2,1)S(1)} %get-tuple-element.20), channel_id=1, source_target_pairs={{0,8},{1,9},{2,10},{3,11},{4,12},{5,13},{6,14},{7,15},{8,0},{9,1},... | collective-permute-start | bytes 221192 | tf_op jit(solution)/shard_map/ppermute | solution.py:459
  7.6 0.8 %table.1 = (bf16[512,768]{1,0:T(8,128)(2,1)S(1)}, bf16[256,512]{1,0:T(8,128)(2,1)S(1)}) custom-call(f32[3,256]{1,0:T(4,128)} %shapes_ref.1), custom_call_target="tpu_custom_call" | custom-call | tf_op jit(solution)/shard_map/table/pallas_call | solution.py:67
  8.5 1.7 %collective-permute-done.rest_1_ = bf16[144,256]{1,0:T(8,128)(2,1)S(1)} collective-permute-done((bf16[144,256]{1,0:T(8,128)(2,1)S(1)}, bf16[144,256]{1,0:T(8,128)(2,1)S(1)}, u32[]{:S(2)}, u32[]{:S(2)}) %collective-permute-start) | collective-permute-done | bytes 73760 | tf_op jit(solution)/shard_map/ppermute | solution.py:459
  10.2 1.9 %collective-permute-done.1.rest_2_ = bf16[144,256]{1,0:T(8,128)(2,1)S(1)} collective-permute-done((bf16[144,256]{1,0:T(8,128)(2,1)S(1)}, bf16[144,256]{1,0:T(8,128)(2,1)S(1)}, u32[]{:S(2)}, u32[]{:S(2)}) %collective-permute-start.1) | collective-permute-done | bytes 73760 | tf_op jit(solution)/shard_map/ppermute | solution.py:459
  12.1 0.7 %collective-permute-done.2.rest_3_ = bf16[144,256]{1,0:T(8,128)(2,1)S(1)} collective-permute-done((bf16[144,256]{1,0:T(8,128)(2,1)S(1)}, bf16[144,256]{1,0:T(8,128)(2,1)S(1)}, u32[]{:S(2)}, u32[]{:S(2)}) %collective-permute-start.2) | collective-permute-done | bytes 73760 | tf_op jit(solution)/shard_map/ppermute | solution.py:459
  12.8 3.0 %route.1 = (bf16[144,256]{1,0:T(8,128)(2,1)S(1)}, bf16[144,256]{1,0:T(8,128)(2,1)S(1)}, bf16[144,256]{1,0:T(8,128)(2,1)S(1)}, bf16[144,256]{1,0:T(8,128)(2,1)S(1)}, f32[4,8,128]{2,1,0:T(8,128)S(1)}) custom-call(bf16[512,768]{1,0:T(8,128)(2,1)S(1)} %get-tuple-element.15.table_ref, bf16[256,512]{1,0:T(8,128)(2,1)S(1)} %get-tuple-element.16.window_ref, ...), custom_call_target="tpu_custom_call" | custom-call | tf_op jit(solution)/shard_map/route/pallas_call | solution.py:501
  15.8 3.3 %collective-permute-start.3 = (bf16[144,256]{1,0:T(8,128)(2,1)S(1)}, bf16[144,256]{1,0:T(8,128)(2,1)S(1)}, u32[]{:S(2)}, u32[]{:S(2)}) collective-permute-start(bf16[144,256]{1,0:T(8,128)(2,1)S(1)} %get-tuple-element.22), channel_id=1, source_target_pairs={{0,12},{1,9},{2,14},{3,11},{4,8},{5,13},{6,10},{7,15},{8,4},{9,1},... | collective-permute-start | bytes 221192 | tf_op jit(solution)/shard_map/ppermute | solution.py:459
  19.0 0.0 collective-permute-start.4
  19.0 1.2 %collective-permute-start.5 = (bf16[144,256]{1,0:T(8,128)(2,1)S(1)}, bf16[144,256]{1,0:T(8,128)(2,1)S(1)}, u32[]{:S(2)}, u32[]{:S(2)}) collective-permute-start(bf16[144,256]{1,0:T(8,128)(2,1)S(1)} %get-tuple-element.24), channel_id=1, source_target_pairs={{0,8},{1,5},{2,10},{3,7},{4,12},{5,1},{6,14},{7,3},{8,0},{9,13},{1... | collective-permute-start | bytes 221192 | tf_op jit(solution)/shard_map/ppermute | solution.py:459
  20.2 2.6 %collective-permute-done.3.refs_1_.rest_1_ = bf16[144,256]{1,0:T(8,128)(2,1)S(1)} collective-permute-done((bf16[144,256]{1,0:T(8,128)(2,1)S(1)}, bf16[144,256]{1,0:T(8,128)(2,1)S(1)}, u32[]{:S(2)}, u32[]{:S(2)}) %collective-permute-start.3) | collective-permute-done | bytes 73760 | tf_op jit(solution)/shard_map/ppermute | solution.py:459
  22.8 0.7 %collective-permute-done.4.refs_2_.rest_2_ = bf16[144,256]{1,0:T(8,128)(2,1)S(1)} collective-permute-done((bf16[144,256]{1,0:T(8,128)(2,1)S(1)}, bf16[144,256]{1,0:T(8,128)(2,1)S(1)}, u32[]{:S(2)}, u32[]{:S(2)}) %collective-permute-start.4) | collective-permute-done | bytes 73760 | tf_op jit(solution)/shard_map/ppermute | solution.py:459
  23.5 0.8 %collective-permute-done.5.refs_3_.rest_3_ = bf16[144,256]{1,0:T(8,128)(2,1)S(1)} collective-permute-done((bf16[144,256]{1,0:T(8,128)(2,1)S(1)}, bf16[144,256]{1,0:T(8,128)(2,1)S(1)}, u32[]{:S(2)}, u32[]{:S(2)}) %collective-permute-start.5) | collective-permute-done | bytes 73760 | tf_op jit(solution)/shard_map/ppermute | solution.py:459
  24.3 0.1 collective-permute-start.8
  24.4 1.6 %collective-permute-start.7 = (f32[8,640]{1,0:T(8,128)S(1)}, f32[8,640]{1,0:T(8,128)S(1)}, u32[]{:S(2)}, u32[]{:S(2)}) collective-permute-start(f32[8,640]{1,0:T(8,128)S(1)} %gather.1.rest_0_), channel_id=1, source_target_pairs={{0,2},{1,3},{2,0},{3,1},{4,6},{5,7},{6,4},{7,5},{8,10},{9,11},{10,... | collective-permute-start | bytes 61448 | tf_op jit(solution)/shard_map/ppermute | solution.py:452
  26.0 0.2 collective-permute-start.6
  26.2 0.8 %unpack.1 = bf16[8,8,2048]{2,1,0:T(8,128)(2,1)} custom-call(bf16[144,256]{1,0:T(8,128)(2,1)S(1)} %get-tuple-element.21.refs_0_.rest_0_, bf16[144,256]{1,0:T(8,128)(2,1)S(1)} %collective-permute-done.3.refs_1_.rest_1_, bf16[144,256]{1,0:T(8,128)(2,1)S(1)} %collective-permute-done.4.refs_2_.rest_2_, bf16[144,256]{1,0:T(8,128)(2,1)S(1)} %collective-permute-done.5.refs_3_.rest_3_), custom_call_target="tpu_custom_call" | custom-call | tf_op jit(solution)/shard_map/unpack/pallas_call | solution.py:532
  27.1 0.7 %collective-permute-done.8.rest_3_ = f32[8,640]{1,0:T(8,128)S(1)} collective-permute-done((f32[8,640]{1,0:T(8,128)S(1)}, f32[8,640]{1,0:T(8,128)S(1)}, u32[]{:S(2)}, u32[]{:S(2)}) %collective-permute-start.8) | collective-permute-done | bytes 20512 | tf_op jit(solution)/shard_map/ppermute | solution.py:452
  27.7 0.5 %collective-permute-done.7.rest_2_ = f32[8,640]{1,0:T(8,128)S(1)} collective-permute-done((f32[8,640]{1,0:T(8,128)S(1)}, f32[8,640]{1,0:T(8,128)S(1)}, u32[]{:S(2)}, u32[]{:S(2)}) %collective-permute-start.7) | collective-permute-done | bytes 20512 | tf_op jit(solution)/shard_map/ppermute | solution.py:452
  28.2 0.0 collective-permute-done.6.rest_1_
  28.2 1.7 %solve.1 = f32[3,8,8]{2,1,0:T(8,128)} custom-call(f32[4,8,128]{2,1,0:T(8,128)S(1)} %get-tuple-element.25.base_ref, f32[3,8,8]{2,1,0:T(8,128)S(1)} %get-tuple-element.26.params_ref, f32[8,640]{1,0:T(8,128)S(1)} %gather.1.rest_0_, f32[8,640]{1,0:T(8,128)S(1)} %collective-permute-done.6.rest_1_, f32[8,640]{1,0:T(8,128)S(1)} %collective-permute-done.7.rest_2_, ...), custom_call_target="tpu_custom_call" | custom-call | tf_op jit(solution)/shard_map/solve/pallas_call | solution.py:540
  (1 shorter events, 0.0 us)
Async XLA Ops:
  1.9 8.3 %collective-permute-start = (bf16[144,256]{1,0:T(8,128)(2,1)S(1)}, bf16[144,256]{1,0:T(8,128)(2,1)S(1)}, u32[]{:S(2)}, u32[]{:S(2)}) collective-permute-start(bf16[144,256]{1,0:T(8,128)(2,1)S(1)} %get-tuple-element.18), channel_id=1, source_target_pairs={{0,12},{1,13},{2,14},{3,15},{4,8},{5,9},{6,10},{7,11},{8,4},{9,5},... | collective-permute-start | bytes 221192 | tf_op jit(solution)/shard_map/ppermute | solution.py:459
  7.0 5.1 %collective-permute-start.1 = (bf16[144,256]{1,0:T(8,128)(2,1)S(1)}, bf16[144,256]{1,0:T(8,128)(2,1)S(1)}, u32[]{:S(2)}, u32[]{:S(2)}) collective-permute-start(bf16[144,256]{1,0:T(8,128)(2,1)S(1)} %get-tuple-element.19), channel_id=1, source_target_pairs={{0,4},{1,5},{2,6},{3,7},{4,0},{5,1},{6,2},{7,3},{8,12},{9,13},{10,... | collective-permute-start | bytes 221192 | tf_op jit(solution)/shard_map/ppermute | solution.py:459
  7.0 5.8 %collective-permute-start.2 = (bf16[144,256]{1,0:T(8,128)(2,1)S(1)}, bf16[144,256]{1,0:T(8,128)(2,1)S(1)}, u32[]{:S(2)}, u32[]{:S(2)}) collective-permute-start(bf16[144,256]{1,0:T(8,128)(2,1)S(1)} %get-tuple-element.20), channel_id=1, source_target_pairs={{0,8},{1,9},{2,10},{3,11},{4,12},{5,13},{6,14},{7,15},{8,0},{9,1},... | collective-permute-start | bytes 221192 | tf_op jit(solution)/shard_map/ppermute | solution.py:459
  15.8 7.1 %collective-permute-start.3 = (bf16[144,256]{1,0:T(8,128)(2,1)S(1)}, bf16[144,256]{1,0:T(8,128)(2,1)S(1)}, u32[]{:S(2)}, u32[]{:S(2)}) collective-permute-start(bf16[144,256]{1,0:T(8,128)(2,1)S(1)} %get-tuple-element.22), channel_id=1, source_target_pairs={{0,12},{1,9},{2,14},{3,11},{4,8},{5,13},{6,10},{7,15},{8,4},{9,1},... | collective-permute-start | bytes 221192 | tf_op jit(solution)/shard_map/ppermute | solution.py:459
  19.0 4.5 %collective-permute-start.4 = (bf16[144,256]{1,0:T(8,128)(2,1)S(1)}, bf16[144,256]{1,0:T(8,128)(2,1)S(1)}, u32[]{:S(2)}, u32[]{:S(2)}) collective-permute-start(bf16[144,256]{1,0:T(8,128)(2,1)S(1)} %get-tuple-element.23), channel_id=1, source_target_pairs={{0,4},{1,13},{2,6},{3,15},{4,0},{5,9},{6,2},{7,11},{8,12},{9,5},{1... | collective-permute-start | bytes 221192 | tf_op jit(solution)/shard_map/ppermute | solution.py:459
  19.0 5.3 %collective-permute-start.5 = (bf16[144,256]{1,0:T(8,128)(2,1)S(1)}, bf16[144,256]{1,0:T(8,128)(2,1)S(1)}, u32[]{:S(2)}, u32[]{:S(2)}) collective-permute-start(bf16[144,256]{1,0:T(8,128)(2,1)S(1)} %get-tuple-element.24), channel_id=1, source_target_pairs={{0,8},{1,5},{2,10},{3,7},{4,12},{5,1},{6,14},{7,3},{8,0},{9,13},{1... | collective-permute-start | bytes 221192 | tf_op jit(solution)/shard_map/ppermute | solution.py:459
  24.3 3.4 %collective-permute-start.8 = (f32[8,640]{1,0:T(8,128)S(1)}, f32[8,640]{1,0:T(8,128)S(1)}, u32[]{:S(2)}, u32[]{:S(2)}) collective-permute-start(f32[8,640]{1,0:T(8,128)S(1)} %gather.1.rest_0_), channel_id=1, source_target_pairs={{0,3},{1,2},{2,1},{3,0},{4,7},{5,6},{6,5},{7,4},{8,11},{9,10},{10,... | collective-permute-start | bytes 61448 | tf_op jit(solution)/shard_map/ppermute | solution.py:452
  24.4 3.8 %collective-permute-start.7 = (f32[8,640]{1,0:T(8,128)S(1)}, f32[8,640]{1,0:T(8,128)S(1)}, u32[]{:S(2)}, u32[]{:S(2)}) collective-permute-start(f32[8,640]{1,0:T(8,128)S(1)} %gather.1.rest_0_), channel_id=1, source_target_pairs={{0,2},{1,3},{2,0},{3,1},{4,6},{5,7},{6,4},{7,5},{8,10},{9,11},{10,... | collective-permute-start | bytes 61448 | tf_op jit(solution)/shard_map/ppermute | solution.py:452
  26.0 2.2 %collective-permute-start.6 = (f32[8,640]{1,0:T(8,128)S(1)}, f32[8,640]{1,0:T(8,128)S(1)}, u32[]{:S(2)}, u32[]{:S(2)}) collective-permute-start(f32[8,640]{1,0:T(8,128)S(1)} %gather.1.rest_0_), channel_id=1, source_target_pairs={{0,1},{1,0},{2,3},{3,2},{4,5},{5,4},{6,7},{7,6},{8,9},{9,8},{10,11... | collective-permute-start | bytes 61448 | tf_op jit(solution)/shard_map/ppermute | solution.py:452

commit v7 on v6

--- a/solution.py
+++ b/solution.py
@@ -94,7 +94,7 @@
     noise_ref,
     *rest,
 ):
-    out_refs, (own_ref, tile_ref, stage_ref, extra_ref) = rest[:-4], rest[-4:]
+    out_refs, (own_ref, tile_ref, base_ref, stage_ref, extra_ref) = rest[:-5], rest[-5:]
     reach_count, members_dev, series_len = runoff_ref.shape
     shape_count = params_ref.shape[0]
     gauge_count, windows = observed_ref.shape
@@ -112,16 +112,15 @@
                 stage_ref[h, at : at + members_dev, :] = series[:, lane : lane + LANES]
     extra_ref[...] = jnp.zeros(extra_ref.shape, jnp.float32)
     for g in range(gauge_count):
-        extra_ref[:members_dev, g * windows : (g + 1) * windows] = (
+        base_ref[:, g * windows : (g + 1) * windows] = (
             observed_ref[g : g + 1, :] / sigma_ref[g] + noise_ref[g]
         )
-    lower = slice(members_dev, members_dev + reach_count)
     for s in range(shape_count):
-        extra_ref[lower, s * members_dev : (s + 1) * members_dev] = params_ref[s]
+        extra_ref[:, s * members_dev : (s + 1) * members_dev] = params_ref[s]
     at_row = lax.broadcasted_iota(jnp.int32, (reach_count, LANES), 0)
     at_lane = lax.broadcasted_iota(jnp.int32, (reach_count, LANES), 1)
     base = shape_count * members_dev
-    facts = extra_ref[lower, :]
+    facts = extra_ref[...]
     cap = reach_count // 4
     facts = jnp.where(
         (at_lane >= base) & (at_lane < base + cap), jnp.float32(reach_count * CODE), facts
@@ -137,17 +136,14 @@
             (at_row == g) & (at_lane == base + cap), gauge_ref[g].astype(jnp.float32), facts
         )
         facts = jnp.where((at_row == g) & (at_lane == base + cap + 1), sigma_ref[g], facts)
-    upper_top, upper_mid, _ = split_two(extra_ref[:members_dev, :])
-    lower_top, lower_mid, lower_low = split_two(facts)
-    half = LANES // 2
-    lower_top = jnp.where(
-        at_lane < half, lower_top.astype(jnp.float32), pltpu.roll(lower_low, half, 1)
-    )
-    tops = jnp.concatenate([upper_top.astype(jnp.float32), lower_top], axis=0)
-    mids = jnp.concatenate(
-        [upper_mid.astype(jnp.float32), lower_mid.astype(jnp.float32)], axis=0
-    )
-    extras = jnp.concatenate([tops, mids], axis=1).astype(jnp.bfloat16)
+    span = LANES // len(out_refs)
+    top, mid, low = split_two(facts)
+    terms = (
+        top.astype(jnp.float32)
+        + pltpu.roll(mid.astype(jnp.float32), span, 1)
+        + pltpu.roll(low, 2 * span, 1)
+    )
+    extras = jnp.concatenate([terms, base_ref[...]], axis=1).astype(jnp.bfloat16)
     for k, out_ref in zip(partners(len(out_refs), "basin"), out_refs):
         to = here ^ k
         for r in range(reach_count):
@@ -172,7 +168,9 @@
     place_params(params_ref, tile_ref)
 
 
-def route_body(table_ref, window_ref, *rest, parts, reach_count, shape_count, gauge_count, members_dev):
+def route_body(
+    table_ref, window_ref, own_base_ref, *rest, parts, reach_count, shape_count, gauge_count, members_dev
+):
     in_refs, rest = rest[:parts], rest[parts:]
     out_refs, rest = rest[:parts], rest[parts:]
     base_ref, state_ref, flows_ref, left_ref, weight_ref, code_ref = rest
@@ -183,7 +181,6 @@
     total = parts * reach_count
     cap = reach_count // 4
     here = lax.axis_index("basin")
-    half = LANES // 2
     base = shape_count * members_dev
     span = LANES // parts
     at_lane = lax.broadcasted_iota(jnp.int32, (reach_count, LANES), 1)
@@ -191,10 +188,10 @@
     for k, in_ref in zip(partners(len(in_refs), "basin"), in_refs):
         source = here ^ k
         extras = in_ref[reach_count * rows :, :].astype(jnp.float32)
-        tops, mids = extras[:, :LANES], extras[:, LANES:]
-        base_ref[source] = tops[:members_dev] + mids[:members_dev]
-        low = pltpu.roll(tops[members_dev:], half, 1)
-        part = jnp.where(at_lane < span, tops[members_dev:] + (mids[members_dev:] + low), 0.0)
+        terms = extras[:, :LANES]
+        base_ref[source] = extras[:, LANES:]
+        rest_terms = pltpu.roll(terms, LANES - span, 1) + pltpu.roll(terms, LANES - 2 * span, 1)
+        part = jnp.where(at_lane < span, terms + rest_terms, 0.0)
         facts = facts + pltpu.roll(part, source * span, 1)
     whole = facts.astype(jnp.int32)
     for level_now in range(LEVELS):
@@ -304,11 +301,15 @@
         scaled.append(jnp.sum(merged, axis=0, keepdims=True) / sigma_row)
     scaled = jnp.concatenate(scaled, axis=0)
     top, mid, low = split_two(scaled)
-    chunks = []
+    _, base_mid, _ = split_two(own_base_ref[...])
+    base_mid = base_mid.astype(jnp.float32)
+    middle = members_dev // 2
+    chunks = [jnp.concatenate([base_mid[:middle], base_mid[middle:]], axis=1)]
     for part in (top.astype(jnp.float32), mid.astype(jnp.float32), low):
         chunks += [part[:, i * block_len : (i + 1) * block_len] for i in range(wide // block_len)]
-    used = len(chunks) * share
-    chunks.append(jnp.zeros((EXTRA - used, block_len), jnp.float32))
+    used = middle + (len(chunks) - 1) * share
+    if used < EXTRA:
+        chunks.append(jnp.zeros((EXTRA - used, block_len), jnp.float32))
     extras = jnp.concatenate(chunks, axis=0).astype(jnp.bfloat16)
     for k, out_ref in zip(partners(len(out_refs), "back"), out_refs):
         to = here ^ k
@@ -317,8 +318,8 @@
         out_ref[reach_count * rows :, :] = extras
 
 
-def gather_body(tile_ref, *rest, wide):
-    in_refs, out_ref = rest[:-1], rest[-1]
+def gather_body(tile_ref, top_ref, *rest, wide):
+    in_refs, (out_ref, base_ref) = rest[:-2], rest[-2:]
     parts = len(in_refs)
     members_dev = out_ref.shape[0]
     share = members_dev // parts
@@ -329,6 +330,11 @@
     placed = [jnp.zeros((members_dev, block_len), jnp.float32)] * pieces
     for k, in_ref in zip(partners(len(in_refs), "back"), in_refs):
         extras = in_ref[in_ref.shape[0] - EXTRA :, :].astype(jnp.float32)
+        middle = members_dev // 2
+        base_ref[here ^ k] = top_ref[here ^ k] + jnp.concatenate(
+            [extras[:middle, :LANES], extras[:middle, LANES:]], axis=0
+        )
+        extras = extras[middle:]
         for i in range(pieces):
             for j in range(share):
                 value = sum(
@@ -417,20 +423,30 @@
     row_at = lax.broadcasted_iota(jnp.int32, system.shape, 0)
     col_at = lax.broadcasted_iota(jnp.int32, system.shape, 1)
     system = system + jnp.where(row_at == col_at, 1.0, 0.0)
+    tiles_down = range(0, members, members_dev)
+    system = [system[g : g + members_dev] for g in tiles_down]
+    tile_row = row_at[:members_dev]
     for first in range(0, members, AHEAD):
         cols = [
-            jnp.broadcast_to(system[:, i : i + 1], system.shape)
+            [jnp.broadcast_to(tile[:, i : i + 1], tile.shape) for tile in system]
             for i in range(first, first + AHEAD)
         ]
         for t in range(AHEAD):
-            i = first + t
-            own_row = row_at == i
-            inverse = 1.0 / cols[t][i : i + 1, :]
-            pivot_row = system[i : i + 1, :] * inverse
-            system = jnp.where(own_row, pivot_row, system - cols[t] * pivot_row)
+            here_tile, here_row = divmod(first + t, members_dev)
+            factors = cols[t]
+            inverse = 1.0 / factors[here_tile][here_row : here_row + 1, :]
+            own_row = tile_row == here_row
+
+            def cleared(tiles):
+                pivot_row = tiles[here_tile][here_row : here_row + 1, :] * inverse
+                done = [tile - factor * pivot_row for tile, factor in zip(tiles, factors)]
+                done[here_tile] = jnp.where(own_row, pivot_row, done[here_tile])
+                return done
+
+            system = cleared(system)
             for u in range(t + 1, AHEAD):
-                pivot_row = cols[u][i : i + 1, :] * inverse
-                cols[u] = jnp.where(own_row, pivot_row, cols[u] - cols[t] * pivot_row)
+                cols[u] = cleared(cols[u])
+    system = jnp.concatenate(system, axis=0)
     gain = system[:, members : members + members_dev]
     theta = jnp.concatenate(
         [tiles[:, s * members : (s + 1) * members] for s in range(shape_count)], axis=0
@@ -483,22 +499,24 @@
     cap = reach_count // 4
     wide = parts * gauge_count * WINDOWS
     members = members_dev * groups
-    sent = pltpu.VMEM((reach_count * rows + EXTRA, block_len), bf16)
-    *packed, own_params, tile = pl.pallas_call(
+    sent = pltpu.VMEM((reach_count * rows + reach_count, block_len), bf16)
+    sent_back = pltpu.VMEM((reach_count * rows + EXTRA, block_len), bf16)
+    base = pltpu.VMEM((members_dev, gauge_count * WINDOWS), f32)
+    *packed, own_params, tile, own_base = pl.pallas_call(
         pack_body,
         out_shape=[sent] * parts
-        + [pltpu.VMEM(route_params.shape, f32), pltpu.VMEM((reach_count, LANES), f32)],
+        + [pltpu.VMEM(route_params.shape, f32), pltpu.VMEM((reach_count, LANES), f32), base],
         in_specs=[smem()] * 4 + [vmem()] * 4,
-        out_specs=[vmem()] * (parts + 2),
+        out_specs=[vmem()] * (parts + 3),
         scratch_shapes=[
             pltpu.VMEM((block_len // LANES, reach_count * members_dev * block_count, LANES), f32),
-            pltpu.VMEM((members_dev + reach_count, LANES), f32),
+            pltpu.VMEM((reach_count, LANES), f32),
         ],
         name="pack",
     )(level_map, down_map, gauge_reach, gauge_sigma, runoff, route_params, observed, obs_noise)
     arrived = swapped(packed, "basin", "basin")
     conv_table, window_table = kernel_table(unit_shapes, series_len // WINDOWS, wide)
-    *routed, noise_base = pl.pallas_call(
+    *routed, base_top = pl.pallas_call(
         functools.partial(
             route_body,
             parts=parts,
@@ -507,9 +525,8 @@
             gauge_count=gauge_count,
             members_dev=members_dev,
         ),
-        out_shape=[sent] * parts
-        + [pltpu.VMEM((parts, members_dev, gauge_count * WINDOWS), f32)],
-        in_specs=[vmem()] * (2 + parts),
+        out_shape=[sent_back] * parts + [pltpu.VMEM((parts,) + base.shape, f32)],
+        in_specs=[vmem()] * (3 + parts),
         out_specs=[vmem()] * (parts + 1),
         scratch_shapes=[
             pltpu.VMEM((total + 2, rows, block_len), f32),
@@ -519,15 +536,18 @@
             pltpu.SMEM((LEVELS * parts * cap,), jnp.int32),
         ],
         name="route",
-    )(kept(conv_table), kept(window_table), *map(kept, arrived))
+    )(kept(conv_table), kept(window_table), kept(own_base), *map(kept, arrived))
     returned = swapped(routed, "basin", "back")
-    local = pl.pallas_call(
+    local, noise_base = pl.pallas_call(
         functools.partial(gather_body, wide=wide),
-        out_shape=pltpu.VMEM((members_dev, wide + LANES), f32),
-        in_specs=[vmem()] * (1 + parts),
-        out_specs=vmem(),
+        out_shape=[
+            pltpu.VMEM((members_dev, wide + LANES), f32),
+            pltpu.VMEM((parts,) + base.shape, f32),
+        ],
+        in_specs=[vmem()] * (2 + parts),
+        out_specs=[vmem()] * 2,
         name="gather",
-    )(kept(tile), *map(kept, returned))
+    )(kept(tile), kept(base_top), *map(kept, returned))
     everyone = swapped([local] * groups, "member", "member")
     flows = pl.pallas_call(
         functools.partial(unpack_body, parts=parts, reach_count=reach_count),
@@ -568,7 +588,7 @@
         and block_len == 2 * LANES
         and gauge_count * WINDOWS == LANES
         and wide % block_len == 0
-        and 3 * share * (wide // block_len) <= EXTRA
+        and members_dev // 2 + 3 * share * (wide // block_len) <= EXTRA
         and shape_count * members_dev + reach_count // 4 + 2 <= LANES // parts
         and 2 * reach_count < CODE
         and parts >= 2

time: 30.1 us -> 30 us (level)
  no operation moved by 1% of the time
where the time goes in v7:
time: 30 us; the launch traced here: 29.8 us
  starting transfers between devices  12.2 us (41%)
  waiting for transfers between devices  9.4 us (31%)
  Pallas kernels  7.54 us (25%)
  between operations  0.67 us (2%)
    ppermute x6, starting transfers between devices, swapped(): results.append(lax.ppermute(piece, (axis, 'member'), pairs))  10.2 us
    ppermute x6, waiting for transfers between devices, swapped(): results.append(lax.ppermute(piece, (axis, 'member'), pairs))  8.22 us
    pallas_call x1, Pallas kernels, per_device_split(): pl.pallas_call(functools.partial(route_body, parts=parts, reach_count=rea...  2.96 us
    ppermute x3, starting transfers between devices, swapped(): results.append(lax.ppermute(piece, axis, pairs))  1.92 us
    pallas_call x1, Pallas kernels, per_device_split(): pl.pallas_call(solve_body, out_shape=jax.ShapeDtypeStruct(route_params.sh...  1.69 us
    pallas_call x1, Pallas kernels, per_device_split(): pl.pallas_call(pack_body, out_shape=[sent] * parts + [pltpu.VMEM(route_pa...  1.21 us
    ppermute x3, waiting for transfers between devices, swapped(): results.append(lax.ppermute(piece, axis, pairs))  1.18 us
    pallas_call x1, Pallas kernels, kernel_table(): pl.pallas_call(functools.partial(table_body, span=span), out_shape=[pltpu...  0.83 us
  transfers between devices with their start and end apart: 9, of which 8 were waited for; matrix products, arithmetic and copies ran while one was open for 0% of the time, Pallas kernels for 6%

profile of v7, /device:TPU:0, one launch (start us, length us, event | category | flops | bytes accessed | tf_op | source)
XLA Modules:
  0.0 29.8 jit_solution(3895875064797621657)
XLA Ops:
  0.6 1.2 %pack.1 = (bf16[136,256]{1,0:T(8,128)(2,1)S(1)}, bf16[136,256]{1,0:T(8,128)(2,1)S(1)}, bf16[136,256]{1,0:T(8,128)(2,1)S(1)}, bf16[136,256]{1,0:T(8,128)(2,1)S(1)...) custom-call(s32[8]{0:T(128)} %level_ref.1, s32[8]{0:T(128)} %down_ref.1, s32[2]{0:T(128)} %gauge_ref.1, ...), custom_call_target="tpu_custom_call" | custom-call | tf_op jit(solution)/shard_map/pack/pallas_call | solution.py:505
  1.8 5.1 %collective-permute-start = (bf16[136,256]{1,0:T(8,128)(2,1)S(1)}, bf16[136,256]{1,0:T(8,128)(2,1)S(1)}, u32[]{:S(2)}, u32[]{:S(2)}) collective-permute-start(bf16[136,256]{1,0:T(8,128)(2,1)S(1)} %get-tuple-element.22), channel_id=1, source_target_pairs={{0,12},{1,13},{2,14},{3,15},{4,8},{5,9},{6,10},{7,11},{8,4},{9,5},... | collective-permute-start | bytes 208904 | tf_op jit(solution)/shard_map/ppermute | solution.py:475
  7.0 0.0 collective-permute-start.1
  7.0 0.6 %collective-permute-start.2 = (bf16[136,256]{1,0:T(8,128)(2,1)S(1)}, bf16[136,256]{1,0:T(8,128)(2,1)S(1)}, u32[]{:S(2)}, u32[]{:S(2)}) collective-permute-start(bf16[136,256]{1,0:T(8,128)(2,1)S(1)} %get-tuple-element.24), channel_id=1, source_target_pairs={{0,8},{1,9},{2,10},{3,11},{4,12},{5,13},{6,14},{7,15},{8,0},{9,1},... | collective-permute-start | bytes 208904 | tf_op jit(solution)/shard_map/ppermute | solution.py:475
  7.6 0.8 %table.1 = (bf16[512,768]{1,0:T(8,128)(2,1)S(1)}, bf16[256,512]{1,0:T(8,128)(2,1)S(1)}) custom-call(f32[3,256]{1,0:T(4,128)} %shapes_ref.1), custom_call_target="tpu_custom_call" | custom-call | tf_op jit(solution)/shard_map/table/pallas_call | solution.py:67
  8.5 1.5 %collective-permute-done.rest_1_ = bf16[136,256]{1,0:T(8,128)(2,1)S(1)} collective-permute-done((bf16[136,256]{1,0:T(8,128)(2,1)S(1)}, bf16[136,256]{1,0:T(8,128)(2,1)S(1)}, u32[]{:S(2)}, u32[]{:S(2)}) %collective-permute-start) | collective-permute-done | bytes 69664 | tf_op jit(solution)/shard_map/ppermute | solution.py:475
  10.0 1.8 %collective-permute-done.1.rest_2_ = bf16[136,256]{1,0:T(8,128)(2,1)S(1)} collective-permute-done((bf16[136,256]{1,0:T(8,128)(2,1)S(1)}, bf16[136,256]{1,0:T(8,128)(2,1)S(1)}, u32[]{:S(2)}, u32[]{:S(2)}) %collective-permute-start.1) | collective-permute-done | bytes 69664 | tf_op jit(solution)/shard_map/ppermute | solution.py:475
  11.9 0.9 %collective-permute-done.2.rest_3_ = bf16[136,256]{1,0:T(8,128)(2,1)S(1)} collective-permute-done((bf16[136,256]{1,0:T(8,128)(2,1)S(1)}, bf16[136,256]{1,0:T(8,128)(2,1)S(1)}, u32[]{:S(2)}, u32[]{:S(2)}) %collective-permute-start.2) | collective-permute-done | bytes 69664 | tf_op jit(solution)/shard_map/ppermute | solution.py:475
  12.7 3.0 %route.1 = (bf16[144,256]{1,0:T(8,128)(2,1)S(1)}, bf16[144,256]{1,0:T(8,128)(2,1)S(1)}, bf16[144,256]{1,0:T(8,128)(2,1)S(1)}, bf16[144,256]{1,0:T(8,128)(2,1)S(1)}, f32[4,8,128]{2,1,0:T(8,128)S(1)}) custom-call(bf16[512,768]{1,0:T(8,128)(2,1)S(1)} %get-tuple-element.18.table_ref, bf16[256,512]{1,0:T(8,128)(2,1)S(1)} %get-tuple-element.19.window_ref, ...), custom_call_target="tpu_custom_call" | custom-call | tf_op jit(solution)/shard_map/route/pallas_call | solution.py:519
  15.7 3.1 %collective-permute-start.3 = (bf16[144,256]{1,0:T(8,128)(2,1)S(1)}, bf16[144,256]{1,0:T(8,128)(2,1)S(1)}, u32[]{:S(2)}, u32[]{:S(2)}) collective-permute-start(bf16[144,256]{1,0:T(8,128)(2,1)S(1)} %get-tuple-element.26), channel_id=1, source_target_pairs={{0,12},{1,9},{2,14},{3,11},{4,8},{5,13},{6,10},{7,15},{8,4},{9,1},... | collective-permute-start | bytes 221192 | tf_op jit(solution)/shard_map/ppermute | solution.py:475
  18.8 0.0 collective-permute-start.4
  18.8 1.4 %collective-permute-start.5 = (bf16[144,256]{1,0:T(8,128)(2,1)S(1)}, bf16[144,256]{1,0:T(8,128)(2,1)S(1)}, u32[]{:S(2)}, u32[]{:S(2)}) collective-permute-start(bf16[144,256]{1,0:T(8,128)(2,1)S(1)} %get-tuple-element.28), channel_id=1, source_target_pairs={{0,8},{1,5},{2,10},{3,7},{4,12},{5,1},{6,14},{7,3},{8,0},{9,13},{1... | collective-permute-start | bytes 221192 | tf_op jit(solution)/shard_map/ppermute | solution.py:475
  20.1 2.6 %collective-permute-done.3.refs_1_.rest_1_ = bf16[144,256]{1,0:T(8,128)(2,1)S(1)} collective-permute-done((bf16[144,256]{1,0:T(8,128)(2,1)S(1)}, bf16[144,256]{1,0:T(8,128)(2,1)S(1)}, u32[]{:S(2)}, u32[]{:S(2)}) %collective-permute-start.3) | collective-permute-done | bytes 73760 | tf_op jit(solution)/shard_map/ppermute | solution.py:475
  22.7 0.6 %collective-permute-done.4.refs_2_.rest_2_ = bf16[144,256]{1,0:T(8,128)(2,1)S(1)} collective-permute-done((bf16[144,256]{1,0:T(8,128)(2,1)S(1)}, bf16[144,256]{1,0:T(8,128)(2,1)S(1)}, u32[]{:S(2)}, u32[]{:S(2)}) %collective-permute-start.4) | collective-permute-done | bytes 73760 | tf_op jit(solution)/shard_map/ppermute | solution.py:475
  23.3 0.8 %collective-permute-done.5.refs_3_.rest_3_ = bf16[144,256]{1,0:T(8,128)(2,1)S(1)} collective-permute-done((bf16[144,256]{1,0:T(8,128)(2,1)S(1)}, bf16[144,256]{1,0:T(8,128)(2,1)S(1)}, u32[]{:S(2)}, u32[]{:S(2)}) %collective-permute-start.5) | collective-permute-done | bytes 73760 | tf_op jit(solution)/shard_map/ppermute | solution.py:475
  24.2 0.1 collective-permute-start.8
  24.2 1.6 %collective-permute-start.7 = (f32[8,640]{1,0:T(8,128)S(1)}, f32[8,640]{1,0:T(8,128)S(1)}, u32[]{:S(2)}, u32[]{:S(2)}) collective-permute-start(f32[8,640]{1,0:T(8,128)S(1)} %get-tuple-element.33.rest_0_), channel_id=1, source_target_pairs={{0,2},{1,3},{2,0},{3,1},{4,6},{5,7},{6,4},{7,5},{8,10},{9,11},{10,... | collective-permute-start | bytes 61448 | tf_op jit(solution)/shard_map/ppermute | solution.py:468
  25.8 0.3 collective-permute-start.6
  26.1 0.8 %unpack.1 = bf16[8,8,2048]{2,1,0:T(8,128)(2,1)} custom-call(bf16[144,256]{1,0:T(8,128)(2,1)S(1)} %get-tuple-element.25.refs_0_.rest_0_, bf16[144,256]{1,0:T(8,128)(2,1)S(1)} %collective-permute-done.3.refs_1_.rest_1_, bf16[144,256]{1,0:T(8,128)(2,1)S(1)} %collective-permute-done.4.refs_2_.rest_2_, bf16[144,256]{1,0:T(8,128)(2,1)S(1)} %collective-permute-done.5.refs_3_.rest_3_), custom_call_target="tpu_custom_call" | custom-call | tf_op jit(solution)/shard_map/unpack/pallas_call | solution.py:552
  26.9 0.7 %collective-permute-done.8.rest_3_ = f32[8,640]{1,0:T(8,128)S(1)} collective-permute-done((f32[8,640]{1,0:T(8,128)S(1)}, f32[8,640]{1,0:T(8,128)S(1)}, u32[]{:S(2)}, u32[]{:S(2)}) %collective-permute-start.8) | collective-permute-done | bytes 20512 | tf_op jit(solution)/shard_map/ppermute | solution.py:468
  27.6 0.5 %collective-permute-done.7.rest_2_ = f32[8,640]{1,0:T(8,128)S(1)} collective-permute-done((f32[8,640]{1,0:T(8,128)S(1)}, f32[8,640]{1,0:T(8,128)S(1)}, u32[]{:S(2)}, u32[]{:S(2)}) %collective-permute-start.7) | collective-permute-done | bytes 20512 | tf_op jit(solution)/shard_map/ppermute | solution.py:468
  28.1 0.0 collective-permute-done.6.rest_1_
  28.1 1.7 %solve.1 = f32[3,8,8]{2,1,0:T(8,128)} custom-call(f32[4,8,128]{2,1,0:T(8,128)S(1)} %get-tuple-element.31.base_ref, f32[3,8,8]{2,1,0:T(8,128)S(1)} %get-tuple-element.32.params_ref, f32[8,640]{1,0:T(8,128)S(1)} %get-tuple-element.33.rest_0_, f32[8,640]{1,0:T(8,128)S(1)} %collective-permute-done.6.rest_1_, f32[8,640]{1,0:T(8,128)S(1)} %collective-permute-done.7.rest_2_, ...), custom_call_target="tpu_custom_call" | custom-call | tf_op jit(solution)/shard_map/solve/pallas_call | solution.py:560
  (1 shorter events, 0.0 us)
Async XLA Ops:
  1.8 8.2 %collective-permute-start = (bf16[136,256]{1,0:T(8,128)(2,1)S(1)}, bf16[136,256]{1,0:T(8,128)(2,1)S(1)}, u32[]{:S(2)}, u32[]{:S(2)}) collective-permute-start(bf16[136,256]{1,0:T(8,128)(2,1)S(1)} %get-tuple-element.22), channel_id=1, source_target_pairs={{0,12},{1,13},{2,14},{3,15},{4,8},{5,9},{6,10},{7,11},{8,4},{9,5},... | collective-permute-start | bytes 208904 | tf_op jit(solution)/shard_map/ppermute | solution.py:475
  7.0 4.9 %collective-permute-start.1 = (bf16[136,256]{1,0:T(8,128)(2,1)S(1)}, bf16[136,256]{1,0:T(8,128)(2,1)S(1)}, u32[]{:S(2)}, u32[]{:S(2)}) collective-permute-start(bf16[136,256]{1,0:T(8,128)(2,1)S(1)} %get-tuple-element.23), channel_id=1, source_target_pairs={{0,4},{1,5},{2,6},{3,7},{4,0},{5,1},{6,2},{7,3},{8,12},{9,13},{10,... | collective-permute-start | bytes 208904 | tf_op jit(solution)/shard_map/ppermute | solution.py:475
  7.0 5.7 %collective-permute-start.2 = (bf16[136,256]{1,0:T(8,128)(2,1)S(1)}, bf16[136,256]{1,0:T(8,128)(2,1)S(1)}, u32[]{:S(2)}, u32[]{:S(2)}) collective-permute-start(bf16[136,256]{1,0:T(8,128)(2,1)S(1)} %get-tuple-element.24), channel_id=1, source_target_pairs={{0,8},{1,9},{2,10},{3,11},{4,12},{5,13},{6,14},{7,15},{8,0},{9,1},... | collective-permute-start | bytes 208904 | tf_op jit(solution)/shard_map/ppermute | solution.py:475
  15.7 7.0 %collective-permute-start.3 = (bf16[144,256]{1,0:T(8,128)(2,1)S(1)}, bf16[144,256]{1,0:T(8,128)(2,1)S(1)}, u32[]{:S(2)}, u32[]{:S(2)}) collective-permute-start(bf16[144,256]{1,0:T(8,128)(2,1)S(1)} %get-tuple-element.26), channel_id=1, source_target_pairs={{0,12},{1,9},{2,14},{3,11},{4,8},{5,13},{6,10},{7,15},{8,4},{9,1},... | collective-permute-start | bytes 221192 | tf_op jit(solution)/shard_map/ppermute | solution.py:475
  18.8 4.6 %collective-permute-start.4 = (bf16[144,256]{1,0:T(8,128)(2,1)S(1)}, bf16[144,256]{1,0:T(8,128)(2,1)S(1)}, u32[]{:S(2)}, u32[]{:S(2)}) collective-permute-start(bf16[144,256]{1,0:T(8,128)(2,1)S(1)} %get-tuple-element.27), channel_id=1, source_target_pairs={{0,4},{1,13},{2,6},{3,15},{4,0},{5,9},{6,2},{7,11},{8,12},{9,5},{1... | collective-permute-start | bytes 221192 | tf_op jit(solution)/shard_map/ppermute | solution.py:475
  18.8 5.3 %collective-permute-start.5 = (bf16[144,256]{1,0:T(8,128)(2,1)S(1)}, bf16[144,256]{1,0:T(8,128)(2,1)S(1)}, u32[]{:S(2)}, u32[]{:S(2)}) collective-permute-start(bf16[144,256]{1,0:T(8,128)(2,1)S(1)} %get-tuple-element.28), channel_id=1, source_target_pairs={{0,8},{1,5},{2,10},{3,7},{4,12},{5,1},{6,14},{7,3},{8,0},{9,13},{1... | collective-permute-start | bytes 221192 | tf_op jit(solution)/shard_map/ppermute | solution.py:475
  24.2 3.4 %collective-permute-start.8 = (f32[8,640]{1,0:T(8,128)S(1)}, f32[8,640]{1,0:T(8,128)S(1)}, u32[]{:S(2)}, u32[]{:S(2)}) collective-permute-start(f32[8,640]{1,0:T(8,128)S(1)} %get-tuple-element.33.rest_0_), channel_id=1, source_target_pairs={{0,3},{1,2},{2,1},{3,0},{4,7},{5,6},{6,5},{7,4},{8,11},{9,10},{10,... | collective-permute-start | bytes 61448 | tf_op jit(solution)/shard_map/ppermute | solution.py:468
  24.2 3.8 %collective-permute-start.7 = (f32[8,640]{1,0:T(8,128)S(1)}, f32[8,640]{1,0:T(8,128)S(1)}, u32[]{:S(2)}, u32[]{:S(2)}) collective-permute-start(f32[8,640]{1,0:T(8,128)S(1)} %get-tuple-element.33.rest_0_), channel_id=1, source_target_pairs={{0,2},{1,3},{2,0},{3,1},{4,6},{5,7},{6,4},{7,5},{8,10},{9,11},{10,... | collective-permute-start | bytes 61448 | tf_op jit(solution)/shard_map/ppermute | solution.py:468
  25.8 2.3 %collective-permute-start.6 = (f32[8,640]{1,0:T(8,128)S(1)}, f32[8,640]{1,0:T(8,128)S(1)}, u32[]{:S(2)}, u32[]{:S(2)}) collective-permute-start(f32[8,640]{1,0:T(8,128)S(1)} %get-tuple-element.33.rest_0_), channel_id=1, source_target_pairs={{0,1},{1,0},{2,3},{3,2},{4,5},{5,4},{6,7},{7,6},{8,9},{9,8},{10,11... | collective-permute-start | bytes 61448 | tf_op jit(solution)/shard_map/ppermute | solution.py:468

commit v8 on v7

--- a/solution.py
+++ b/solution.py
@@ -26,7 +26,7 @@
 
 
 ORDERS = {
-    "basin": ((3, 1, 2), (3, 1, 2)),
+    "basin": ((3, 1, 2), (3, 2, 1)),
     "back": ((3, 1, 2), (2, 3, 1)),
     "member": ((1, 2, 3), (1, 2, 3)),
 }

time: 30 us -> 29.6 us (0.987)
  waiting for transfers between devices: 9.4 us -> 9.03 us
    ppermute x6, waiting for transfers between devices: 8.22 us -> 7.85 us  [swapped(): results.append(lax.ppermute(piece, (axis, 'member'), pairs))]
  transfers between devices with their start and end apart: 9 -> 9, of which waited for: 8 -> 7; matrix products, arithmetic and copies ran while one was open for 0% -> 0% of each run, Pallas kernels for 6% -> 6%
where the time goes in v8:
time: 29.6 us; the launch traced here: 29.4 us
  starting transfers between devices  12.2 us (41%)
  waiting for transfers between devices  9.03 us (31%)
  Pallas kernels  7.53 us (25%)
  between operations  0.67 us (2%)
    ppermute x6, starting transfers between devices, swapped(): results.append(lax.ppermute(piece, (axis, 'member'), pairs))  10.2 us
    ppermute x6, waiting for transfers between devices, swapped(): results.append(lax.ppermute(piece, (axis, 'member'), pairs))  7.85 us
    pallas_call x1, Pallas kernels, per_device_split(): pl.pallas_call(functools.partial(route_body, parts=parts, reach_count=rea...  2.96 us
    ppermute x3, starting transfers between devices, swapped(): results.append(lax.ppermute(piece, axis, pairs))  1.92 us
    pallas_call x1, Pallas kernels, per_device_split(): pl.pallas_call(solve_body, out_shape=jax.ShapeDtypeStruct(route_params.sh...  1.69 us
    pallas_call x1, Pallas kernels, per_device_split(): pl.pallas_call(pack_body, out_shape=[sent] * parts + [pltpu.VMEM(route_pa...  1.21 us
    ppermute x3, waiting for transfers between devices, swapped(): results.append(lax.ppermute(piece, axis, pairs))  1.18 us
    pallas_call x1, Pallas kernels, kernel_table(): pl.pallas_call(functools.partial(table_body, span=span), out_shape=[pltpu...  0.83 us
  transfers between devices with their start and end apart: 9, of which 7 were waited for; matrix products, arithmetic and copies ran while one was open for 0% of the time, Pallas kernels for 6%

profile of v8, /device:TPU:0, one launch (start us, length us, event | category | flops | bytes accessed | tf_op | source)
XLA Modules:
  0.0 29.4 jit_solution(14978170532873568402)
XLA Ops:
  0.6 1.2 %pack.1 = (bf16[136,256]{1,0:T(8,128)(2,1)S(1)}, bf16[136,256]{1,0:T(8,128)(2,1)S(1)}, bf16[136,256]{1,0:T(8,128)(2,1)S(1)}, bf16[136,256]{1,0:T(8,128)(2,1)S(1)...) custom-call(s32[8]{0:T(128)} %level_ref.1, s32[8]{0:T(128)} %down_ref.1, s32[2]{0:T(128)} %gauge_ref.1, ...), custom_call_target="tpu_custom_call" | custom-call | tf_op jit(solution)/shard_map/pack/pallas_call | solution.py:505
  1.8 5.1 %collective-permute-start = (bf16[136,256]{1,0:T(8,128)(2,1)S(1)}, bf16[136,256]{1,0:T(8,128)(2,1)S(1)}, u32[]{:S(2)}, u32[]{:S(2)}) collective-permute-start(bf16[136,256]{1,0:T(8,128)(2,1)S(1)} %get-tuple-element.22), channel_id=1, source_target_pairs={{0,12},{1,13},{2,14},{3,15},{4,8},{5,9},{6,10},{7,11},{8,4},{9,5},... | collective-permute-start | bytes 208904 | tf_op jit(solution)/shard_map/ppermute | solution.py:475
  7.0 0.0 collective-permute-start.1
  7.0 0.6 %collective-permute-start.2 = (bf16[136,256]{1,0:T(8,128)(2,1)S(1)}, bf16[136,256]{1,0:T(8,128)(2,1)S(1)}, u32[]{:S(2)}, u32[]{:S(2)}) collective-permute-start(bf16[136,256]{1,0:T(8,128)(2,1)S(1)} %get-tuple-element.24), channel_id=1, source_target_pairs={{0,8},{1,5},{2,10},{3,7},{4,12},{5,1},{6,14},{7,3},{8,0},{9,13},{1... | collective-permute-start | bytes 208904 | tf_op jit(solution)/shard_map/ppermute | solution.py:475
  7.6 0.8 %table.1 = (bf16[512,768]{1,0:T(8,128)(2,1)S(1)}, bf16[256,512]{1,0:T(8,128)(2,1)S(1)}) custom-call(f32[3,256]{1,0:T(4,128)} %shapes_ref.1), custom_call_target="tpu_custom_call" | custom-call | tf_op jit(solution)/shard_map/table/pallas_call | solution.py:67
  8.5 1.1 %collective-permute-done.rest_1_ = bf16[136,256]{1,0:T(8,128)(2,1)S(1)} collective-permute-done((bf16[136,256]{1,0:T(8,128)(2,1)S(1)}, bf16[136,256]{1,0:T(8,128)(2,1)S(1)}, u32[]{:S(2)}, u32[]{:S(2)}) %collective-permute-start) | collective-permute-done | bytes 69664 | tf_op jit(solution)/shard_map/ppermute | solution.py:475
  9.6 3.1 %collective-permute-done.1.rest_2_ = bf16[136,256]{1,0:T(8,128)(2,1)S(1)} collective-permute-done((bf16[136,256]{1,0:T(8,128)(2,1)S(1)}, bf16[136,256]{1,0:T(8,128)(2,1)S(1)}, u32[]{:S(2)}, u32[]{:S(2)}) %collective-permute-start.1) | collective-permute-done | bytes 69664 | tf_op jit(solution)/shard_map/ppermute | solution.py:475
  12.7 0.0 collective-permute-done.2.rest_3_
  12.7 3.0 %route.1 = (bf16[144,256]{1,0:T(8,128)(2,1)S(1)}, bf16[144,256]{1,0:T(8,128)(2,1)S(1)}, bf16[144,256]{1,0:T(8,128)(2,1)S(1)}, bf16[144,256]{1,0:T(8,128)(2,1)S(1)}, f32[4,8,128]{2,1,0:T(8,128)S(1)}) custom-call(bf16[512,768]{1,0:T(8,128)(2,1)S(1)} %get-tuple-element.18.table_ref, bf16[256,512]{1,0:T(8,128)(2,1)S(1)} %get-tuple-element.19.window_ref, ...), custom_call_target="tpu_custom_call" | custom-call | tf_op jit(solution)/shard_map/route/pallas_call | solution.py:519
  15.6 2.3 %collective-permute-start.3 = (bf16[144,256]{1,0:T(8,128)(2,1)S(1)}, bf16[144,256]{1,0:T(8,128)(2,1)S(1)}, u32[]{:S(2)}, u32[]{:S(2)}) collective-permute-start(bf16[144,256]{1,0:T(8,128)(2,1)S(1)} %get-tuple-element.26), channel_id=1, source_target_pairs={{0,12},{1,9},{2,14},{3,11},{4,8},{5,13},{6,10},{7,15},{8,4},{9,1},... | collective-permute-start | bytes 221192 | tf_op jit(solution)/shard_map/ppermute | solution.py:475
  17.9 0.5 %collective-permute-start.4 = (bf16[144,256]{1,0:T(8,128)(2,1)S(1)}, bf16[144,256]{1,0:T(8,128)(2,1)S(1)}, u32[]{:S(2)}, u32[]{:S(2)}) collective-permute-start(bf16[144,256]{1,0:T(8,128)(2,1)S(1)} %get-tuple-element.27), channel_id=1, source_target_pairs={{0,4},{1,13},{2,6},{3,15},{4,0},{5,9},{6,2},{7,11},{8,12},{9,5},{1... | collective-permute-start | bytes 221192 | tf_op jit(solution)/shard_map/ppermute | solution.py:475
  18.4 1.6 %collective-permute-start.5 = (bf16[144,256]{1,0:T(8,128)(2,1)S(1)}, bf16[144,256]{1,0:T(8,128)(2,1)S(1)}, u32[]{:S(2)}, u32[]{:S(2)}) collective-permute-start(bf16[144,256]{1,0:T(8,128)(2,1)S(1)} %get-tuple-element.28), channel_id=1, source_target_pairs={{0,8},{1,5},{2,10},{3,7},{4,12},{5,1},{6,14},{7,3},{8,0},{9,13},{1... | collective-permute-start | bytes 221192 | tf_op jit(solution)/shard_map/ppermute | solution.py:475
  20.1 2.1 %collective-permute-done.3.refs_1_.rest_1_ = bf16[144,256]{1,0:T(8,128)(2,1)S(1)} collective-permute-done((bf16[144,256]{1,0:T(8,128)(2,1)S(1)}, bf16[144,256]{1,0:T(8,128)(2,1)S(1)}, u32[]{:S(2)}, u32[]{:S(2)}) %collective-permute-start.3) | collective-permute-done | bytes 73760 | tf_op jit(solution)/shard_map/ppermute | solution.py:475
  22.2 0.8 %collective-permute-done.4.refs_2_.rest_2_ = bf16[144,256]{1,0:T(8,128)(2,1)S(1)} collective-permute-done((bf16[144,256]{1,0:T(8,128)(2,1)S(1)}, bf16[144,256]{1,0:T(8,128)(2,1)S(1)}, u32[]{:S(2)}, u32[]{:S(2)}) %collective-permute-start.4) | collective-permute-done | bytes 73760 | tf_op jit(solution)/shard_map/ppermute | solution.py:475
  23.0 0.8 %collective-permute-done.5.refs_3_.rest_3_ = bf16[144,256]{1,0:T(8,128)(2,1)S(1)} collective-permute-done((bf16[144,256]{1,0:T(8,128)(2,1)S(1)}, bf16[144,256]{1,0:T(8,128)(2,1)S(1)}, u32[]{:S(2)}, u32[]{:S(2)}) %collective-permute-start.5) | collective-permute-done | bytes 73760 | tf_op jit(solution)/shard_map/ppermute | solution.py:475
  23.8 0.1 collective-permute-start.8
  23.9 1.6 %collective-permute-start.7 = (f32[8,640]{1,0:T(8,128)S(1)}, f32[8,640]{1,0:T(8,128)S(1)}, u32[]{:S(2)}, u32[]{:S(2)}) collective-permute-start(f32[8,640]{1,0:T(8,128)S(1)} %get-tuple-element.33.rest_0_), channel_id=1, source_target_pairs={{0,2},{1,3},{2,0},{3,1},{4,6},{5,7},{6,4},{7,5},{8,10},{9,11},{10,... | collective-permute-start | bytes 61448 | tf_op jit(solution)/shard_map/ppermute | solution.py:468
  25.4 0.3 collective-permute-start.6
  25.7 0.8 %unpack.1 = bf16[8,8,2048]{2,1,0:T(8,128)(2,1)} custom-call(bf16[144,256]{1,0:T(8,128)(2,1)S(1)} %get-tuple-element.25.refs_0_.rest_0_, bf16[144,256]{1,0:T(8,128)(2,1)S(1)} %collective-permute-done.3.refs_1_.rest_1_, bf16[144,256]{1,0:T(8,128)(2,1)S(1)} %collective-permute-done.4.refs_2_.rest_2_, bf16[144,256]{1,0:T(8,128)(2,1)S(1)} %collective-permute-done.5.refs_3_.rest_3_), custom_call_target="tpu_custom_call" | custom-call | tf_op jit(solution)/shard_map/unpack/pallas_call | solution.py:552
  26.5 0.7 %collective-permute-done.8.rest_3_ = f32[8,640]{1,0:T(8,128)S(1)} collective-permute-done((f32[8,640]{1,0:T(8,128)S(1)}, f32[8,640]{1,0:T(8,128)S(1)}, u32[]{:S(2)}, u32[]{:S(2)}) %collective-permute-start.8) | collective-permute-done | bytes 20512 | tf_op jit(solution)/shard_map/ppermute | solution.py:468
  27.2 0.5 %collective-permute-done.7.rest_2_ = f32[8,640]{1,0:T(8,128)S(1)} collective-permute-done((f32[8,640]{1,0:T(8,128)S(1)}, f32[8,640]{1,0:T(8,128)S(1)}, u32[]{:S(2)}, u32[]{:S(2)}) %collective-permute-start.7) | collective-permute-done | bytes 20512 | tf_op jit(solution)/shard_map/ppermute | solution.py:468
  27.7 0.0 collective-permute-done.6.rest_1_
  27.7 1.7 %solve.1 = f32[3,8,8]{2,1,0:T(8,128)} custom-call(f32[4,8,128]{2,1,0:T(8,128)S(1)} %get-tuple-element.31.base_ref, f32[3,8,8]{2,1,0:T(8,128)S(1)} %get-tuple-element.32.params_ref, f32[8,640]{1,0:T(8,128)S(1)} %get-tuple-element.33.rest_0_, f32[8,640]{1,0:T(8,128)S(1)} %collective-permute-done.6.rest_1_, f32[8,640]{1,0:T(8,128)S(1)} %collective-permute-done.7.rest_2_, ...), custom_call_target="tpu_custom_call" | custom-call | tf_op jit(solution)/shard_map/solve/pallas_call | solution.py:560
  (1 shorter events, 0.0 us)
Async XLA Ops:
  1.8 7.7 %collective-permute-start = (bf16[136,256]{1,0:T(8,128)(2,1)S(1)}, bf16[136,256]{1,0:T(8,128)(2,1)S(1)}, u32[]{:S(2)}, u32[]{:S(2)}) collective-permute-start(bf16[136,256]{1,0:T(8,128)(2,1)S(1)} %get-tuple-element.22), channel_id=1, source_target_pairs={{0,12},{1,13},{2,14},{3,15},{4,8},{5,9},{6,10},{7,11},{8,4},{9,5},... | collective-permute-start | bytes 208904 | tf_op jit(solution)/shard_map/ppermute | solution.py:475
  7.0 5.7 %collective-permute-start.1 = (bf16[136,256]{1,0:T(8,128)(2,1)S(1)}, bf16[136,256]{1,0:T(8,128)(2,1)S(1)}, u32[]{:S(2)}, u32[]{:S(2)}) collective-permute-start(bf16[136,256]{1,0:T(8,128)(2,1)S(1)} %get-tuple-element.23), channel_id=1, source_target_pairs={{0,4},{1,9},{2,6},{3,11},{4,0},{5,13},{6,2},{7,15},{8,12},{9,1},{1... | collective-permute-start | bytes 208904 | tf_op jit(solution)/shard_map/ppermute | solution.py:475
  7.0 5.7 %collective-permute-start.2 = (bf16[136,256]{1,0:T(8,128)(2,1)S(1)}, bf16[136,256]{1,0:T(8,128)(2,1)S(1)}, u32[]{:S(2)}, u32[]{:S(2)}) collective-permute-start(bf16[136,256]{1,0:T(8,128)(2,1)S(1)} %get-tuple-element.24), channel_id=1, source_target_pairs={{0,8},{1,5},{2,10},{3,7},{4,12},{5,1},{6,14},{7,3},{8,0},{9,13},{1... | collective-permute-start | bytes 208904 | tf_op jit(solution)/shard_map/ppermute | solution.py:475
  15.6 6.5 %collective-permute-start.3 = (bf16[144,256]{1,0:T(8,128)(2,1)S(1)}, bf16[144,256]{1,0:T(8,128)(2,1)S(1)}, u32[]{:S(2)}, u32[]{:S(2)}) collective-permute-start(bf16[144,256]{1,0:T(8,128)(2,1)S(1)} %get-tuple-element.26), channel_id=1, source_target_pairs={{0,12},{1,9},{2,14},{3,11},{4,8},{5,13},{6,10},{7,15},{8,4},{9,1},... | collective-permute-start | bytes 221192 | tf_op jit(solution)/shard_map/ppermute | solution.py:475
  17.9 5.1 %collective-permute-start.4 = (bf16[144,256]{1,0:T(8,128)(2,1)S(1)}, bf16[144,256]{1,0:T(8,128)(2,1)S(1)}, u32[]{:S(2)}, u32[]{:S(2)}) collective-permute-start(bf16[144,256]{1,0:T(8,128)(2,1)S(1)} %get-tuple-element.27), channel_id=1, source_target_pairs={{0,4},{1,13},{2,6},{3,15},{4,0},{5,9},{6,2},{7,11},{8,12},{9,5},{1... | collective-permute-start | bytes 221192 | tf_op jit(solution)/shard_map/ppermute | solution.py:475
  18.4 5.3 %collective-permute-start.5 = (bf16[144,256]{1,0:T(8,128)(2,1)S(1)}, bf16[144,256]{1,0:T(8,128)(2,1)S(1)}, u32[]{:S(2)}, u32[]{:S(2)}) collective-permute-start(bf16[144,256]{1,0:T(8,128)(2,1)S(1)} %get-tuple-element.28), channel_id=1, source_target_pairs={{0,8},{1,5},{2,10},{3,7},{4,12},{5,1},{6,14},{7,3},{8,0},{9,13},{1... | collective-permute-start | bytes 221192 | tf_op jit(solution)/shard_map/ppermute | solution.py:475
  23.8 3.4 %collective-permute-start.8 = (f32[8,640]{1,0:T(8,128)S(1)}, f32[8,640]{1,0:T(8,128)S(1)}, u32[]{:S(2)}, u32[]{:S(2)}) collective-permute-start(f32[8,640]{1,0:T(8,128)S(1)} %get-tuple-element.33.rest_0_), channel_id=1, source_target_pairs={{0,3},{1,2},{2,1},{3,0},{4,7},{5,6},{6,5},{7,4},{8,11},{9,10},{10,... | collective-permute-start | bytes 61448 | tf_op jit(solution)/shard_map/ppermute | solution.py:468
  23.9 3.8 %collective-permute-start.7 = (f32[8,640]{1,0:T(8,128)S(1)}, f32[8,640]{1,0:T(8,128)S(1)}, u32[]{:S(2)}, u32[]{:S(2)}) collective-permute-start(f32[8,640]{1,0:T(8,128)S(1)} %get-tuple-element.33.rest_0_), channel_id=1, source_target_pairs={{0,2},{1,3},{2,0},{3,1},{4,6},{5,7},{6,4},{7,5},{8,10},{9,11},{10,... | collective-permute-start | bytes 61448 | tf_op jit(solution)/shard_map/ppermute | solution.py:468
  25.4 2.3 %collective-permute-start.6 = (f32[8,640]{1,0:T(8,128)S(1)}, f32[8,640]{1,0:T(8,128)S(1)}, u32[]{:S(2)}, u32[]{:S(2)}) collective-permute-start(f32[8,640]{1,0:T(8,128)S(1)} %get-tuple-element.33.rest_0_), channel_id=1, source_target_pairs={{0,1},{1,0},{2,3},{3,2},{4,5},{5,4},{6,7},{7,6},{8,9},{9,8},{10,11... | collective-permute-start | bytes 61448 | tf_op jit(solution)/shard_map/ppermute | solution.py:468
